TPU v7x, 768 devices: a whole 4x8x12 slice. The times are simulated.
768 devices in a mesh: curve: 384 (over z, y, x), sub: 2 (over core).
Axes of the slice: x: 4, y: 8, z: 12, core: 2. Of those that a mesh axis runs over, the one named last changes fastest.
Arguments:
- pressure: float32 [3072, 4096], P(('curve', 'sub')), may hold values from -6 to 6
- source_term: float32 [3072, 4096], P(('curve', 'sub')), may hold values from -7 to 7
- coefficient: float32 [3072, 4096], P(('curve', 'sub')), may hold values from 0.05 to 2
- new_slot: int32 [3072], P(('curve', 'sub')), may hold values from 0 to 7, as said below
- face_links: int32 [3072, 6], P(('curve', 'sub')), may hold values from -1 to 3071, as said below
Outputs:
- corrected: float32 [3072, 4096], P(('curve', 'sub'))
Inputs may be any that keep to these rules, and one draw needn't show every extreme that they name: `new_slot`: every block stays within its Z-order range of 8 blocks; within a range the slots form a permutation, each device receives exactly 4 blocks, and one device hands at most 2 blocks to one device, a bound reached by every device. `face_links`: A neighbour of block b lies in range b // 8 - 1, b // 8 or b // 8 + 1.
All inputs are finite; a program needn't handle non-finite values.
Results may differ from a plain program's by a relative error of at most 0.0001.
Values sent between devices are 32-bit elements; how exact they have to be, the bound alone decides.
No kernel may reach another device: no remote copies, remote signals or barrier semaphores. Data moves between devices by JAX's collectives and lax.ppermute only.
A program may use at most 32 MiB of HBM per device.

v0:
```python
import jax
import jax.numpy as jnp
from jax import lax
from jax.sharding import PartitionSpec as P

PRE_SWEEPS = 2
COARSE_SWEEPS = 4


relaxation = 0.8
highest = lax.Precision.HIGHEST


def with_halo(block, sides, width):
    for axis, dim in sides:
        count = lax.axis_size(axis)
        forward = [(i, i + 1) for i in range(count - 1)]
        backward = [(target, source) for source, target in forward]
        low = lax.ppermute(
            lax.slice_in_dim(block, block.shape[dim] - width, None, axis=dim), axis, forward
        )
        high = lax.ppermute(lax.slice_in_dim(block, 0, width, axis=dim), axis, backward)
        block = jnp.concatenate([low, block, high], axis=dim)
    return block


def face_stack(field):
    cubes = field.reshape(-1, 16, 16, 16)
    layers = [
        cubes[:, 0],
        cubes[:, -1],
        cubes[:, :, 0],
        cubes[:, :, -1],
        cubes[:, :, :, 0],
        cubes[:, :, :, -1],
    ]
    return jnp.stack(layers, axis=1).reshape(-1, 6, 256)


def apply_operator(field, ghosts, coefficient):
    cubes = field.reshape(-1, 16, 16, 16)
    sides = ghosts.reshape(-1, 6, 16, 16)
    x_plus = jnp.concatenate([cubes[:, 1:], sides[:, 1][:, None]], axis=1)
    x_minus = jnp.concatenate([sides[:, 0][:, None], cubes[:, :-1]], axis=1)
    y_plus = jnp.concatenate([cubes[:, :, 1:], sides[:, 3][:, :, None]], axis=2)
    y_minus = jnp.concatenate([sides[:, 2][:, :, None], cubes[:, :, :-1]], axis=2)
    z_plus = jnp.concatenate([cubes[:, :, :, 1:], sides[:, 5][:, :, :, None]], axis=3)
    z_minus = jnp.concatenate([sides[:, 4][:, :, :, None], cubes[:, :, :, :-1]], axis=3)
    beside = x_plus + x_minus
    beside = beside + y_plus + y_minus
    beside = beside + z_plus + z_minus
    return (6.0 + coefficient) * field - beside.reshape(-1, 4096)


def select_faces(links, window, base):
    columns = jnp.arange(window.shape[0], dtype=jnp.int32)
    local_links = links - base
    selector = (
        (local_links[:, :, None] == columns[None, None, :]) & (links >= 0)[:, :, None]
    ).astype(jnp.float32)
    return jnp.einsum("bdw,wdx->bdx", selector, window, precision=highest)


def ghost_layers(field, face_links):
    faces = face_stack(field)
    flipped = jnp.array([1, 0, 3, 2, 5, 4], dtype=jnp.int32)
    ranged = lax.all_gather(faces, "sub", axis=0, tiled=True)
    window = with_halo(ranged, (("curve", 0),), ranged.shape[0])
    span = window.shape[0] // 3
    return select_faces(face_links, window[:, flipped], (lax.axis_index("curve") - 1) * span)


def sweep(field, source, coefficient, face_links):
    image = apply_operator(field, ghost_layers(field, face_links), coefficient)
    return field + relaxation * (source - image) / (6.0 + coefficient)


def near_errors(block_error):
    ranged = lax.all_gather(block_error, "sub", axis=0, tiled=True)
    window = with_halo(ranged, (("curve", 0),), ranged.shape[0])
    return window


def window_sum(window, face_links):
    span = window.shape[0] // 3
    base = (lax.axis_index("curve") - 1) * span
    local_links = face_links - base
    clipped = jnp.clip(local_links, 0, window.shape[0] - 1)
    return jnp.sum(jnp.where(face_links >= 0, window[clipped], 0.0), axis=1)


def earlier_same(targets):
    same_target = (targets[..., :, None] == targets[..., None, :]).astype(jnp.int32)
    return jnp.sum(jnp.tril(same_target, -1), axis=-1)


def on_device(pressure, source_term, coefficient, new_slot, face_links):
    blocks_here = pressure.shape[0]
    nsub = lax.axis_size("sub")
    most = max(1, blocks_here // nsub)
    own_sub = lax.axis_index("sub")
    all_slots = lax.all_gather(new_slot, "sub", axis=0, tiled=True).reshape(nsub, blocks_here)
    target_dev = new_slot // blocks_here
    order_rank = earlier_same(target_dev)
    peers = jnp.arange(nsub, dtype=jnp.int32)
    places = jnp.arange(most, dtype=jnp.int32)
    send_sel = (
        (target_dev[None, None, :] == peers[:, None, None])
        & (order_rank[None, None, :] == places[None, :, None])
    ).astype(jnp.float32)
    stacked = jnp.stack([pressure, source_term, coefficient], axis=1)
    outgoing = jnp.einsum("qmj,jcx->qmcx", send_sel, stacked, precision=highest)
    incoming = lax.all_to_all(outgoing, "sub", split_axis=0, concat_axis=0, tiled=True)
    all_targets = all_slots // blocks_here
    all_ranks = earlier_same(all_targets)
    all_places = all_slots % blocks_here
    arrivals = all_targets == own_sub
    slots_here = jnp.arange(blocks_here, dtype=jnp.int32)
    matched = (
        arrivals[None, :, :, None]
        & (all_places[None, :, :, None] == slots_here[:, None, None, None])
        & (all_ranks[None, :, :, None] == places[None, None, None, :])
    )
    recv_sel = jnp.sum(matched.astype(jnp.float32), axis=2)
    moved = jnp.einsum("kpm,pmcx->kcx", recv_sel, incoming, precision=highest)
    moved_p = moved[:, 0]
    moved_f = moved[:, 1]
    moved_c = moved[:, 2]
    smoothed = moved_p
    for step in range(PRE_SWEEPS):
        smoothed = sweep(smoothed, moved_f, moved_c, face_links)
    residual = moved_f - apply_operator(smoothed, ghost_layers(smoothed, face_links), moved_c)
    block_residual = jnp.mean(residual, axis=1)
    block_diag = 6.0 + jnp.mean(moved_c, axis=1)
    block_error = jnp.zeros((blocks_here,), jnp.float32)
    for step in range(COARSE_SWEEPS):
        if step == 0:
            beside = jnp.zeros((blocks_here,), jnp.float32)
        else:
            beside = window_sum(near_errors(block_error), face_links)
        block_error = (
            block_error
            + relaxation * (block_residual - block_diag * block_error + beside) / block_diag
        )
    lifted = smoothed + block_error[:, None]
    return sweep(lifted, moved_f, moved_c, face_links)


def solution(mesh):
    placed = (
        P(("curve", "sub"), None),
        P(("curve", "sub"), None),
        P(("curve", "sub"), None),
        P(("curve", "sub")),
        P(("curve", "sub"), None),
    )
    return jax.shard_map(
        on_device, mesh=mesh, in_specs=placed, out_specs=P(("curve", "sub"), None), check_vma=False
    )
```

profile of v0, /device:TPU:254, one launch (start us, length us, event | category | flops | bytes accessed | tf_op | source)
XLA Modules:
  0.0 164.9 jit_solution(1735565340957212959)
XLA Ops:
  0.9 2.0 %fusion.16 = f32[2,2,3,4096]{3,1,2,0:T(2,128)} fusion(f32[4,1,4096]{2,0,1:T(4,128)} %bitcast.233, f32[4,1,4096]{2,0,1:T(4,128)} %bitcast.234, f32[4,1,4096]{2,0,1:T(4,128)} %bitcast.235, pred[2,2,4,1]{2,0,1,3:T(4,128)(4,1)S(1)} %and_bitcast_fusion), kind=kOutput, calls=%fused_computation.36 | convolution fusion | flops 2457600 | bytes 393232 | tf_op jit(solution)/shard_map/qmj,jcx->qmcx/dot_general | solution.py:112
  2.8 3.4 %all-to-all-start = ((f32[2,2,3,4096]{3,1,2,0:T(2,128)}), f32[2,2,3,4096]{3,1,2,0:T(2,128)S(1)}, u32[]{:S(2)}, u32[]{:S(2)}) async-start(f32[2,2,3,4096]{3,1,2,0:T(2,128)} %fusion.16), calls=%async_computation | async-start | bytes 393216 | tf_op jit(solution)/shard_map/all_to_all | solution.py:113
  9.1 1.9 %all-reduce = s32[8]{0:T(128)S(1)} all-reduce(s32[8]{0:T(128)S(1)} %dynamic-update-slice), channel_id=1, replica_groups=mesh['curve'=384,'sub'=2] {'sub'}, use_global_device_ids=true, to_apply=%add | all-reduce | flops 8 | bytes 64
  14.3 1.9 %all_gather.25 = f32[8,6,256]{2,1,0:T(8,128)S(1)} all-gather(f32[4,6,256]{2,1,0:T(8,128)S(1)} %copy.216), channel_id=1, replica_groups=mesh['curve'=384,'sub'=2] {'sub'}, dimensions={0}, use_global_device_ids=true | all-gather | bytes 73728 | tf_op jit(solution)/shard_map/all_gather | solution.py:67
  16.2 4.6 %collective-permute-start = (f32[8,6,256]{2,0,1:T(8,128)S(1)}, f32[8,6,256]{2,0,1:T(8,128)S(1)}, u32[]{:S(2)}, u32[]{:S(2)}) collective-permute-start(f32[8,6,256]{2,0,1:T(8,128)S(1)} %copy.217), channel_id=1, source_target_pairs={{0,2},{2,4},{4,6},{6,8},{8,10},{10,12},{12,14},{14,16},{16,18},{18... | collective-permute-start | bytes 147464 | tf_op jit(solution)/shard_map/ppermute | solution.py:19
  20.8 1.9 %collective-permute-start.1 = (f32[8,6,256]{2,0,1:T(8,128)S(1)}, f32[8,6,256]{2,0,1:T(8,128)S(1)}, u32[]{:S(2)}, u32[]{:S(2)}) collective-permute-start(f32[8,6,256]{2,0,1:T(8,128)S(1)} %copy.217), channel_id=1, source_target_pairs={{2,0},{4,2},{6,4},{8,6},{10,8},{12,10},{14,12},{16,14},{18,16},{20... | collective-permute-start | bytes 147464 | tf_op jit(solution)/shard_map/ppermute | solution.py:22
  28.4 3.8 %collective-permute-done.1 = f32[8,6,256]{2,0,1:T(8,128)S(1)} collective-permute-done((f32[8,6,256]{2,0,1:T(8,128)S(1)}, f32[8,6,256]{2,0,1:T(8,128)S(1)}, u32[]{:S(2)}, u32[]{:S(2)}) %collective-permute-start.1) | collective-permute-done | bytes 49184 | tf_op jit(solution)/shard_map/ppermute | solution.py:22
  35.3 2.7 %divide_add_fusion.1 = (f32[4,16,16,16]{2,1,0,3:T(8,128)S(1)}, f32[4,16,16,16]{2,1,0,3:T(8,128)S(1)}) fusion(f32[4,16,16,16]{2,1,0,3:T(8,128)S(1)} %copy.213, f32[4,16,16,16]{2,1,0,3:T(8,128)S(1)} %copy.232, f32[4,16,16,16]{2,1,0,3:T(8,128)S(1)} %copy.234, f32[4,16,16,15]{2,1,0,3:T(8,128)} %get-tuple-element.64, f32[4,16,16,1]{2,1,0,3:T(8,128)S(1)} %get-tuple-element.92, ...), kind=kLoop, calls=%fused_computation.33 | loop fusion | flops 278528 | bytes 720896 | tf_op jit(solution)/shard_map/add | solution.py:75
  41.8 5.6 %collective-permute-start.2 = (f32[8,6,256]{2,0,1:T(8,128)S(1)}, f32[8,6,256]{2,0,1:T(8,128)S(1)}, u32[]{:S(2)}, u32[]{:S(2)}) collective-permute-start(f32[8,6,256]{2,0,1:T(8,128)S(1)} %copy.242), channel_id=1, source_target_pairs={{0,2},{2,4},{4,6},{6,8},{8,10},{10,12},{12,14},{14,16},{16,18},{18... | collective-permute-start | bytes 147464 | tf_op jit(solution)/shard_map/ppermute | solution.py:19
  47.4 1.9 %collective-permute-start.3 = (f32[8,6,256]{2,0,1:T(8,128)S(1)}, f32[8,6,256]{2,0,1:T(8,128)S(1)}, u32[]{:S(2)}, u32[]{:S(2)}) collective-permute-start(f32[8,6,256]{2,0,1:T(8,128)S(1)} %copy.242), channel_id=1, source_target_pairs={{2,0},{4,2},{6,4},{8,6},{10,8},{12,10},{14,12},{16,14},{18,16},{20... | collective-permute-start | bytes 147464 | tf_op jit(solution)/shard_map/ppermute | solution.py:22
  53.2 5.6 %collective-permute-done.3 = f32[8,6,256]{2,0,1:T(8,128)S(1)} collective-permute-done((f32[8,6,256]{2,0,1:T(8,128)S(1)}, f32[8,6,256]{2,0,1:T(8,128)S(1)}, u32[]{:S(2)}, u32[]{:S(2)}) %collective-permute-start.3) | collective-permute-done | bytes 49184 | tf_op jit(solution)/shard_map/ppermute | solution.py:22
  61.9 2.7 %divide_add_fusion = (f32[4,16,16,16]{2,1,0,3:T(8,128)S(1)}, f32[4,16,16,16]{2,1,0,3:T(8,128)S(1)}) fusion(f32[4,16,16,16]{2,1,0,3:T(8,128)S(1)} %get-tuple-element.19, f32[4,16,16,16]{2,1,0,3:T(8,128)S(1)} %copy.232, f32[4,16,16,16]{2,1,0,3:T(8,128)S(1)} %copy.234, f32[4,16,16,15]{2,1,0,3:T(8,128)} %get-tuple-element.52, ...), kind=kLoop, calls=%fused_computation.32 | loop fusion | flops 278528 | bytes 720896 | tf_op jit(solution)/shard_map/add | solution.py:75
  68.4 3.7 %collective-permute-start.4 = (f32[8,6,256]{2,0,1:T(8,128)S(1)}, f32[8,6,256]{2,0,1:T(8,128)S(1)}, u32[]{:S(2)}, u32[]{:S(2)}) collective-permute-start(f32[8,6,256]{2,0,1:T(8,128)S(1)} %copy.258), channel_id=1, source_target_pairs={{0,2},{2,4},{4,6},{6,8},{8,10},{10,12},{12,14},{14,16},{16,18},{18... | collective-permute-start | bytes 147464 | tf_op jit(solution)/shard_map/ppermute | solution.py:19
  72.2 2.3 %collective-permute-start.5 = (f32[8,6,256]{2,0,1:T(8,128)S(1)}, f32[8,6,256]{2,0,1:T(8,128)S(1)}, u32[]{:S(2)}, u32[]{:S(2)}) collective-permute-start(f32[8,6,256]{2,0,1:T(8,128)S(1)} %copy.258), channel_id=1, source_target_pairs={{2,0},{4,2},{6,4},{8,6},{10,8},{12,10},{14,12},{16,14},{18,16},{20... | collective-permute-start | bytes 147464 | tf_op jit(solution)/shard_map/ppermute | solution.py:22
  77.4 6.2 %collective-permute-done.5 = f32[8,6,256]{2,0,1:T(8,128)S(1)} collective-permute-done((f32[8,6,256]{2,0,1:T(8,128)S(1)}, f32[8,6,256]{2,0,1:T(8,128)S(1)}, u32[]{:S(2)}, u32[]{:S(2)}) %collective-permute-start.5) | collective-permute-done | bytes 49184 | tf_op jit(solution)/shard_map/ppermute | solution.py:22
  87.3 2.0 %fusion.11 = f32[4,16,16,16]{2,1,0,3:T(8,128)S(1)} fusion(f32[4,1,16,16]{2,1,0,3:T(1,128)} %copy.261, f32[4,15,16,16]{2,1,0,3:T(8,128)} %get-tuple-element.40, f32[4,15,16,16]{2,1,0,3:T(8,128)} %get-tuple-element.39, f32[4,1,16,16]{2,1,0,3:T(1,128)} %copy.262, f32[4,16,1,16]{2,1,0,3:T(8,128)S(1)} %copy.263, f32[4,16,15,16]{2,1,0,3:T(8,128)S(1)} %get-tuple-element.38, ...), kind=kLoop, calls=%fused_computation.26 | loop fusion | flops 180224 | bytes 458752 | tf_op jit(solution)/shard_map/add | solution.py:51
  90.8 2.5 %all-reduce.1 = f32[8]{0:T(128)S(1)} all-reduce(f32[8]{0:T(128)S(1)} %get-tuple-element.13), channel_id=1, replica_groups=mesh['curve'=384,'sub'=2] {'sub'}, use_global_device_ids=true, to_apply=%add.1 | all-reduce | flops 8 | bytes 64
  93.3 3.0 %collective-permute-start.6 = (f32[8]{0:T(128)S(1)}, f32[8]{0:T(128)S(1)}, u32[]{:S(2)}, u32[]{:S(2)}) collective-permute-start(f32[8]{0:T(128)S(1)} %all-reduce.1), channel_id=1, source_target_pairs={{0,2},{2,4},{4,6},{6,8},{8,10},{10,12},{12,14},{14,16},{16,18},{18... | collective-permute-start | bytes 104 | tf_op jit(solution)/shard_map/ppermute | solution.py:19
  96.3 2.8 %collective-permute-start.7 = (f32[8]{0:T(128)S(1)}, f32[8]{0:T(128)S(1)}, u32[]{:S(2)}, u32[]{:S(2)}) collective-permute-start(f32[8]{0:T(128)S(1)} %all-reduce.1), channel_id=1, source_target_pairs={{2,0},{4,2},{6,4},{8,6},{10,8},{12,10},{14,12},{16,14},{18,16},{20... | collective-permute-start | bytes 104 | tf_op jit(solution)/shard_map/ppermute | solution.py:22
  99.1 8.0 %collective-permute-done.7 = f32[8]{0:T(128)S(1)} collective-permute-done((f32[8]{0:T(128)S(1)}, f32[8]{0:T(128)S(1)}, u32[]{:S(2)}, u32[]{:S(2)}) %collective-permute-start.7) | collective-permute-done | bytes 64 | tf_op jit(solution)/shard_map/ppermute | solution.py:22
  108.3 2.5 %all-reduce.2 = f32[8]{0:T(128)S(1)} all-reduce(f32[8]{0:T(128)S(1)} %get-tuple-element.9), channel_id=1, replica_groups=mesh['curve'=384,'sub'=2] {'sub'}, use_global_device_ids=true, to_apply=%add.2 | all-reduce | flops 8 | bytes 64
  110.7 1.9 %collective-permute-start.8 = (f32[8]{0:T(128)S(1)}, f32[8]{0:T(128)S(1)}, u32[]{:S(2)}, u32[]{:S(2)}) collective-permute-start(f32[8]{0:T(128)S(1)} %all-reduce.2), channel_id=1, source_target_pairs={{0,2},{2,4},{4,6},{6,8},{8,10},{10,12},{12,14},{14,16},{16,18},{18... | collective-permute-start | bytes 104 | tf_op jit(solution)/shard_map/ppermute | solution.py:19
  112.6 3.9 %collective-permute-start.9 = (f32[8]{0:T(128)S(1)}, f32[8]{0:T(128)S(1)}, u32[]{:S(2)}, u32[]{:S(2)}) collective-permute-start(f32[8]{0:T(128)S(1)} %all-reduce.2), channel_id=1, source_target_pairs={{2,0},{4,2},{6,4},{8,6},{10,8},{12,10},{14,12},{16,14},{18,16},{20... | collective-permute-start | bytes 104 | tf_op jit(solution)/shard_map/ppermute | solution.py:22
  116.6 7.0 %collective-permute-done.9 = f32[8]{0:T(128)S(1)} collective-permute-done((f32[8]{0:T(128)S(1)}, f32[8]{0:T(128)S(1)}, u32[]{:S(2)}, u32[]{:S(2)}) %collective-permute-start.9) | collective-permute-done | bytes 64 | tf_op jit(solution)/shard_map/ppermute | solution.py:22
  124.6 2.5 %all-reduce.3 = f32[8]{0:T(128)S(1)} all-reduce(f32[8]{0:T(128)S(1)} %get-tuple-element.7), channel_id=1, replica_groups=mesh['curve'=384,'sub'=2] {'sub'}, use_global_device_ids=true, to_apply=%add.3 | all-reduce | flops 8 | bytes 64
  127.1 1.9 %collective-permute-start.10 = (f32[8]{0:T(128)S(1)}, f32[8]{0:T(128)S(1)}, u32[]{:S(2)}, u32[]{:S(2)}) collective-permute-start(f32[8]{0:T(128)S(1)} %all-reduce.3), channel_id=1, source_target_pairs={{0,2},{2,4},{4,6},{6,8},{8,10},{10,12},{12,14},{14,16},{16,18},{18... | collective-permute-start | bytes 104 | tf_op jit(solution)/shard_map/ppermute | solution.py:19
  129.0 3.9 %collective-permute-start.11 = (f32[8]{0:T(128)S(1)}, f32[8]{0:T(128)S(1)}, u32[]{:S(2)}, u32[]{:S(2)}) collective-permute-start(f32[8]{0:T(128)S(1)} %all-reduce.3), channel_id=1, source_target_pairs={{2,0},{4,2},{6,4},{8,6},{10,8},{12,10},{14,12},{16,14},{18,16},{20... | collective-permute-start | bytes 104 | tf_op jit(solution)/shard_map/ppermute | solution.py:22
  132.9 7.0 %collective-permute-done.11 = f32[8]{0:T(128)S(1)} collective-permute-done((f32[8]{0:T(128)S(1)}, f32[8]{0:T(128)S(1)}, u32[]{:S(2)}, u32[]{:S(2)}) %collective-permute-start.11) | collective-permute-done | bytes 64 | tf_op jit(solution)/shard_map/ppermute | solution.py:22
  145.3 1.9 %collective-permute-start.12 = (f32[8,6,256]{2,0,1:T(8,128)S(1)}, f32[8,6,256]{2,0,1:T(8,128)S(1)}, u32[]{:S(2)}, u32[]{:S(2)}) collective-permute-start(f32[8,6,256]{2,0,1:T(8,128)S(1)} %copy.271), channel_id=1, source_target_pairs={{0,2},{2,4},{4,6},{6,8},{8,10},{10,12},{12,14},{14,16},{16,18},{18... | collective-permute-start | bytes 147464 | tf_op jit(solution)/shard_map/ppermute | solution.py:19
  147.2 3.9 %collective-permute-start.13 = (f32[8,6,256]{2,0,1:T(8,128)S(1)}, f32[8,6,256]{2,0,1:T(8,128)S(1)}, u32[]{:S(2)}, u32[]{:S(2)}) collective-permute-start(f32[8,6,256]{2,0,1:T(8,128)S(1)} %copy.271), channel_id=1, source_target_pairs={{2,0},{4,2},{6,4},{8,6},{10,8},{12,10},{14,12},{16,14},{18,16},{20... | collective-permute-start | bytes 147464 | tf_op jit(solution)/shard_map/ppermute | solution.py:22
  153.3 5.3 %collective-permute-done.13 = f32[8,6,256]{2,0,1:T(8,128)S(1)} collective-permute-done((f32[8,6,256]{2,0,1:T(8,128)S(1)}, f32[8,6,256]{2,0,1:T(8,128)S(1)}, u32[]{:S(2)}, u32[]{:S(2)}) %collective-permute-start.13) | collective-permute-done | bytes 49184 | tf_op jit(solution)/shard_map/ppermute | solution.py:22
  161.1 1.9 %fusion.15 = f32[4,16,16,16]{2,1,0,3:T(8,128)S(1)} fusion(f32[4,1,16,16]{2,1,0,3:T(1,128)S(1)} %copy.274, f32[4,15,16,16]{2,1,0,3:T(8,128)} %get-tuple-element.28, f32[4,15,16,16]{2,1,0,3:T(8,128)S(1)} %get-tuple-element.27, f32[4,1,16,16]{2,1,0,3:T(1,128)S(1)} %copy.275, f32[4,16,1,16]{2,1,0,3:T(8,128)S(1)} %copy.276, ...), kind=kLoop, calls=%fused_computation.31 | loop fusion | flops 180224 | bytes 458752 | tf_op jit(solution)/shard_map/add | solution.py:51
  (214 shorter events, 51.6 us)
Async XLA Ops:
  2.8 8.7 %all-to-all-start = ((f32[2,2,3,4096]{3,1,2,0:T(2,128)}), f32[2,2,3,4096]{3,1,2,0:T(2,128)S(1)}, u32[]{:S(2)}, u32[]{:S(2)}) async-start(f32[2,2,3,4096]{3,1,2,0:T(2,128)} %fusion.16), calls=%async_computation | async-start | bytes 393216 | tf_op jit(solution)/shard_map/all_to_all | solution.py:113
  8.2 0.7 copy-start.6
  16.2 12.2 %collective-permute-start = (f32[8,6,256]{2,0,1:T(8,128)S(1)}, f32[8,6,256]{2,0,1:T(8,128)S(1)}, u32[]{:S(2)}, u32[]{:S(2)}) collective-permute-start(f32[8,6,256]{2,0,1:T(8,128)S(1)} %copy.217), channel_id=1, source_target_pairs={{0,2},{2,4},{4,6},{6,8},{8,10},{10,12},{12,14},{14,16},{16,18},{18... | collective-permute-start | bytes 147464 | tf_op jit(solution)/shard_map/ppermute | solution.py:19
  20.8 11.4 %collective-permute-start.1 = (f32[8,6,256]{2,0,1:T(8,128)S(1)}, f32[8,6,256]{2,0,1:T(8,128)S(1)}, u32[]{:S(2)}, u32[]{:S(2)}) collective-permute-start(f32[8,6,256]{2,0,1:T(8,128)S(1)} %copy.217), channel_id=1, source_target_pairs={{2,0},{4,2},{6,4},{8,6},{10,8},{12,10},{14,12},{16,14},{18,16},{20... | collective-permute-start | bytes 147464 | tf_op jit(solution)/shard_map/ppermute | solution.py:22
  25.0 1.1 copy-start.5
  26.0 32.8 %copy-start.2 = (s32[1024]{0:T(1024)}, s32[1024]{0:T(1024)S(1)}, u32[]{:S(2)}) copy-start(s32[1024]{0:T(1024)S(1)} %pad_clamp_fusion.1) | copy-start | bytes 12292
  26.1 0.7 copy-start
  41.8 11.4 %collective-permute-start.2 = (f32[8,6,256]{2,0,1:T(8,128)S(1)}, f32[8,6,256]{2,0,1:T(8,128)S(1)}, u32[]{:S(2)}, u32[]{:S(2)}) collective-permute-start(f32[8,6,256]{2,0,1:T(8,128)S(1)} %copy.242), channel_id=1, source_target_pairs={{0,2},{2,4},{4,6},{6,8},{8,10},{10,12},{12,14},{14,16},{16,18},{18... | collective-permute-start | bytes 147464 | tf_op jit(solution)/shard_map/ppermute | solution.py:19
  47.4 11.4 %collective-permute-start.3 = (f32[8,6,256]{2,0,1:T(8,128)S(1)}, f32[8,6,256]{2,0,1:T(8,128)S(1)}, u32[]{:S(2)}, u32[]{:S(2)}) collective-permute-start(f32[8,6,256]{2,0,1:T(8,128)S(1)} %copy.242), channel_id=1, source_target_pairs={{2,0},{4,2},{6,4},{8,6},{10,8},{12,10},{14,12},{16,14},{18,16},{20... | collective-permute-start | bytes 147464 | tf_op jit(solution)/shard_map/ppermute | solution.py:22
  68.4 9.0 %collective-permute-start.4 = (f32[8,6,256]{2,0,1:T(8,128)S(1)}, f32[8,6,256]{2,0,1:T(8,128)S(1)}, u32[]{:S(2)}, u32[]{:S(2)}) collective-permute-start(f32[8,6,256]{2,0,1:T(8,128)S(1)} %copy.258), channel_id=1, source_target_pairs={{0,2},{2,4},{4,6},{6,8},{8,10},{10,12},{12,14},{14,16},{16,18},{18... | collective-permute-start | bytes 147464 | tf_op jit(solution)/shard_map/ppermute | solution.py:19
  72.2 11.4 %collective-permute-start.5 = (f32[8,6,256]{2,0,1:T(8,128)S(1)}, f32[8,6,256]{2,0,1:T(8,128)S(1)}, u32[]{:S(2)}, u32[]{:S(2)}) collective-permute-start(f32[8,6,256]{2,0,1:T(8,128)S(1)} %copy.258), channel_id=1, source_target_pairs={{2,0},{4,2},{6,4},{8,6},{10,8},{12,10},{14,12},{16,14},{18,16},{20... | collective-permute-start | bytes 147464 | tf_op jit(solution)/shard_map/ppermute | solution.py:22
  90.1 0.6 copy-start.1
  93.3 5.8 %collective-permute-start.6 = (f32[8]{0:T(128)S(1)}, f32[8]{0:T(128)S(1)}, u32[]{:S(2)}, u32[]{:S(2)}) collective-permute-start(f32[8]{0:T(128)S(1)} %all-reduce.1), channel_id=1, source_target_pairs={{0,2},{2,4},{4,6},{6,8},{8,10},{10,12},{12,14},{14,16},{16,18},{18... | collective-permute-start | bytes 104 | tf_op jit(solution)/shard_map/ppermute | solution.py:19
  96.3 10.9 %collective-permute-start.7 = (f32[8]{0:T(128)S(1)}, f32[8]{0:T(128)S(1)}, u32[]{:S(2)}, u32[]{:S(2)}) collective-permute-start(f32[8]{0:T(128)S(1)} %all-reduce.1), channel_id=1, source_target_pairs={{2,0},{4,2},{6,4},{8,6},{10,8},{12,10},{14,12},{16,14},{18,16},{20... | collective-permute-start | bytes 104 | tf_op jit(solution)/shard_map/ppermute | solution.py:22
  110.7 5.8 %collective-permute-start.8 = (f32[8]{0:T(128)S(1)}, f32[8]{0:T(128)S(1)}, u32[]{:S(2)}, u32[]{:S(2)}) collective-permute-start(f32[8]{0:T(128)S(1)} %all-reduce.2), channel_id=1, source_target_pairs={{0,2},{2,4},{4,6},{6,8},{8,10},{10,12},{12,14},{14,16},{16,18},{18... | collective-permute-start | bytes 104 | tf_op jit(solution)/shard_map/ppermute | solution.py:19
  112.6 10.9 %collective-permute-start.9 = (f32[8]{0:T(128)S(1)}, f32[8]{0:T(128)S(1)}, u32[]{:S(2)}, u32[]{:S(2)}) collective-permute-start(f32[8]{0:T(128)S(1)} %all-reduce.2), channel_id=1, source_target_pairs={{2,0},{4,2},{6,4},{8,6},{10,8},{12,10},{14,12},{16,14},{18,16},{20... | collective-permute-start | bytes 104 | tf_op jit(solution)/shard_map/ppermute | solution.py:22
  127.1 5.8 %collective-permute-start.10 = (f32[8]{0:T(128)S(1)}, f32[8]{0:T(128)S(1)}, u32[]{:S(2)}, u32[]{:S(2)}) collective-permute-start(f32[8]{0:T(128)S(1)} %all-reduce.3), channel_id=1, source_target_pairs={{0,2},{2,4},{4,6},{6,8},{8,10},{10,12},{12,14},{14,16},{16,18},{18... | collective-permute-start | bytes 104 | tf_op jit(solution)/shard_map/ppermute | solution.py:19
  129.0 10.9 %collective-permute-start.11 = (f32[8]{0:T(128)S(1)}, f32[8]{0:T(128)S(1)}, u32[]{:S(2)}, u32[]{:S(2)}) collective-permute-start(f32[8]{0:T(128)S(1)} %all-reduce.3), channel_id=1, source_target_pairs={{2,0},{4,2},{6,4},{8,6},{10,8},{12,10},{14,12},{16,14},{18,16},{20... | collective-permute-start | bytes 104 | tf_op jit(solution)/shard_map/ppermute | solution.py:22
  140.9 0.5 copy-start.3
  145.3 8.1 %collective-permute-start.12 = (f32[8,6,256]{2,0,1:T(8,128)S(1)}, f32[8,6,256]{2,0,1:T(8,128)S(1)}, u32[]{:S(2)}, u32[]{:S(2)}) collective-permute-start(f32[8,6,256]{2,0,1:T(8,128)S(1)} %copy.271), channel_id=1, source_target_pairs={{0,2},{2,4},{4,6},{6,8},{8,10},{10,12},{12,14},{14,16},{16,18},{18... | collective-permute-start | bytes 147464 | tf_op jit(solution)/shard_map/ppermute | solution.py:19
  147.2 11.4 %collective-permute-start.13 = (f32[8,6,256]{2,0,1:T(8,128)S(1)}, f32[8,6,256]{2,0,1:T(8,128)S(1)}, u32[]{:S(2)}, u32[]{:S(2)}) collective-permute-start(f32[8,6,256]{2,0,1:T(8,128)S(1)} %copy.271), channel_id=1, source_target_pairs={{2,0},{4,2},{6,4},{8,6},{10,8},{12,10},{14,12},{16,14},{18,16},{20... | collective-permute-start | bytes 147464 | tf_op jit(solution)/shard_map/ppermute | solution.py:22
  163.6 0.7 copy-start.4
where the time goes:
time: 166 us; the launch traced here: 165 us
  starting transfers between devices  46.8 us (28%)
  waiting for transfers between devices  42.8 us (26%)
  local copies, waits for them, and re-layouts  40.5 us (24%)
  blocking collectives  16.7 us (10%)
  other arithmetic  13.2 us (8%)
  matrix products  3.46 us (2%)
    ppermute x7, waiting for transfers between devices, with_halo(): lax.ppermute(lax.slice_in_dim(block, 0, width, axis=dim), axis, backward)  42.8 us
    ppermute x7, starting transfers between devices, with_halo(): lax.ppermute(lax.slice_in_dim(block, block.shape[dim] - width, None, axis...  22.7 us
    ppermute x7, starting transfers between devices, with_halo(): lax.ppermute(lax.slice_in_dim(block, 0, width, axis=dim), axis, backward)  20.7 us
    unnamed x4, blocking collectives  9.31 us
    all_gather x4, blocking collectives, ghost_layers(): ranged = lax.all_gather(faces, 'sub', axis=0, tiled=True)  7.42 us
    add x3, other arithmetic, sweep(): return field + relaxation * (source - image) / (6.0 + coefficient)  6.04 us
    unnamed x40, local copies, waits for them, and re-layouts  4.59 us
    add x2, other arithmetic, apply_operator(): beside = beside + z_plus + z_minus  3.9 us
  transfers between devices with their start and end apart: 15, of which 7 were waited for; matrix products, arithmetic and copies ran while one was open for 10% of the time, Pallas kernels for 0%

commit v1 on v0

v1 whole, which is shorter than its diff:
```python
import functools

import jax
import jax.numpy as jnp
from jax import lax
from jax.experimental import pallas as pl
from jax.experimental.pallas import tpu as pltpu
from jax.sharding import Mesh, PartitionSpec as P

PRE_SWEEPS = 2
COARSE_SWEEPS = 4
RELAXATION = 0.8

SIDE = 16
RANGE = 8
LANES = 128
CELLS = 4096
FACES = 6
FLIPPED = (1, 0, 3, 2, 5, 4)
ROW = 4
SLOTS = LANES // RANGE

VMEM = pl.BlockSpec(memory_space=pltpu.VMEM)
SMEM = pl.BlockSpec(memory_space=pltpu.SMEM)


def f32(*shape):
    return jax.ShapeDtypeStruct(shape, jnp.float32)


def lanes():
    return lax.broadcasted_iota(jnp.int32, (RANGE, LANES), 1)


def sublanes():
    return lax.broadcasted_iota(jnp.int32, (RANGE, LANES), 0)


def roll(tile, amount):
    amount = amount % LANES
    return tile if amount == 0 else pltpu.roll(tile, amount, 1)


def load(ref):
    return [[ref[2 * x + h] for h in range(2)] for x in range(SIDE)]


def store(ref, tiles):
    for x in range(SIDE):
        for h in range(2):
            ref[2 * x + h] = tiles[x][h]


def pack_faces(tiles):
    lane = lanes()
    zero = jnp.zeros((RANGE, LANES), jnp.float32)
    y_low, y_high, z_low, z_high = [[zero, zero] for _ in range(4)]
    for x in range(SIDE):
        part, place = x // 8, x % 8
        here = lane // SIDE == place
        y_low[part] = jnp.where(here, roll(tiles[x][0], SIDE * place), y_low[part])
        y_high[part] = jnp.where(here, roll(tiles[x][1], SIDE * place + SIDE), y_high[part])
        column = lane % SIDE == x
        for h in range(2):
            z_low[h] = jnp.where(column, roll(tiles[x][h], x), z_low[h])
            z_high[h] = jnp.where(column, roll(tiles[x][h], x - (SIDE - 1)), z_high[h])
    return [tiles[0], tiles[SIDE - 1], y_low, y_high, z_low, z_high]


def store_faces(ref, faces):
    for f in range(FACES):
        for h in range(2):
            ref[:, (2 * f + h) * LANES : (2 * f + h + 1) * LANES] = faces[f][h]


def load_face(ref, f, h, *lead):
    return ref[(*lead, slice(None), slice((2 * f + h) * LANES, (2 * f + h + 1) * LANES))]


def pick_rows(tile, rows):
    return jnp.take_along_axis(tile, rows, axis=0)


def ghost_faces(links, base, before, own, after):
    ghosts, valid = [], []
    for d in range(FACES):
        link = jnp.broadcast_to(links[:, d : d + 1], (RANGE, LANES))
        local = link - base
        rows = link & (RANGE - 1)
        face = FLIPPED[d]
        halves = []
        for h in range(2):
            low = pick_rows(before(face, h), rows)
            mid = pick_rows(own(face, h), rows)
            high = pick_rows(after(face, h), rows)
            picked = jnp.where(local < 0, low, jnp.where(local >= RANGE, high, mid))
            halves.append(jnp.where(link >= 0, picked, 0.0))
        ghosts.append(halves)
        valid.append(link >= 0)
    return ghosts, valid


def beside(tiles, ghosts, x, h):
    lane = lanes()
    here = tiles[x][h]
    minus = tiles[x - 1][h] if x > 0 else ghosts[0][h]
    plus = tiles[x + 1][h] if x < SIDE - 1 else ghosts[1][h]
    total = minus + plus
    part, place = x // 8, x % 8
    if h == 0:
        outer_minus = roll(ghosts[2][part], -SIDE * place)
        outer_plus = roll(tiles[x][1], -SIDE)
    else:
        outer_minus = roll(tiles[x][0], SIDE)
        outer_plus = roll(ghosts[3][part], LANES - SIDE - SIDE * place)
    total = total + jnp.where(lane < SIDE, outer_minus, roll(here, SIDE))
    total = total + jnp.where(lane >= LANES - SIDE, outer_plus, roll(here, -SIDE))
    z = lane % SIDE
    total = total + jnp.where(z == 0, roll(ghosts[4][h], -x), roll(here, 1))
    total = total + jnp.where(z == SIDE - 1, roll(ghosts[5][h], SIDE - 1 - x), roll(here, -1))
    return total


def sweep(tiles, ghosts, source_ref, coefficient_ref):
    out = []
    for x in range(SIDE):
        out.append([])
        for h in range(2):
            weight = RELAXATION / (6.0 + coefficient_ref[2 * x + h])
            gathered = source_ref[2 * x + h] + beside(tiles, ghosts, x, h)
            out[x].append((1.0 - RELAXATION) * tiles[x][h] + weight * gathered)
    return out


def both(ref):
    return jnp.concatenate([ref[0], ref[1]], axis=0)


def range_base():
    return lax.axis_index("d") // 2 * RANGE


def reorder_kernel(slot_ref, p_ref, f_ref, c_ref, links_ref, p_out, f_out, c_out, links_out, faces_out):
    row = sublanes()
    rows = jnp.zeros((RANGE, LANES), jnp.int32)
    for i in range(RANGE):
        rows = jnp.where(row == slot_ref[i // 4, i % 4], i, rows)
    for source, target in ((p_ref, p_out), (f_ref, f_out), (c_ref, c_out)):
        for t in range(CELLS // LANES):
            span = slice(t * LANES, (t + 1) * LANES)
            tile = jnp.concatenate([source[0, :, span], source[1, :, span]], axis=0)
            target[t] = pick_rows(tile, rows)
    links_out[...] = both(links_ref)
    store_faces(faces_out, pack_faces(load(p_out)))


def window(pair_ref, faces_ref):
    before = lambda f, h: load_face(pair_ref, f, h, 1, 0)
    own = lambda f, h: load_face(faces_ref, f, h)
    after = lambda f, h: load_face(pair_ref, f, h, 0, 1)
    return before, own, after


def sweep_kernel(u_ref, f_ref, c_ref, links_ref, faces_ref, pair_ref, u_out, faces_out):
    ghosts, _ = ghost_faces(links_ref[...], range_base(), *window(pair_ref, faces_ref))
    tiles = sweep(load(u_ref), ghosts, f_ref, c_ref)
    store(u_out, tiles)
    store_faces(faces_out, pack_faces(tiles))


def lane_sum(tile):
    return jnp.sum(tile, axis=1, keepdims=True)


def face_sums(face):
    return [lane_sum(face(FLIPPED[d], 0) + face(FLIPPED[d], 1)) * (1.0 / CELLS) for d in range(FACES)]


def to_lanes(columns, range_index):
    at = lanes() == range_index % SLOTS * RANGE + sublanes()
    row = sublanes()
    tile = jnp.zeros((RANGE, LANES), jnp.float32)
    for i, column in enumerate(columns):
        spread = jnp.sum(jnp.where(at, column, 0.0), axis=0, keepdims=True)
        tile = jnp.where(row == i, spread, tile)
    return tile


def smooth_kernel(u_ref, f_ref, c_ref, links_ref, faces_ref, pair_ref, u_out, faces_out, coarse_out):
    links = links_ref[...]
    ghosts, _ = ghost_faces(links, range_base(), *window(pair_ref, faces_ref))
    tiles = sweep(load(u_ref), ghosts, f_ref, c_ref)
    store(u_out, tiles)
    faces = pack_faces(tiles)
    store_faces(faces_out, faces)
    defect = jnp.zeros((RANGE, LANES), jnp.float32)
    weights = jnp.zeros((RANGE, LANES), jnp.float32)
    for x in range(SIDE):
        for h in range(2):
            c = c_ref[2 * x + h]
            defect = defect + (f_ref[2 * x + h] - c * tiles[x][h])
            weights = weights + c
    sums = face_sums(lambda f, h: faces[f][h])
    inner = lane_sum(defect) * (1.0 / CELLS)
    for s in sums:
        inner = inner - s
    diag = 6.0 + lane_sum(weights) * (1.0 / CELLS)
    me = lax.axis_index("d") // 2
    values = to_lanes(sums + [inner, diag], me)
    names = to_lanes([links[:, d : d + 1].astype(jnp.float32) for d in range(FACES)], me)
    for i in range(ROW):
        coarse_out[i, 0:RANGE] = values
        coarse_out[i, RANGE : 2 * RANGE] = names


def row_kernel(coarse_ref, met_ref, out_ref):
    me = lax.axis_index("d")
    core, curve = me % 2, me // 2
    edge = jnp.where(core == 0, curve % ROW == ROW - 1, curve % ROW == 0)
    met = jnp.where(core == 0, curve + 1, curve + SLOTS - 1)
    sums = to_lanes(face_sums(lambda f, h: load_face(met_ref, f, h)), met)
    out_ref[0 : 2 * RANGE] = coarse_ref[0] + coarse_ref[1] + coarse_ref[2] + coarse_ref[3]
    out_ref[2 * RANGE : 3 * RANGE] = jnp.where(edge, sums, 0.0)


def final_kernel(u_ref, f_ref, c_ref, links_ref, faces_ref, met_ref, row_ref, rows_ref, out_ref):
    core, curve = lax.axis_index("d") % 2, lax.axis_index("d") // 2
    row = sublanes()
    spans = [slice(i * RANGE, (i + 1) * RANGE) for i in range(3)]
    values = row_ref[spans[0]] + rows_ref[0, 0, spans[0]] + rows_ref[1, 1, spans[0]]
    names = row_ref[spans[1]] + rows_ref[0, 0, spans[1]] + rows_ref[1, 1, spans[1]]
    sums = values + rows_ref[0, 0, spans[2]] + rows_ref[1, 1, spans[2]]
    valid = jnp.logical_and(names >= 0.0, row < FACES)
    at = names.astype(jnp.int32) & (LANES - 1)

    def named(tile):
        return jnp.where(valid, jnp.take_along_axis(tile, at, axis=1), 0.0)

    def total(tile):
        return jnp.broadcast_to(jnp.sum(tile, axis=0, keepdims=True), (RANGE, LANES))

    inner = jnp.broadcast_to(values[FACES : FACES + 1], (RANGE, LANES))
    diag = jnp.broadcast_to(values[FACES + 1 : FACES + 2], (RANGE, LANES))
    diag = jnp.where(diag > 0.0, diag, 1.0)
    residual = inner + total(named(sums))
    error = jnp.zeros((RANGE, LANES), jnp.float32)
    for step in range(COARSE_SWEEPS):
        near = total(named(error)) if step else 0.0
        error = error + RELAXATION * (residual - diag * error + near) / diag
    near = named(error)
    own = lanes() == curve % SLOTS * RANGE + row
    lift = lane_sum(jnp.where(own, error, 0.0))
    before = lambda f, h: load_face(met_ref, f, h, 1)
    mine = lambda f, h: load_face(faces_ref, f, h)
    after = lambda f, h: load_face(met_ref, f, h, 0)
    ghosts, _ = ghost_faces(links_ref[...], range_base(), before, mine, after)
    for d in range(FACES):
        raised = lane_sum(jnp.where(own, jnp.broadcast_to(near[d : d + 1], (RANGE, LANES)), 0.0))
        ghosts[d] = [half + raised for half in ghosts[d]]
    tiles = [[tile + lift for tile in pair] for pair in load(u_ref)]
    tiles = sweep(tiles, ghosts, f_ref, c_ref)
    for x in range(SIDE):
        for h in range(2):
            tile = tiles[x][h]
            half = jnp.where(core == 0, tile[0 : RANGE // 2], tile[RANGE // 2 :])
            t = 2 * x + h
            out_ref[:, t * LANES : (t + 1) * LANES] = half


def call(kernel, out_shape, name, *args, scalars=0):
    many = isinstance(out_shape, (list, tuple))
    return pl.pallas_call(
        kernel,
        out_shape=out_shape,
        in_specs=[SMEM] * scalars + [VMEM] * (len(args) - scalars),
        out_specs=[VMEM] * len(out_shape) if many else VMEM,
        name=name,
    )(*args)


def on_device(groups, pressure, source_term, coefficient, new_slot, face_links):
    cores, pairs, rows, row_pairs, exchange = groups
    gather = lambda array, members: lax.all_gather(array, "d", axis=0, axis_index_groups=members)
    field = f32(CELLS // LANES, RANGE, LANES)
    packed = f32(RANGE, FACES * 2 * LANES)
    p, f, c, slots, links = [
        gather(array, cores) for array in (pressure, source_term, coefficient, new_slot, face_links)
    ]
    u, f, c, links, faces = call(
        reorder_kernel,
        [field, field, field, jax.ShapeDtypeStruct((RANGE, FACES), jnp.int32), packed],
        "reorder",
        slots,
        p,
        f,
        c,
        links,
        scalars=1,
    )
    pair = gather(gather(faces, pairs), cores)
    u, faces = call(sweep_kernel, [field, packed], "sweep", u, f, c, links, faces, pair)
    pair = gather(gather(faces, pairs), cores)
    u, faces, coarse = call(
        smooth_kernel, [field, packed, f32(ROW, 2 * RANGE, LANES)], "smooth", u, f, c, links, faces, pair
    )
    met = lax.ppermute(faces, "d", exchange)
    coarse = lax.all_to_all(coarse, "d", 0, 0, axis_index_groups=rows, tiled=True)
    row = call(row_kernel, f32(3 * RANGE, LANES), "row", coarse, met)
    met, near_rows = gather(met, cores), gather(gather(row, row_pairs), cores)
    return call(
        final_kernel, f32(RANGE // 2, CELLS), "final", u, f, c, links, faces, met, row, near_rows
    )


def solution(mesh):
    devices = mesh.devices.reshape(-1)
    count = devices.size // 2
    cores = [[2 * i, 2 * i + 1] for i in range(count)]
    pairs = [[2 * i, 2 * i + 3] for i in range(count - 1)] + [[2 * count - 2, 1]]
    rows = [[2 * (i + k) + core for k in range(ROW)] for i in range(0, count, ROW) for core in range(2)]
    row_pairs = [[2 * i + 1, 2 * ((i + ROW) % count)] for i in range(count)]
    exchange = [pair for i in range(count - 1) for pair in ((2 * i, 2 * i + 3), (2 * i + 3, 2 * i))]
    split, line = P("d", None), P("d")
    return jax.shard_map(
        functools.partial(on_device, (cores, pairs, rows, row_pairs, exchange)),
        mesh=Mesh(devices, ("d",)),
        in_specs=(split, split, split, line, split),
        out_specs=split,
        check_vma=False,
    )
```

time: 166 us -> 84.6 us (0.51)
  the two profiles are of different devices: /device:TPU:254 before, /device:TPU:1 now
where the time goes in v1:
time: 84.6 us; the launch traced here: 83.9 us
  blocking collectives  68.8 us (81%)
  Pallas kernels  10.3 us (12%)
  local copies, waits for them, and re-layouts  3.41 us (4%)
    all_gather x11, blocking collectives, on_device(): lax.all_gather(array, 'd', axis=0, axis_index_groups=members)  48.5 us
    unnamed x1, blocking collectives  11.9 us
    pallas_call x5, Pallas kernels, call(): pl.pallas_call(kernel, out_shape=out_shape, in_specs=[SMEM] * scalars + [...  10.3 us
    all_to_all x1, blocking collectives, on_device(): lax.all_to_all(coarse, 'd', 0, 0, axis_index_groups=rows, tiled=True)  8.43 us
    unnamed x15, local copies, waits for them, and re-layouts  2.75 us
  transfers between devices with their start and end apart: 1, of which 0 were waited for; matrix products, arithmetic and copies ran while one was open for 0% of the time, Pallas kernels for 0%

profile of v1, /device:TPU:1, one launch (start us, length us, event | category | flops | bytes accessed | tf_op | source)
XLA Modules:
  0.0 83.9 jit_solution(2295157999118208768)
XLA Ops:
  0.0 1.3 %dynamic-slice = u32[1]{0:T(128)} dynamic-slice(u32[768]{0:T(1024)} %constant.7, u32[]{:T(128)S(6)} %add), dynamic_slice_sizes={1} | dynamic-slice | bytes 12
  1.9 0.0 copy-start.5
  1.9 0.6 copy-done.5
  2.6 0.2 dynamic-update-slice
  2.8 11.9 %all-reduce = s32[8]{0:T(128)S(1)} all-reduce(s32[8]{0:T(128)S(1)} %dynamic-update-slice), channel_id=2, replica_groups={{0,1},{2,3},{4,5},{6,7},{8,9},{10,11},{12,13},{14,15},{16,17},{18,19},{..., use_global_device_ids=true, to_apply=%add | all-reduce | flops 8 | bytes 64
  14.7 0.0 copy-start.4
  14.7 0.7 reshape.slot_ref
  15.4 0.0 copy-done.4
  15.4 2.0 %all-gather.15.links_ref = s32[2,4,6]{2,1,0:T(4,128)} all-gather(s32[1,4,6]{2,1,0:T(4,128)S(1)} %bitcast.22), channel_id=6, replica_groups={{0,1},{2,3},{4,5},{6,7},{8,9},{10,11},{12,13},{14,15},{16,17},{18,19},{..., dimensions={0}, use_global_device_ids=true | all-gather | bytes 288 | tf_op jit(solution)/shard_map/all_gather | solution.py:283
  17.4 0.0 copy-start.2
  17.4 3.7 %all-gather.12.p_ref = f32[2,4,4096]{2,1,0:T(4,128)} all-gather(f32[1,4,4096]{2,1,0:T(4,128)} %bitcast.19), channel_id=3, replica_groups={{0,1},{2,3},{4,5},{6,7},{8,9},{10,11},{12,13},{14,15},{16,17},{18,19},{..., dimensions={0}, use_global_device_ids=true | all-gather | bytes 196608 | tf_op jit(solution)/shard_map/all_gather | solution.py:283
  21.0 0.0 copy-done.2
  21.0 2.2 %all-gather.13.f_ref = f32[2,4,4096]{2,1,0:T(4,128)} all-gather(f32[1,4,4096]{2,1,0:T(4,128)S(1)} %bitcast.20), channel_id=4, replica_groups={{0,1},{2,3},{4,5},{6,7},{8,9},{10,11},{12,13},{14,15},{16,17},{18,19},{..., dimensions={0}, use_global_device_ids=true | all-gather | bytes 196608 | tf_op jit(solution)/shard_map/all_gather | solution.py:283
  23.2 0.0 copy-done.3
  23.2 2.0 %all-gather.14.c_ref = f32[2,4,4096]{2,1,0:T(4,128)} all-gather(f32[1,4,4096]{2,1,0:T(4,128)S(1)} %bitcast.21), channel_id=5, replica_groups={{0,1},{2,3},{4,5},{6,7},{8,9},{10,11},{12,13},{14,15},{16,17},{18,19},{..., dimensions={0}, use_global_device_ids=true | all-gather | bytes 196608 | tf_op jit(solution)/shard_map/all_gather | solution.py:283
  25.2 1.9 %reorder.1 = (f32[32,8,128]{2,1,0:T(8,128)}, f32[32,8,128]{2,1,0:T(8,128)}, f32[32,8,128]{2,1,0:T(8,128)}, s32[8,6]{1,0:T(8,128)}, f32[8,1536]{1,0:T(8,128)}) custom-call(s32[2,4]{1,0:T(2,128)} %reshape.slot_ref, f32[2,4,4096]{2,1,0:T(4,128)} %all-gather.12.p_ref, f32[2,4,4096]{2,1,0:T(4,128)} %all-gather.13.f_ref, f32[2,4,4096]{2,1,0:T(4,128)} %all-gather.14.c_ref, ...), custom_call_target="tpu_custom_call" | custom-call | tf_op jit(solution)/shard_map/reorder/pallas_call | solution.py:272
  27.1 11.3 %all-gather.5 = f32[16,1536]{1,0:T(8,128)S(1)} all-gather(f32[8,1536]{1,0:T(8,128)} %get-tuple-element.19.faces_ref), channel_id=7, replica_groups={{0,3},{2,5},{4,7},{6,9},{8,11},{10,13},{12,15},{14,17},{16,19},{18,21},..., dimensions={0}, use_global_device_ids=true | all-gather | bytes 147456 | tf_op jit(solution)/shard_map/all_gather | solution.py:283
  38.3 2.1 %all-gather.6 = f32[4,8,1536]{2,1,0:T(8,128)} all-gather(f32[2,8,1536]{2,1,0:T(8,128)S(1)} %bitcast.14), channel_id=8, replica_groups={{0,1},{2,3},{4,5},{6,7},{8,9},{10,11},{12,13},{14,15},{16,17},{18,19},{..., dimensions={0}, use_global_device_ids=true | all-gather | bytes 294912 | tf_op jit(solution)/shard_map/all_gather | solution.py:283
  40.4 2.2 %sweep.1 = (f32[32,8,128]{2,1,0:T(8,128)}, f32[8,1536]{1,0:T(8,128)}) custom-call(f32[32,8,128]{2,1,0:T(8,128)} %get-tuple-element.15.u_ref, f32[32,8,128]{2,1,0:T(8,128)} %get-tuple-element.16.f_ref, f32[32,8,128]{2,1,0:T(8,128)} %get-tuple-element.17.c_ref, s32[8,6]{1,0:T(8,128)} %get-tuple-element.18.links_ref, f32[8,1536]{1,0:T(8,128)} %get-tuple-element.19.faces_ref, ...), custom_call_target="tpu_custom_call" | custom-call | tf_op jit(solution)/shard_map/sweep/pallas_call | solution.py:272
  42.6 9.8 %all-gather.7 = f32[16,1536]{1,0:T(8,128)S(1)} all-gather(f32[8,1536]{1,0:T(8,128)} %get-tuple-element.21.faces_ref), channel_id=9, replica_groups={{0,3},{2,5},{4,7},{6,9},{8,11},{10,13},{12,15},{14,17},{16,19},{18,21},..., dimensions={0}, use_global_device_ids=true | all-gather | bytes 147456 | tf_op jit(solution)/shard_map/all_gather | solution.py:283
  52.4 2.1 %all-gather.8 = f32[4,8,1536]{2,1,0:T(8,128)} all-gather(f32[2,8,1536]{2,1,0:T(8,128)S(1)} %bitcast.15), channel_id=10, replica_groups={{0,1},{2,3},{4,5},{6,7},{8,9},{10,11},{12,13},{14,15},{16,17},{18,19},{..., dimensions={0}, use_global_device_ids=true | all-gather | bytes 294912 | tf_op jit(solution)/shard_map/all_gather | solution.py:283
  54.5 2.3 %smooth.1 = (f32[32,8,128]{2,1,0:T(8,128)}, f32[8,1536]{1,0:T(8,128)}, f32[4,16,128]{2,1,0:T(8,128)}) custom-call(f32[32,8,128]{2,1,0:T(8,128)} %get-tuple-element.20.u_ref, f32[32,8,128]{2,1,0:T(8,128)} %get-tuple-element.16.f_ref, f32[32,8,128]{2,1,0:T(8,128)} %get-tuple-element.17.c_ref, s32[8,6]{1,0:T(8,128)} %get-tuple-element.18.links_ref, ...), custom_call_target="tpu_custom_call" | custom-call | tf_op jit(solution)/shard_map/smooth/pallas_call | solution.py:272
  56.8 0.7 collective-permute-start
  57.5 8.4 %all_to_all.5.coarse_ref = f32[4,16,128]{2,1,0:T(8,128)} all-to-all(f32[4,16,128]{2,1,0:T(8,128)} %get-tuple-element.24), channel_id=1, replica_groups={{0,2,4,6},{1,3,5,7},{8,10,12,14},{9,11,13,15},{16,18,20,22},{17,19,21,2..., dimensions={0} | all-to-all | bytes 65536 | tf_op jit(solution)/shard_map/all_to_all | solution.py:307
  65.9 0.0 collective-permute-done.met_ref
  65.9 0.6 copy-done
  66.5 1.5 %row.1.row_ref = f32[24,128]{1,0:T(8,128)} custom-call(f32[4,16,128]{2,1,0:T(8,128)} %all_to_all.5.coarse_ref, f32[8,1536]{1,0:T(8,128)} %copy-done), custom_call_target="tpu_custom_call" | custom-call | tf_op jit(solution)/shard_map/row/pallas_call | solution.py:272
  68.0 4.2 %all-gather.10 = f32[48,128]{1,0:T(8,128)S(1)} all-gather(f32[24,128]{1,0:T(8,128)} %row.1.row_ref), channel_id=12, replica_groups={{1,8},{3,10},{5,12},{7,14},{9,16},{11,18},{13,20},{15,22},{17,24},{19,2..., dimensions={0}, use_global_device_ids=true | all-gather | bytes 36864 | tf_op jit(solution)/shard_map/all_gather | solution.py:283
  72.2 7.3 %all-gather.11 = f32[4,24,128]{2,1,0:T(8,128)} all-gather(f32[2,24,128]{2,1,0:T(8,128)S(1)} %bitcast.18), channel_id=13, replica_groups={{0,1},{2,3},{4,5},{6,7},{8,9},{10,11},{12,13},{14,15},{16,17},{18,19},{..., dimensions={0}, use_global_device_ids=true | all-gather | bytes 73728 | tf_op jit(solution)/shard_map/all_gather | solution.py:283
  79.5 0.0 copy-done.1
  79.5 2.0 %all-gather.9 = f32[16,1536]{1,0:T(8,128)} all-gather(f32[8,1536]{1,0:T(8,128)S(1)} %copy-done.1), channel_id=11, replica_groups={{0,1},{2,3},{4,5},{6,7},{8,9},{10,11},{12,13},{14,15},{16,17},{18,19},{..., dimensions={0}, use_global_device_ids=true | all-gather | bytes 147456 | tf_op jit(solution)/shard_map/all_gather | solution.py:283
  81.5 2.4 %final.1 = f32[4,4096]{1,0:T(4,128)} custom-call(f32[32,8,128]{2,1,0:T(8,128)} %get-tuple-element.22.u_ref, f32[32,8,128]{2,1,0:T(8,128)} %get-tuple-element.16.f_ref, f32[32,8,128]{2,1,0:T(8,128)} %get-tuple-element.17.c_ref, s32[8,6]{1,0:T(8,128)} %get-tuple-element.18.links_ref, f32[8,1536]{1,0:T(8,128)} %get-tuple-element.23.faces_ref, ...), custom_call_target="tpu_custom_call" | custom-call | tf_op jit(solution)/shard_map/final/pallas_call | solution.py:272
  (4 shorter events, 0.0 us)
Async XLA Ops:
  1.9 0.7 copy-start.5
  14.7 0.7 copy-start.4
  17.4 3.7 %copy-start.2 = (f32[4,4096]{1,0:T(4,128)S(1)}, f32[4,4096]{1,0:T(4,128)}, u32[]{:S(2)}) copy-start(f32[4,4096]{1,0:T(4,128)} %param.6) | copy-start | bytes 196612
  21.0 2.2 %copy-start.3 = (f32[4,4096]{1,0:T(4,128)S(1)}, f32[4,4096]{1,0:T(4,128)}, u32[]{:S(2)}) copy-start(f32[4,4096]{1,0:T(4,128)} %param.7) | copy-start | bytes 196612
  56.8 9.1 %collective-permute-start = (f32[8,1536]{1,0:T(8,128)}, f32[8,1536]{1,0:T(8,128)S(1)}, u32[]{:S(2)}, u32[]{:S(2)}) collective-permute-start(f32[8,1536]{1,0:T(8,128)} %get-tuple-element.23.faces_ref), channel_id=1, source_target_pairs={{0,3},{3,0},{2,5},{5,2},{4,7},{7,4},{6,9},{9,6},{8,11},{11,8},{10,... | collective-permute-start | bytes 147464 | tf_op jit(solution)/shard_map/ppermute | solution.py:306
  65.9 0.6 copy-start
  68.0 11.4 %copy-start.1 = (f32[8,1536]{1,0:T(8,128)S(1)}, f32[8,1536]{1,0:T(8,128)}, u32[]{:S(2)}) copy-start(f32[8,1536]{1,0:T(8,128)} %copy-done) | copy-start | bytes 147460

commit v2 on v1

--- a/solution.py
+++ b/solution.py
@@ -17,11 +17,12 @@
 CELLS = 4096
 FACES = 6
 FLIPPED = (1, 0, 3, 2, 5, 4)
-ROW = 4
-SLOTS = LANES // RANGE
+GROUP = 16
+PACKED = 3 * CELLS + LANES
 
 VMEM = pl.BlockSpec(memory_space=pltpu.VMEM)
-SMEM = pl.BlockSpec(memory_space=pltpu.SMEM)
+HBM = pl.BlockSpec(memory_space=pltpu.HBM)
+GRANT = 4 * 1024 * 1024
 
 
 def f32(*shape):
@@ -132,25 +133,47 @@
     return out
 
 
-def both(ref):
-    return jnp.concatenate([ref[0], ref[1]], axis=0)
-
-
 def range_base():
     return lax.axis_index("d") // 2 * RANGE
 
 
-def reorder_kernel(slot_ref, p_ref, f_ref, c_ref, links_ref, p_out, f_out, c_out, links_out, faces_out):
-    row = sublanes()
-    rows = jnp.zeros((RANGE, LANES), jnp.int32)
-    for i in range(RANGE):
-        rows = jnp.where(row == slot_ref[i // 4, i % 4], i, rows)
-    for source, target in ((p_ref, p_out), (f_ref, f_out), (c_ref, c_out)):
+def pack_kernel(p_ref, f_ref, c_ref, slot_ref, links_ref, out_ref, slots, links, sems):
+    small = [pltpu.make_async_copy(slot_ref, slots, sems.at[3]), pltpu.make_async_copy(links_ref, links, sems.at[4])]
+    large = [
+        pltpu.make_async_copy(ref, out_ref.at[:, i * CELLS : (i + 1) * CELLS], sems.at[i])
+        for i, ref in enumerate((p_ref, f_ref, c_ref))
+    ]
+    for copy in small + large:
+        copy.start()
+    for copy in small:
+        copy.wait()
+    lane = lanes()[: RANGE // 2]
+    row = sublanes()[: RANGE // 2]
+    tile = jnp.zeros((RANGE // 2, LANES), jnp.int32)
+    for d in range(FACES):
+        tile = jnp.where(lane == d, links[:, d : d + 1], tile)
+    for i in range(RANGE // 2):
+        tile = jnp.where(jnp.logical_and(lane == FACES, row == i), slots[i], tile)
+    out_ref[:, 3 * CELLS :] = tile.astype(jnp.float32)
+    for copy in large:
+        copy.wait()
+
+
+def reorder_kernel(packed_ref, p_out, f_out, c_out, links_out, faces_out):
+    def both(start):
+        span = slice(start, start + LANES)
+        return jnp.concatenate([packed_ref[0, :, span], packed_ref[1, :, span]], axis=0)
+
+    lane, row = lanes(), sublanes()
+    names = both(3 * CELLS)
+    links_out[...] = names.astype(jnp.int32)
+    slot = jnp.broadcast_to(names[:, FACES : FACES + 1], (RANGE, LANES)).astype(jnp.int32)
+    placed = jnp.sum(jnp.where(slot == lane, row, 0).astype(jnp.float32), axis=0, keepdims=True)
+    chosen = jnp.sum(jnp.where(lane == row, placed, 0.0), axis=1, keepdims=True)
+    rows = jnp.broadcast_to(chosen, (RANGE, LANES)).astype(jnp.int32)
+    for i, target in enumerate((p_out, f_out, c_out)):
         for t in range(CELLS // LANES):
-            span = slice(t * LANES, (t + 1) * LANES)
-            tile = jnp.concatenate([source[0, :, span], source[1, :, span]], axis=0)
-            target[t] = pick_rows(tile, rows)
-    links_out[...] = both(links_ref)
+            target[t] = pick_rows(both(i * CELLS + t * LANES), rows)
     store_faces(faces_out, pack_faces(load(p_out)))
 
 
@@ -174,16 +197,6 @@
 
 def face_sums(face):
     return [lane_sum(face(FLIPPED[d], 0) + face(FLIPPED[d], 1)) * (1.0 / CELLS) for d in range(FACES)]
-
-
-def to_lanes(columns, range_index):
-    at = lanes() == range_index % SLOTS * RANGE + sublanes()
-    row = sublanes()
-    tile = jnp.zeros((RANGE, LANES), jnp.float32)
-    for i, column in enumerate(columns):
-        spread = jnp.sum(jnp.where(at, column, 0.0), axis=0, keepdims=True)
-        tile = jnp.where(row == i, spread, tile)
-    return tile
 
 
 def smooth_kernel(u_ref, f_ref, c_ref, links_ref, faces_ref, pair_ref, u_out, faces_out, coarse_out):
@@ -205,31 +218,27 @@
     for s in sums:
         inner = inner - s
     diag = 6.0 + lane_sum(weights) * (1.0 / CELLS)
-    me = lax.axis_index("d") // 2
-    values = to_lanes(sums + [inner, diag], me)
-    names = to_lanes([links[:, d : d + 1].astype(jnp.float32) for d in range(FACES)], me)
-    for i in range(ROW):
-        coarse_out[i, 0:RANGE] = values
-        coarse_out[i, RANGE : 2 * RANGE] = names
-
-
-def row_kernel(coarse_ref, met_ref, out_ref):
-    me = lax.axis_index("d")
-    core, curve = me % 2, me // 2
-    edge = jnp.where(core == 0, curve % ROW == ROW - 1, curve % ROW == 0)
-    met = jnp.where(core == 0, curve + 1, curve + SLOTS - 1)
-    sums = to_lanes(face_sums(lambda f, h: load_face(met_ref, f, h)), met)
-    out_ref[0 : 2 * RANGE] = coarse_ref[0] + coarse_ref[1] + coarse_ref[2] + coarse_ref[3]
-    out_ref[2 * RANGE : 3 * RANGE] = jnp.where(edge, sums, 0.0)
-
-
-def final_kernel(u_ref, f_ref, c_ref, links_ref, faces_ref, met_ref, row_ref, rows_ref, out_ref):
+    lane = lanes()
+    tile = jnp.zeros((RANGE, LANES), jnp.float32)
+    for d in range(FACES):
+        tile = jnp.where(lane == d, sums[d], tile)
+        tile = jnp.where(lane == RANGE + d, links[:, d : d + 1].astype(jnp.float32), tile)
+    tile = jnp.where(lane == FACES, inner, tile)
+    tile = jnp.where(lane == FACES + 1, diag, tile)
+    for i in range(GROUP):
+        coarse_out[i] = tile
+
+
+def final_kernel(u_ref, f_ref, c_ref, links_ref, faces_ref, met_ref, coarse_ref, out_ref):
     core, curve = lax.axis_index("d") % 2, lax.axis_index("d") // 2
     row = sublanes()
-    spans = [slice(i * RANGE, (i + 1) * RANGE) for i in range(3)]
-    values = row_ref[spans[0]] + rows_ref[0, 0, spans[0]] + rows_ref[1, 1, spans[0]]
-    names = row_ref[spans[1]] + rows_ref[0, 0, spans[1]] + rows_ref[1, 1, spans[1]]
-    sums = values + rows_ref[0, 0, spans[2]] + rows_ref[1, 1, spans[2]]
+    nearest = []
+    for i in range(GROUP):
+        ahead = i - curve % GROUP
+        aligned = jnp.logical_and(ahead >= -GROUP // 2, ahead < GROUP // 2)
+        nearest.append(jnp.where(aligned, coarse_ref[0, i], coarse_ref[1, (i + GROUP // 2) % GROUP]))
+    values = jnp.concatenate(nearest, axis=0).T
+    sums, names = values[:RANGE], values[RANGE : 2 * RANGE]
     valid = jnp.logical_and(names >= 0.0, row < FACES)
     at = names.astype(jnp.int32) & (LANES - 1)
 
@@ -239,8 +248,8 @@
     def total(tile):
         return jnp.broadcast_to(jnp.sum(tile, axis=0, keepdims=True), (RANGE, LANES))
 
-    inner = jnp.broadcast_to(values[FACES : FACES + 1], (RANGE, LANES))
-    diag = jnp.broadcast_to(values[FACES + 1 : FACES + 2], (RANGE, LANES))
+    inner = jnp.broadcast_to(sums[FACES : FACES + 1], (RANGE, LANES))
+    diag = jnp.broadcast_to(sums[FACES + 1 : FACES + 2], (RANGE, LANES))
     diag = jnp.where(diag > 0.0, diag, 1.0)
     residual = inner + total(named(sums))
     error = jnp.zeros((RANGE, LANES), jnp.float32)
@@ -248,7 +257,7 @@
         near = total(named(error)) if step else 0.0
         error = error + RELAXATION * (residual - diag * error + near) / diag
     near = named(error)
-    own = lanes() == curve % SLOTS * RANGE + row
+    own = lanes() == curve % GROUP * RANGE + row
     lift = lane_sum(jnp.where(own, error, 0.0))
     before = lambda f, h: load_face(met_ref, f, h, 1)
     mine = lambda f, h: load_face(faces_ref, f, h)
@@ -267,49 +276,55 @@
             out_ref[:, t * LANES : (t + 1) * LANES] = half
 
 
-def call(kernel, out_shape, name, *args, scalars=0):
+def call(kernel, out_shape, name, *args, specs=None, scratch=()):
     many = isinstance(out_shape, (list, tuple))
     return pl.pallas_call(
         kernel,
         out_shape=out_shape,
-        in_specs=[SMEM] * scalars + [VMEM] * (len(args) - scalars),
+        in_specs=specs or [VMEM] * len(args),
         out_specs=[VMEM] * len(out_shape) if many else VMEM,
+        scratch_shapes=scratch,
+        compiler_params=pltpu.CompilerParams(vmem_limit_bytes=GRANT),
         name=name,
     )(*args)
 
 
 def on_device(groups, pressure, source_term, coefficient, new_slot, face_links):
-    cores, pairs, rows, row_pairs, exchange = groups
+    cores, pairs, groups16, exchange = groups
     gather = lambda array, members: lax.all_gather(array, "d", axis=0, axis_index_groups=members)
     field = f32(CELLS // LANES, RANGE, LANES)
     packed = f32(RANGE, FACES * 2 * LANES)
-    p, f, c, slots, links = [
-        gather(array, cores) for array in (pressure, source_term, coefficient, new_slot, face_links)
-    ]
+    whole = call(
+        pack_kernel,
+        f32(RANGE // 2, PACKED),
+        "pack",
+        *[
+            pltpu.with_memory_space_constraint(array, pltpu.HBM)
+            for array in (pressure, source_term, coefficient, new_slot, face_links)
+        ],
+        specs=[HBM] * 5,
+        scratch=[
+            pltpu.SMEM((RANGE // 2,), jnp.int32),
+            pltpu.VMEM((RANGE // 2, FACES), jnp.int32),
+            pltpu.SemaphoreType.DMA((5,)),
+        ],
+    )
     u, f, c, links, faces = call(
         reorder_kernel,
-        [field, field, field, jax.ShapeDtypeStruct((RANGE, FACES), jnp.int32), packed],
+        [field, field, field, jax.ShapeDtypeStruct((RANGE, LANES), jnp.int32), packed],
         "reorder",
-        slots,
-        p,
-        f,
-        c,
-        links,
-        scalars=1,
+        gather(whole, cores),
     )
     pair = gather(gather(faces, pairs), cores)
     u, faces = call(sweep_kernel, [field, packed], "sweep", u, f, c, links, faces, pair)
     pair = gather(gather(faces, pairs), cores)
     u, faces, coarse = call(
-        smooth_kernel, [field, packed, f32(ROW, 2 * RANGE, LANES)], "smooth", u, f, c, links, faces, pair
+        smooth_kernel, [field, packed, f32(GROUP, RANGE, LANES)], "smooth", u, f, c, links, faces, pair
     )
     met = lax.ppermute(faces, "d", exchange)
-    coarse = lax.all_to_all(coarse, "d", 0, 0, axis_index_groups=rows, tiled=True)
-    row = call(row_kernel, f32(3 * RANGE, LANES), "row", coarse, met)
-    met, near_rows = gather(met, cores), gather(gather(row, row_pairs), cores)
-    return call(
-        final_kernel, f32(RANGE // 2, CELLS), "final", u, f, c, links, faces, met, row, near_rows
-    )
+    coarse = lax.all_to_all(coarse, "d", 0, 0, axis_index_groups=groups16, tiled=True)
+    met, coarse = gather(met, cores), gather(coarse, cores)
+    return call(final_kernel, f32(RANGE // 2, CELLS), "final", u, f, c, links, faces, met, coarse)
 
 
 def solution(mesh):
@@ -317,12 +332,15 @@
     count = devices.size // 2
     cores = [[2 * i, 2 * i + 1] for i in range(count)]
     pairs = [[2 * i, 2 * i + 3] for i in range(count - 1)] + [[2 * count - 2, 1]]
-    rows = [[2 * (i + k) + core for k in range(ROW)] for i in range(0, count, ROW) for core in range(2)]
-    row_pairs = [[2 * i + 1, 2 * ((i + ROW) % count)] for i in range(count)]
+    groups16 = [
+        [2 * ((i + core * GROUP // 2 + k) % count) + core for k in range(GROUP)]
+        for i in range(0, count, GROUP)
+        for core in range(2)
+    ]
     exchange = [pair for i in range(count - 1) for pair in ((2 * i, 2 * i + 3), (2 * i + 3, 2 * i))]
     split, line = P("d", None), P("d")
     return jax.shard_map(
-        functools.partial(on_device, (cores, pairs, rows, row_pairs, exchange)),
+        functools.partial(on_device, (cores, pairs, groups16, exchange)),
         mesh=Mesh(devices, ("d",)),
         in_specs=(split, split, split, line, split),
         out_specs=split,

time: 84.6 us -> 61.3 us (0.72)
  the two profiles are of different devices: /device:TPU:1 before, /device:TPU:9 now
where the time goes in v2:
time: 61.3 us; the launch traced here: 61 us
  starting transfers between devices  28.4 us (46%)
  blocking collectives  22.6 us (37%)
  waiting for transfers between devices  5.59 us (9%)
  Pallas kernels  4.35 us (7%)
    all_to_all x1, starting transfers between devices, on_device(): lax.all_to_all(coarse, 'd', 0, 0, axis_index_groups=groups16, tiled=True)  26.5 us
    all_gather x7, blocking collectives, on_device(): lax.all_gather(array, 'd', axis=0, axis_index_groups=members)  22.6 us
    ppermute x1, waiting for transfers between devices, on_device(): met = lax.ppermute(faces, 'd', exchange)  5.59 us
    pallas_call x5, Pallas kernels, call(): pl.pallas_call(kernel, out_shape=out_shape, in_specs=specs or [VMEM] * le...  4.35 us
    ppermute x1, starting transfers between devices, on_device(): met = lax.ppermute(faces, 'd', exchange)  1.91 us
  transfers between devices with their start and end apart: 2, of which 1 were waited for; matrix products, arithmetic and copies ran while one was open for 0% of the time, Pallas kernels for 0%

profile of v2, /device:TPU:9, one launch (start us, length us, event | category | flops | bytes accessed | tf_op | source)
XLA Modules:
  0.0 61.0 jit_solution(11150983628020350888)
XLA Ops:
  0.0 1.0 %pack.1 = f32[4,12416]{1,0:T(4,128)S(1)} custom-call(f32[4,4096]{1,0:T(4,128)} %p_ref.1, f32[4,4096]{1,0:T(4,128)} %f_ref.1, f32[4,4096]{1,0:T(4,128)} %c_ref.1, s32[4]{0:T(128)} %slot_ref.1, s32[4,6]{1,0:T(4,128)} %links_ref.1), custom_call_target="tpu_custom_call" | custom-call | tf_op jit(solution)/shard_map/pack/pallas_call | solution.py:281
  1.0 2.4 %all-gather.7.packed_ref = f32[2,4,12416]{2,1,0:T(4,128)S(1)} all-gather(f32[1,4,12416]{2,1,0:T(4,128)S(1)} %bitcast.7), channel_id=2, replica_groups={{0,1},{2,3},{4,5},{6,7},{8,9},{10,11},{12,13},{14,15},{16,17},{18,19},{..., dimensions={0}, use_global_device_ids=true | all-gather | bytes 595968 | tf_op jit(solution)/shard_map/all_gather | solution.py:294
  3.4 0.3 reorder.1
  3.7 6.3 %all-gather.1 = f32[16,1536]{1,0:T(8,128)S(1)} all-gather(f32[8,1536]{1,0:T(8,128)S(1)} %get-tuple-element.19.faces_ref), channel_id=3, replica_groups={{0,3},{2,5},{4,7},{6,9},{8,11},{10,13},{12,15},{14,17},{16,19},{18,21},..., dimensions={0}, use_global_device_ids=true | all-gather | bytes 147456 | tf_op jit(solution)/shard_map/all_gather | solution.py:294
  10.0 1.9 %all-gather.2 = f32[4,8,1536]{2,1,0:T(8,128)S(1)} all-gather(f32[2,8,1536]{2,1,0:T(8,128)S(1)} %bitcast.12), channel_id=4, replica_groups={{0,1},{2,3},{4,5},{6,7},{8,9},{10,11},{12,13},{14,15},{16,17},{18,19},{..., dimensions={0}, use_global_device_ids=true | all-gather | bytes 294912 | tf_op jit(solution)/shard_map/all_gather | solution.py:294
  11.9 0.4 sweep.1
  12.4 6.3 %all-gather.3 = f32[16,1536]{1,0:T(8,128)S(1)} all-gather(f32[8,1536]{1,0:T(8,128)S(1)} %get-tuple-element.21.faces_ref), channel_id=5, replica_groups={{0,3},{2,5},{4,7},{6,9},{8,11},{10,13},{12,15},{14,17},{16,19},{18,21},..., dimensions={0}, use_global_device_ids=true | all-gather | bytes 147456 | tf_op jit(solution)/shard_map/all_gather | solution.py:294
  18.7 1.9 %all-gather.4 = f32[4,8,1536]{2,1,0:T(8,128)S(1)} all-gather(f32[2,8,1536]{2,1,0:T(8,128)S(1)} %bitcast.13), channel_id=6, replica_groups={{0,1},{2,3},{4,5},{6,7},{8,9},{10,11},{12,13},{14,15},{16,17},{18,19},{..., dimensions={0}, use_global_device_ids=true | all-gather | bytes 294912 | tf_op jit(solution)/shard_map/all_gather | solution.py:294
  20.6 1.2 %smooth.1 = (f32[32,8,128]{2,1,0:T(8,128)S(1)}, f32[8,1536]{1,0:T(8,128)S(1)}, f32[16,8,128]{2,1,0:T(8,128)}) custom-call(f32[32,8,128]{2,1,0:T(8,128)S(1)} %get-tuple-element.20.u_ref, f32[32,8,128]{2,1,0:T(8,128)S(1)} %get-tuple-element.16.f_ref, f32[32,8,128]{2,1,0:T(8,128)S(1)} %get-tuple-element.17.c_ref, s32[8,128]{1,0:T(8,128)S(1)} %get-tuple-element.18.links_ref, ...), custom_call_target="tpu_custom_call" | custom-call | tf_op jit(solution)/shard_map/smooth/pallas_call | solution.py:281
  21.8 26.5 %all-to-all-start = ((f32[16,8,128]{2,1,0:T(8,128)}), f32[16,8,128]{2,1,0:T(8,128)S(1)}, u32[]{:S(2)}, u32[]{:S(2)}) async-start(f32[16,8,128]{2,1,0:T(8,128)} %get-tuple-element.24), calls=%async_computation | async-start | bytes 131072 | tf_op jit(solution)/shard_map/all_to_all | solution.py:325
  48.3 1.9 %collective-permute-start = (f32[8,1536]{1,0:T(8,128)S(1)}, f32[8,1536]{1,0:T(8,128)S(1)}, u32[]{:S(2)}, u32[]{:S(2)}) collective-permute-start(f32[8,1536]{1,0:T(8,128)S(1)} %get-tuple-element.23.faces_ref), channel_id=1, source_target_pairs={{0,3},{3,0},{2,5},{5,2},{4,7},{7,4},{6,9},{9,6},{8,11},{11,8},{10,... | collective-permute-start | bytes 147464 | tf_op jit(solution)/shard_map/ppermute | solution.py:324
  50.2 5.6 %collective-permute-done = f32[8,1536]{1,0:T(8,128)S(1)} collective-permute-done((f32[8,1536]{1,0:T(8,128)S(1)}, f32[8,1536]{1,0:T(8,128)S(1)}, u32[]{:S(2)}, u32[]{:S(2)}) %collective-permute-start) | collective-permute-done | bytes 49184 | tf_op jit(solution)/shard_map/ppermute | solution.py:324
  55.8 1.9 %all-gather.5 = f32[16,1536]{1,0:T(8,128)S(1)} all-gather(f32[8,1536]{1,0:T(8,128)S(1)} %collective-permute-done), channel_id=7, replica_groups={{0,1},{2,3},{4,5},{6,7},{8,9},{10,11},{12,13},{14,15},{16,17},{18,19},{..., dimensions={0}, use_global_device_ids=true | all-gather | bytes 147456 | tf_op jit(solution)/shard_map/all_gather | solution.py:294
  57.7 0.0 all-to-all-done
  57.7 1.9 %all-gather.6 = f32[32,8,128]{2,1,0:T(8,128)S(1)} all-gather(f32[16,8,128]{2,1,0:T(8,128)S(1)} %all-to-all-done), channel_id=8, replica_groups={{0,1},{2,3},{4,5},{6,7},{8,9},{10,11},{12,13},{14,15},{16,17},{18,19},{..., dimensions={0}, use_global_device_ids=true | all-gather | bytes 196608 | tf_op jit(solution)/shard_map/all_gather | solution.py:294
  59.6 1.4 %final.1 = f32[4,4096]{1,0:T(4,128)} custom-call(f32[32,8,128]{2,1,0:T(8,128)S(1)} %get-tuple-element.22.u_ref, f32[32,8,128]{2,1,0:T(8,128)S(1)} %get-tuple-element.16.f_ref, f32[32,8,128]{2,1,0:T(8,128)S(1)} %get-tuple-element.17.c_ref, s32[8,128]{1,0:T(8,128)S(1)} %get-tuple-element.18.links_ref, f32[8,1536]{1,0:T(8,128)S(1)} %get-tuple-element.23.faces_ref, ...), custom_call_target="tpu_custom_call" | custom-call | tf_op jit(solution)/shard_map/final/pallas_call | solution.py:281
Async XLA Ops:
  21.8 35.9 %all-to-all-start = ((f32[16,8,128]{2,1,0:T(8,128)}), f32[16,8,128]{2,1,0:T(8,128)S(1)}, u32[]{:S(2)}, u32[]{:S(2)}) async-start(f32[16,8,128]{2,1,0:T(8,128)} %get-tuple-element.24), calls=%async_computation | async-start | bytes 131072 | tf_op jit(solution)/shard_map/all_to_all | solution.py:325
  48.3 7.5 %collective-permute-start = (f32[8,1536]{1,0:T(8,128)S(1)}, f32[8,1536]{1,0:T(8,128)S(1)}, u32[]{:S(2)}, u32[]{:S(2)}) collective-permute-start(f32[8,1536]{1,0:T(8,128)S(1)} %get-tuple-element.23.faces_ref), channel_id=1, source_target_pairs={{0,3},{3,0},{2,5},{5,2},{4,7},{7,4},{6,9},{9,6},{8,11},{11,8},{10,... | collective-permute-start | bytes 147464 | tf_op jit(solution)/shard_map/ppermute | solution.py:324

commit v3 on v2

--- a/solution.py
+++ b/solution.py
@@ -76,6 +76,11 @@
 
 def load_face(ref, f, h, *lead):
     return ref[(*lead, slice(None), slice((2 * f + h) * LANES, (2 * f + h + 1) * LANES))]
+
+
+def load_coarse(ref, core, member):
+    start = (2 * FACES + member) * LANES
+    return ref[core, :, start : start + LANES]
 
 
 def pick_rows(tile, rows):
@@ -177,15 +182,15 @@
     store_faces(faces_out, pack_faces(load(p_out)))
 
 
-def window(pair_ref, faces_ref):
-    before = lambda f, h: load_face(pair_ref, f, h, 1, 0)
+def window(met_ref, faces_ref):
+    before = lambda f, h: load_face(met_ref, f, h, 1)
     own = lambda f, h: load_face(faces_ref, f, h)
-    after = lambda f, h: load_face(pair_ref, f, h, 0, 1)
+    after = lambda f, h: load_face(met_ref, f, h, 0)
     return before, own, after
 
 
-def sweep_kernel(u_ref, f_ref, c_ref, links_ref, faces_ref, pair_ref, u_out, faces_out):
-    ghosts, _ = ghost_faces(links_ref[...], range_base(), *window(pair_ref, faces_ref))
+def sweep_kernel(u_ref, f_ref, c_ref, links_ref, faces_ref, met_ref, u_out, faces_out):
+    ghosts, _ = ghost_faces(links_ref[...], range_base(), *window(met_ref, faces_ref))
     tiles = sweep(load(u_ref), ghosts, f_ref, c_ref)
     store(u_out, tiles)
     store_faces(faces_out, pack_faces(tiles))
@@ -199,9 +204,9 @@
     return [lane_sum(face(FLIPPED[d], 0) + face(FLIPPED[d], 1)) * (1.0 / CELLS) for d in range(FACES)]
 
 
-def smooth_kernel(u_ref, f_ref, c_ref, links_ref, faces_ref, pair_ref, u_out, faces_out, coarse_out):
+def smooth_kernel(u_ref, f_ref, c_ref, links_ref, faces_ref, met_ref, u_out, faces_out, coarse_out):
     links = links_ref[...]
-    ghosts, _ = ghost_faces(links, range_base(), *window(pair_ref, faces_ref))
+    ghosts, _ = ghost_faces(links, range_base(), *window(met_ref, faces_ref))
     tiles = sweep(load(u_ref), ghosts, f_ref, c_ref)
     store(u_out, tiles)
     faces = pack_faces(tiles)
@@ -229,14 +234,23 @@
         coarse_out[i] = tile
 
 
-def final_kernel(u_ref, f_ref, c_ref, links_ref, faces_ref, met_ref, coarse_ref, out_ref):
+def join_kernel(met_ref, coarse_ref, out_ref):
+    width = FACES * 2 * LANES
+    out_ref[:, :width] = met_ref[...]
+    for i in range(GROUP):
+        out_ref[:, width + i * LANES : width + (i + 1) * LANES] = coarse_ref[i]
+
+
+def final_kernel(u_ref, f_ref, c_ref, links_ref, faces_ref, met_ref, out_ref):
     core, curve = lax.axis_index("d") % 2, lax.axis_index("d") // 2
     row = sublanes()
     nearest = []
     for i in range(GROUP):
         ahead = i - curve % GROUP
         aligned = jnp.logical_and(ahead >= -GROUP // 2, ahead < GROUP // 2)
-        nearest.append(jnp.where(aligned, coarse_ref[0, i], coarse_ref[1, (i + GROUP // 2) % GROUP]))
+        first = load_coarse(met_ref, 0, i)
+        second = load_coarse(met_ref, 1, (i + GROUP // 2) % GROUP)
+        nearest.append(jnp.where(aligned, first, second))
     values = jnp.concatenate(nearest, axis=0).T
     sums, names = values[:RANGE], values[RANGE : 2 * RANGE]
     valid = jnp.logical_and(names >= 0.0, row < FACES)
@@ -259,10 +273,7 @@
     near = named(error)
     own = lanes() == curve % GROUP * RANGE + row
     lift = lane_sum(jnp.where(own, error, 0.0))
-    before = lambda f, h: load_face(met_ref, f, h, 1)
-    mine = lambda f, h: load_face(faces_ref, f, h)
-    after = lambda f, h: load_face(met_ref, f, h, 0)
-    ghosts, _ = ghost_faces(links_ref[...], range_base(), before, mine, after)
+    ghosts, _ = ghost_faces(links_ref[...], range_base(), *window(met_ref, faces_ref))
     for d in range(FACES):
         raised = lane_sum(jnp.where(own, jnp.broadcast_to(near[d : d + 1], (RANGE, LANES)), 0.0))
         ghosts[d] = [half + raised for half in ghosts[d]]
@@ -290,7 +301,8 @@
 
 
 def on_device(groups, pressure, source_term, coefficient, new_slot, face_links):
-    cores, pairs, groups16, exchange = groups
+    cores, groups16, exchange = groups
+    meet = lambda array: lax.ppermute(array, "d", exchange)
     gather = lambda array, members: lax.all_gather(array, "d", axis=0, axis_index_groups=members)
     field = f32(CELLS // LANES, RANGE, LANES)
     packed = f32(RANGE, FACES * 2 * LANES)
@@ -315,23 +327,22 @@
         "reorder",
         gather(whole, cores),
     )
-    pair = gather(gather(faces, pairs), cores)
-    u, faces = call(sweep_kernel, [field, packed], "sweep", u, f, c, links, faces, pair)
-    pair = gather(gather(faces, pairs), cores)
+    met = gather(meet(faces), cores)
+    u, faces = call(sweep_kernel, [field, packed], "sweep", u, f, c, links, faces, met)
+    met = gather(meet(faces), cores)
     u, faces, coarse = call(
-        smooth_kernel, [field, packed, f32(GROUP, RANGE, LANES)], "smooth", u, f, c, links, faces, pair
+        smooth_kernel, [field, packed, f32(GROUP, RANGE, LANES)], "smooth", u, f, c, links, faces, met
     )
-    met = lax.ppermute(faces, "d", exchange)
+    met = meet(faces)
     coarse = lax.all_to_all(coarse, "d", 0, 0, axis_index_groups=groups16, tiled=True)
-    met, coarse = gather(met, cores), gather(coarse, cores)
-    return call(final_kernel, f32(RANGE // 2, CELLS), "final", u, f, c, links, faces, met, coarse)
+    joined = call(join_kernel, f32(RANGE, (2 * FACES + GROUP) * LANES), "join", met, coarse)
+    return call(final_kernel, f32(RANGE // 2, CELLS), "final", u, f, c, links, faces, gather(joined, cores))
 
 
 def solution(mesh):
     devices = mesh.devices.reshape(-1)
     count = devices.size // 2
     cores = [[2 * i, 2 * i + 1] for i in range(count)]
-    pairs = [[2 * i, 2 * i + 3] for i in range(count - 1)] + [[2 * count - 2, 1]]
     groups16 = [
         [2 * ((i + core * GROUP // 2 + k) % count) + core for k in range(GROUP)]
         for i in range(0, count, GROUP)
@@ -340,7 +351,7 @@
     exchange = [pair for i in range(count - 1) for pair in ((2 * i, 2 * i + 3), (2 * i + 3, 2 * i))]
     split, line = P("d", None), P("d")
     return jax.shard_map(
-        functools.partial(on_device, (cores, pairs, groups16, exchange)),
+        functools.partial(on_device, (cores, groups16, exchange)),
         mesh=Mesh(devices, ("d",)),
         in_specs=(split, split, split, line, split),
         out_specs=split,

time: 61.3 us -> 55.1 us (0.90)
  blocking collectives: 22.6 us -> 8.09 us
  waiting for transfers between devices: 5.59 us -> 11.6 us
  starting transfers between devices: 28.4 us -> 30.7 us
    all_gather x7 -> x4, blocking collectives: 22.6 us -> 8.09 us  [on_device(): lax.all_gather(array, 'd', axis=0, axis_index_groups=members)]
    ppermute x1 -> x3, starting transfers between devices: 1.91 us -> 11 us  [on_device(): meet = lambda array: lax.ppermute(array, 'd', exchange)]
    all_to_all x1, starting transfers between devices: 26.5 us -> 19.8 us  [on_device(): lax.all_to_all(coarse, 'd', 0, 0, axis_index_groups=groups16, tiled=True)]
    ppermute x1 -> x3, waiting for transfers between devices: 5.59 us -> 11.5 us  [on_device(): meet = lambda array: lax.ppermute(array, 'd', exchange)]
    pallas_call x5 -> x6, Pallas kernels: 4.35 us -> 4.36 us  [call(): pl.pallas_call(kernel, out_shape=out_shape, in_specs=specs or [VMEM] * le...]
  transfers between devices with their start and end apart: 2 -> 4, of which waited for: 1 -> 3; matrix products, arithmetic and copies ran while one was open for 0% -> 0% of each run, Pallas kernels for 0% -> 0%
where the time goes in v3:
time: 55.1 us; the launch traced here: 54.8 us
  starting transfers between devices  30.7 us (56%)
  waiting for transfers between devices  11.6 us (21%)
  blocking collectives  8.09 us (15%)
  Pallas kernels  4.36 us (8%)
    all_to_all x1, starting transfers between devices, on_device(): lax.all_to_all(coarse, 'd', 0, 0, axis_index_groups=groups16, tiled=True)  19.8 us
    ppermute x3, waiting for transfers between devices, on_device(): meet = lambda array: lax.ppermute(array, 'd', exchange)  11.5 us
    ppermute x3, starting transfers between devices, on_device(): meet = lambda array: lax.ppermute(array, 'd', exchange)  11 us
    all_gather x4, blocking collectives, on_device(): lax.all_gather(array, 'd', axis=0, axis_index_groups=members)  8.09 us
    pallas_call x6, Pallas kernels, call(): pl.pallas_call(kernel, out_shape=out_shape, in_specs=specs or [VMEM] * le...  4.36 us
  transfers between devices with their start and end apart: 4, of which 3 were waited for; matrix products, arithmetic and copies ran while one was open for 0% of the time, Pallas kernels for 0%

profile of v3, /device:TPU:9, one launch (start us, length us, event | category | flops | bytes accessed | tf_op | source)
XLA Modules:
  0.0 54.8 jit_solution(14671591464604538703)
XLA Ops:
  0.0 1.0 %pack.1 = f32[4,12416]{1,0:T(4,128)S(1)} custom-call(f32[4,4096]{1,0:T(4,128)} %p_ref.1, f32[4,4096]{1,0:T(4,128)} %f_ref.1, f32[4,4096]{1,0:T(4,128)} %c_ref.1, s32[4]{0:T(128)} %slot_ref.1, s32[4,6]{1,0:T(4,128)} %links_ref.1), custom_call_target="tpu_custom_call" | custom-call | tf_op jit(solution)/shard_map/pack/pallas_call | solution.py:292
  1.0 2.4 %all-gather.4.packed_ref = f32[2,4,12416]{2,1,0:T(4,128)S(1)} all-gather(f32[1,4,12416]{2,1,0:T(4,128)S(1)} %bitcast.5), channel_id=2, replica_groups={{0,1},{2,3},{4,5},{6,7},{8,9},{10,11},{12,13},{14,15},{16,17},{18,19},{..., dimensions={0}, use_global_device_ids=true | all-gather | bytes 595968 | tf_op jit(solution)/shard_map/all_gather | solution.py:306
  3.4 0.3 reorder.1
  3.7 4.5 %collective-permute-start = (f32[8,1536]{1,0:T(8,128)S(1)}, f32[8,1536]{1,0:T(8,128)S(1)}, u32[]{:S(2)}, u32[]{:S(2)}) collective-permute-start(f32[8,1536]{1,0:T(8,128)S(1)} %get-tuple-element.19.faces_ref), channel_id=1, source_target_pairs={{0,3},{3,0},{2,5},{5,2},{4,7},{7,4},{6,9},{9,6},{8,11},{11,8},{10,... | collective-permute-start | bytes 147464 | tf_op jit(solution)/shard_map/ppermute | solution.py:305
  8.2 3.0 %collective-permute-done = f32[8,1536]{1,0:T(8,128)S(1)} collective-permute-done((f32[8,1536]{1,0:T(8,128)S(1)}, f32[8,1536]{1,0:T(8,128)S(1)}, u32[]{:S(2)}, u32[]{:S(2)}) %collective-permute-start) | collective-permute-done | bytes 49184 | tf_op jit(solution)/shard_map/ppermute | solution.py:305
  11.2 1.9 %all-gather.1 = f32[16,1536]{1,0:T(8,128)S(1)} all-gather(f32[8,1536]{1,0:T(8,128)S(1)} %collective-permute-done), channel_id=3, replica_groups={{0,1},{2,3},{4,5},{6,7},{8,9},{10,11},{12,13},{14,15},{16,17},{18,19},{..., dimensions={0}, use_global_device_ids=true | all-gather | bytes 147456 | tf_op jit(solution)/shard_map/all_gather | solution.py:306
  13.1 0.4 sweep.1
  13.5 4.5 %collective-permute-start.1 = (f32[8,1536]{1,0:T(8,128)S(1)}, f32[8,1536]{1,0:T(8,128)S(1)}, u32[]{:S(2)}, u32[]{:S(2)}) collective-permute-start(f32[8,1536]{1,0:T(8,128)S(1)} %get-tuple-element.21.faces_ref), channel_id=1, source_target_pairs={{0,3},{3,0},{2,5},{5,2},{4,7},{7,4},{6,9},{9,6},{8,11},{11,8},{10,... | collective-permute-start | bytes 147464 | tf_op jit(solution)/shard_map/ppermute | solution.py:305
  18.1 3.0 %collective-permute-done.1 = f32[8,1536]{1,0:T(8,128)S(1)} collective-permute-done((f32[8,1536]{1,0:T(8,128)S(1)}, f32[8,1536]{1,0:T(8,128)S(1)}, u32[]{:S(2)}, u32[]{:S(2)}) %collective-permute-start.1) | collective-permute-done | bytes 49184 | tf_op jit(solution)/shard_map/ppermute | solution.py:305
  21.1 1.9 %all-gather.2 = f32[16,1536]{1,0:T(8,128)S(1)} all-gather(f32[8,1536]{1,0:T(8,128)S(1)} %collective-permute-done.1), channel_id=4, replica_groups={{0,1},{2,3},{4,5},{6,7},{8,9},{10,11},{12,13},{14,15},{16,17},{18,19},{..., dimensions={0}, use_global_device_ids=true | all-gather | bytes 147456 | tf_op jit(solution)/shard_map/all_gather | solution.py:306
  22.9 1.2 %smooth.1 = (f32[32,8,128]{2,1,0:T(8,128)S(1)}, f32[8,1536]{1,0:T(8,128)S(1)}, f32[16,8,128]{2,1,0:T(8,128)}) custom-call(f32[32,8,128]{2,1,0:T(8,128)S(1)} %get-tuple-element.20.u_ref, f32[32,8,128]{2,1,0:T(8,128)S(1)} %get-tuple-element.16.f_ref, f32[32,8,128]{2,1,0:T(8,128)S(1)} %get-tuple-element.17.c_ref, s32[8,128]{1,0:T(8,128)S(1)} %get-tuple-element.18.links_ref, ...), custom_call_target="tpu_custom_call" | custom-call | tf_op jit(solution)/shard_map/smooth/pallas_call | solution.py:292
  24.1 19.8 %all-to-all-start = ((f32[16,8,128]{2,1,0:T(8,128)}), f32[16,8,128]{2,1,0:T(8,128)S(1)}, u32[]{:S(2)}, u32[]{:S(2)}) async-start(f32[16,8,128]{2,1,0:T(8,128)} %get-tuple-element.24), calls=%async_computation | async-start | bytes 131072 | tf_op jit(solution)/shard_map/all_to_all | solution.py:337
  43.9 1.9 %collective-permute-start.2 = (f32[8,1536]{1,0:T(8,128)S(1)}, f32[8,1536]{1,0:T(8,128)S(1)}, u32[]{:S(2)}, u32[]{:S(2)}) collective-permute-start(f32[8,1536]{1,0:T(8,128)S(1)} %get-tuple-element.23.faces_ref), channel_id=1, source_target_pairs={{0,3},{3,0},{2,5},{5,2},{4,7},{7,4},{6,9},{9,6},{8,11},{11,8},{10,... | collective-permute-start | bytes 147464 | tf_op jit(solution)/shard_map/ppermute | solution.py:305
  45.8 5.6 %collective-permute-done.2.met_ref = f32[8,1536]{1,0:T(8,128)S(1)} collective-permute-done((f32[8,1536]{1,0:T(8,128)S(1)}, f32[8,1536]{1,0:T(8,128)S(1)}, u32[]{:S(2)}, u32[]{:S(2)}) %collective-permute-start.2) | collective-permute-done | bytes 49184 | tf_op jit(solution)/shard_map/ppermute | solution.py:305
  51.4 0.0 all-to-all-done.coarse_ref
  51.4 2.0 %all-gather.3 = f32[16,3584]{1,0:T(8,128)S(1)} all-gather(f32[8,3584]{1,0:T(8,128)S(1)} %join.1), channel_id=5, replica_groups={{0,1},{2,3},{4,5},{6,7},{8,9},{10,11},{12,13},{14,15},{16,17},{18,19},{..., dimensions={0}, use_global_device_ids=true | all-gather | bytes 344064 | tf_op jit(solution)/shard_map/all_gather | solution.py:306
  53.4 1.4 %final.1 = f32[4,4096]{1,0:T(4,128)} custom-call(f32[32,8,128]{2,1,0:T(8,128)S(1)} %get-tuple-element.22.u_ref, f32[32,8,128]{2,1,0:T(8,128)S(1)} %get-tuple-element.16.f_ref, f32[32,8,128]{2,1,0:T(8,128)S(1)} %get-tuple-element.17.c_ref, s32[8,128]{1,0:T(8,128)S(1)} %get-tuple-element.18.links_ref, f32[8,1536]{1,0:T(8,128)S(1)} %get-tuple-element.23.faces_ref, ...), custom_call_target="tpu_custom_call" | custom-call | tf_op jit(solution)/shard_map/final/pallas_call | solution.py:292
  (1 shorter events, 0.0 us)
Async XLA Ops:
  3.7 7.5 %collective-permute-start = (f32[8,1536]{1,0:T(8,128)S(1)}, f32[8,1536]{1,0:T(8,128)S(1)}, u32[]{:S(2)}, u32[]{:S(2)}) collective-permute-start(f32[8,1536]{1,0:T(8,128)S(1)} %get-tuple-element.19.faces_ref), channel_id=1, source_target_pairs={{0,3},{3,0},{2,5},{5,2},{4,7},{7,4},{6,9},{9,6},{8,11},{11,8},{10,... | collective-permute-start | bytes 147464 | tf_op jit(solution)/shard_map/ppermute | solution.py:305
  13.5 7.5 %collective-permute-start.1 = (f32[8,1536]{1,0:T(8,128)S(1)}, f32[8,1536]{1,0:T(8,128)S(1)}, u32[]{:S(2)}, u32[]{:S(2)}) collective-permute-start(f32[8,1536]{1,0:T(8,128)S(1)} %get-tuple-element.21.faces_ref), channel_id=1, source_target_pairs={{0,3},{3,0},{2,5},{5,2},{4,7},{7,4},{6,9},{9,6},{8,11},{11,8},{10,... | collective-permute-start | bytes 147464 | tf_op jit(solution)/shard_map/ppermute | solution.py:305
  24.1 27.3 %all-to-all-start = ((f32[16,8,128]{2,1,0:T(8,128)}), f32[16,8,128]{2,1,0:T(8,128)S(1)}, u32[]{:S(2)}, u32[]{:S(2)}) async-start(f32[16,8,128]{2,1,0:T(8,128)} %get-tuple-element.24), calls=%async_computation | async-start | bytes 131072 | tf_op jit(solution)/shard_map/all_to_all | solution.py:337
  43.9 7.5 %collective-permute-start.2 = (f32[8,1536]{1,0:T(8,128)S(1)}, f32[8,1536]{1,0:T(8,128)S(1)}, u32[]{:S(2)}, u32[]{:S(2)}) collective-permute-start(f32[8,1536]{1,0:T(8,128)S(1)} %get-tuple-element.23.faces_ref), channel_id=1, source_target_pairs={{0,3},{3,0},{2,5},{5,2},{4,7},{7,4},{6,9},{9,6},{8,11},{11,8},{10,... | collective-permute-start | bytes 147464 | tf_op jit(solution)/shard_map/ppermute | solution.py:305

commit v4 on v3

--- a/solution.py
+++ b/solution.py
@@ -7,7 +7,7 @@
 from jax.experimental.pallas import tpu as pltpu
 from jax.sharding import Mesh, PartitionSpec as P
 
-PRE_SWEEPS = 2
+
 COARSE_SWEEPS = 4
 RELAXATION = 0.8
 
@@ -204,21 +204,15 @@
     return [lane_sum(face(FLIPPED[d], 0) + face(FLIPPED[d], 1)) * (1.0 / CELLS) for d in range(FACES)]
 
 
-def smooth_kernel(u_ref, f_ref, c_ref, links_ref, faces_ref, met_ref, u_out, faces_out, coarse_out):
+def coarse_kernel(u_ref, f_ref, c_ref, links_ref, faces_ref, coarse_out):
     links = links_ref[...]
-    ghosts, _ = ghost_faces(links, range_base(), *window(met_ref, faces_ref))
-    tiles = sweep(load(u_ref), ghosts, f_ref, c_ref)
-    store(u_out, tiles)
-    faces = pack_faces(tiles)
-    store_faces(faces_out, faces)
     defect = jnp.zeros((RANGE, LANES), jnp.float32)
     weights = jnp.zeros((RANGE, LANES), jnp.float32)
-    for x in range(SIDE):
-        for h in range(2):
-            c = c_ref[2 * x + h]
-            defect = defect + (f_ref[2 * x + h] - c * tiles[x][h])
-            weights = weights + c
-    sums = face_sums(lambda f, h: faces[f][h])
+    for t in range(CELLS // LANES):
+        c = c_ref[t]
+        defect = defect + (f_ref[t] - c * u_ref[t])
+        weights = weights + c
+    sums = face_sums(lambda f, h: load_face(faces_ref, f, h))
     inner = lane_sum(defect) * (1.0 / CELLS)
     for s in sums:
         inner = inner - s
@@ -287,7 +281,7 @@
             out_ref[:, t * LANES : (t + 1) * LANES] = half
 
 
-def call(kernel, out_shape, name, *args, specs=None, scratch=()):
+def call(kernel, out_shape, *args, specs=None, scratch=()):
     many = isinstance(out_shape, (list, tuple))
     return pl.pallas_call(
         kernel,
@@ -296,7 +290,6 @@
         out_specs=[VMEM] * len(out_shape) if many else VMEM,
         scratch_shapes=scratch,
         compiler_params=pltpu.CompilerParams(vmem_limit_bytes=GRANT),
-        name=name,
     )(*args)
 
 
@@ -309,7 +302,6 @@
     whole = call(
         pack_kernel,
         f32(RANGE // 2, PACKED),
-        "pack",
         *[
             pltpu.with_memory_space_constraint(array, pltpu.HBM)
             for array in (pressure, source_term, coefficient, new_slot, face_links)
@@ -324,19 +316,17 @@
     u, f, c, links, faces = call(
         reorder_kernel,
         [field, field, field, jax.ShapeDtypeStruct((RANGE, LANES), jnp.int32), packed],
-        "reorder",
         gather(whole, cores),
     )
     met = gather(meet(faces), cores)
-    u, faces = call(sweep_kernel, [field, packed], "sweep", u, f, c, links, faces, met)
+    u, faces = call(sweep_kernel, [field, packed], u, f, c, links, faces, met)
     met = gather(meet(faces), cores)
-    u, faces, coarse = call(
-        smooth_kernel, [field, packed, f32(GROUP, RANGE, LANES)], "smooth", u, f, c, links, faces, met
-    )
+    u, faces = call(sweep_kernel, [field, packed], u, f, c, links, faces, met)
     met = meet(faces)
+    coarse = call(coarse_kernel, pltpu.VMEM((GROUP, RANGE, LANES), jnp.float32), u, f, c, links, faces)
     coarse = lax.all_to_all(coarse, "d", 0, 0, axis_index_groups=groups16, tiled=True)
-    joined = call(join_kernel, f32(RANGE, (2 * FACES + GROUP) * LANES), "join", met, coarse)
-    return call(final_kernel, f32(RANGE // 2, CELLS), "final", u, f, c, links, faces, gather(joined, cores))
+    joined = call(join_kernel, f32(RANGE, (2 * FACES + GROUP) * LANES), met, coarse)
+    return call(final_kernel, f32(RANGE // 2, CELLS), u, f, c, links, faces, gather(joined, cores))
 
 
 def solution(mesh):

time: 55.1 us -> 55.2 us (level)
    pallas_call x6 -> x7, Pallas kernels: 4.36 us -> 4.42 us  [call(): pl.pallas_call(kernel, out_shape=out_shape, in_specs=specs or [VMEM] * le...]
where the time goes in v4:
time: 55.2 us; the launch traced here: 54.9 us
  starting transfers between devices  30.7 us (56%)
  waiting for transfers between devices  11.6 us (21%)
  blocking collectives  8.09 us (15%)
  Pallas kernels  4.42 us (8%)
    all_to_all x1, starting transfers between devices, on_device(): lax.all_to_all(coarse, 'd', 0, 0, axis_index_groups=groups16, tiled=True)  19.8 us
    ppermute x3, waiting for transfers between devices, on_device(): meet = lambda array: lax.ppermute(array, 'd', exchange)  11.5 us
    ppermute x3, starting transfers between devices, on_device(): meet = lambda array: lax.ppermute(array, 'd', exchange)  11 us
    all_gather x4, blocking collectives, on_device(): lax.all_gather(array, 'd', axis=0, axis_index_groups=members)  8.09 us
    pallas_call x7, Pallas kernels, call(): pl.pallas_call(kernel, out_shape=out_shape, in_specs=specs or [VMEM] * le...  4.42 us
  transfers between devices with their start and end apart: 4, of which 3 were waited for; matrix products, arithmetic and copies ran while one was open for 0% of the time, Pallas kernels for 0%

profile of v4, /device:TPU:9, one launch (start us, length us, event | category | flops | bytes accessed | tf_op | source)
XLA Modules:
  0.0 54.9 jit_solution(7137325706417080031)
XLA Ops:
  0.0 1.0 %shard_map.55 = f32[4,12416]{1,0:T(4,128)S(1)} custom-call(f32[4,4096]{1,0:T(4,128)} %p_ref.1, f32[4,4096]{1,0:T(4,128)} %f_ref.1, f32[4,4096]{1,0:T(4,128)} %c_ref.1, s32[4]{0:T(128)} %slot_ref.1, s32[4,6]{1,0:T(4,128)} %links_ref.1), custom_call_target="tpu_custom_call" | custom-call | tf_op jit(solution)/shard_map/pallas_call | solution.py:286
  1.0 2.4 %all-gather.4.packed_ref = f32[2,4,12416]{2,1,0:T(4,128)S(1)} all-gather(f32[1,4,12416]{2,1,0:T(4,128)S(1)} %bitcast.5), channel_id=2, replica_groups={{0,1},{2,3},{4,5},{6,7},{8,9},{10,11},{12,13},{14,15},{16,17},{18,19},{..., dimensions={0}, use_global_device_ids=true | all-gather | bytes 595968 | tf_op jit(solution)/shard_map/all_gather | solution.py:299
  3.4 0.3 shard_map.56
  3.7 4.5 %collective-permute-start = (f32[8,1536]{1,0:T(8,128)S(1)}, f32[8,1536]{1,0:T(8,128)S(1)}, u32[]{:S(2)}, u32[]{:S(2)}) collective-permute-start(f32[8,1536]{1,0:T(8,128)S(1)} %get-tuple-element.18.faces_ref), channel_id=1, source_target_pairs={{0,3},{3,0},{2,5},{5,2},{4,7},{7,4},{6,9},{9,6},{8,11},{11,8},{10,... | collective-permute-start | bytes 147464 | tf_op jit(solution)/shard_map/ppermute | solution.py:298
  8.2 3.0 %collective-permute-done = f32[8,1536]{1,0:T(8,128)S(1)} collective-permute-done((f32[8,1536]{1,0:T(8,128)S(1)}, f32[8,1536]{1,0:T(8,128)S(1)}, u32[]{:S(2)}, u32[]{:S(2)}) %collective-permute-start) | collective-permute-done | bytes 49184 | tf_op jit(solution)/shard_map/ppermute | solution.py:298
  11.2 1.9 %all-gather.1 = f32[16,1536]{1,0:T(8,128)S(1)} all-gather(f32[8,1536]{1,0:T(8,128)S(1)} %collective-permute-done), channel_id=3, replica_groups={{0,1},{2,3},{4,5},{6,7},{8,9},{10,11},{12,13},{14,15},{16,17},{18,19},{..., dimensions={0}, use_global_device_ids=true | all-gather | bytes 147456 | tf_op jit(solution)/shard_map/all_gather | solution.py:299
  13.1 0.4 shard_map.57
  13.5 4.5 %collective-permute-start.1 = (f32[8,1536]{1,0:T(8,128)S(1)}, f32[8,1536]{1,0:T(8,128)S(1)}, u32[]{:S(2)}, u32[]{:S(2)}) collective-permute-start(f32[8,1536]{1,0:T(8,128)S(1)} %get-tuple-element.20.faces_ref), channel_id=1, source_target_pairs={{0,3},{3,0},{2,5},{5,2},{4,7},{7,4},{6,9},{9,6},{8,11},{11,8},{10,... | collective-permute-start | bytes 147464 | tf_op jit(solution)/shard_map/ppermute | solution.py:298
  18.1 3.0 %collective-permute-done.1 = f32[8,1536]{1,0:T(8,128)S(1)} collective-permute-done((f32[8,1536]{1,0:T(8,128)S(1)}, f32[8,1536]{1,0:T(8,128)S(1)}, u32[]{:S(2)}, u32[]{:S(2)}) %collective-permute-start.1) | collective-permute-done | bytes 49184 | tf_op jit(solution)/shard_map/ppermute | solution.py:298
  21.1 1.9 %all-gather.2 = f32[16,1536]{1,0:T(8,128)S(1)} all-gather(f32[8,1536]{1,0:T(8,128)S(1)} %collective-permute-done.1), channel_id=4, replica_groups={{0,1},{2,3},{4,5},{6,7},{8,9},{10,11},{12,13},{14,15},{16,17},{18,19},{..., dimensions={0}, use_global_device_ids=true | all-gather | bytes 147456 | tf_op jit(solution)/shard_map/all_gather | solution.py:299
  22.9 0.4 shard_map.58
  23.4 0.8 %shard_map.59 = f32[16,8,128]{2,1,0:T(8,128)} custom-call(f32[32,8,128]{2,1,0:T(8,128)S(1)} %get-tuple-element.21.u_ref, f32[32,8,128]{2,1,0:T(8,128)S(1)} %get-tuple-element.15.f_ref, f32[32,8,128]{2,1,0:T(8,128)S(1)} %get-tuple-element.16.c_ref, s32[8,128]{1,0:T(8,128)S(1)} %get-tuple-element.17.links_ref, f32[8,1536]{1,0:T(8,128)S(1)} %get-tuple-element.22.faces_ref), custom_call_target="tpu_custom_call" | custom-call | tf_op jit(solution)/shard_map/pallas_call | solution.py:286
  24.2 19.8 %all-to-all-start = ((f32[16,8,128]{2,1,0:T(8,128)}), f32[16,8,128]{2,1,0:T(8,128)S(1)}, u32[]{:S(2)}, u32[]{:S(2)}) async-start(f32[16,8,128]{2,1,0:T(8,128)} %shard_map.59), calls=%async_computation | async-start | bytes 131072 | tf_op jit(solution)/shard_map/all_to_all | solution.py:327
  43.9 1.9 %collective-permute-start.2 = (f32[8,1536]{1,0:T(8,128)S(1)}, f32[8,1536]{1,0:T(8,128)S(1)}, u32[]{:S(2)}, u32[]{:S(2)}) collective-permute-start(f32[8,1536]{1,0:T(8,128)S(1)} %get-tuple-element.22.faces_ref), channel_id=1, source_target_pairs={{0,3},{3,0},{2,5},{5,2},{4,7},{7,4},{6,9},{9,6},{8,11},{11,8},{10,... | collective-permute-start | bytes 147464 | tf_op jit(solution)/shard_map/ppermute | solution.py:298
  45.8 5.6 %collective-permute-done.2.met_ref = f32[8,1536]{1,0:T(8,128)S(1)} collective-permute-done((f32[8,1536]{1,0:T(8,128)S(1)}, f32[8,1536]{1,0:T(8,128)S(1)}, u32[]{:S(2)}, u32[]{:S(2)}) %collective-permute-start.2) | collective-permute-done | bytes 49184 | tf_op jit(solution)/shard_map/ppermute | solution.py:298
  51.4 0.0 all-to-all-done.coarse_ref
  51.4 2.0 %all-gather.3 = f32[16,3584]{1,0:T(8,128)S(1)} all-gather(f32[8,3584]{1,0:T(8,128)S(1)} %shard_map.60), channel_id=5, replica_groups={{0,1},{2,3},{4,5},{6,7},{8,9},{10,11},{12,13},{14,15},{16,17},{18,19},{..., dimensions={0}, use_global_device_ids=true | all-gather | bytes 344064 | tf_op jit(solution)/shard_map/all_gather | solution.py:299
  53.4 1.4 %shard_map.61 = f32[4,4096]{1,0:T(4,128)} custom-call(f32[32,8,128]{2,1,0:T(8,128)S(1)} %get-tuple-element.21.u_ref, f32[32,8,128]{2,1,0:T(8,128)S(1)} %get-tuple-element.15.f_ref, f32[32,8,128]{2,1,0:T(8,128)S(1)} %get-tuple-element.16.c_ref, s32[8,128]{1,0:T(8,128)S(1)} %get-tuple-element.17.links_ref, f32[8,1536]{1,0:T(8,128)S(1)} %get-tuple-element.22.faces_ref, ...), custom_call_target="tpu_custom_call" | custom-call | tf_op jit(solution)/shard_map/pallas_call | solution.py:286
  (1 shorter events, 0.0 us)
Async XLA Ops:
  3.7 7.5 %collective-permute-start = (f32[8,1536]{1,0:T(8,128)S(1)}, f32[8,1536]{1,0:T(8,128)S(1)}, u32[]{:S(2)}, u32[]{:S(2)}) collective-permute-start(f32[8,1536]{1,0:T(8,128)S(1)} %get-tuple-element.18.faces_ref), channel_id=1, source_target_pairs={{0,3},{3,0},{2,5},{5,2},{4,7},{7,4},{6,9},{9,6},{8,11},{11,8},{10,... | collective-permute-start | bytes 147464 | tf_op jit(solution)/shard_map/ppermute | solution.py:298
  13.5 7.5 %collective-permute-start.1 = (f32[8,1536]{1,0:T(8,128)S(1)}, f32[8,1536]{1,0:T(8,128)S(1)}, u32[]{:S(2)}, u32[]{:S(2)}) collective-permute-start(f32[8,1536]{1,0:T(8,128)S(1)} %get-tuple-element.20.faces_ref), channel_id=1, source_target_pairs={{0,3},{3,0},{2,5},{5,2},{4,7},{7,4},{6,9},{9,6},{8,11},{11,8},{10,... | collective-permute-start | bytes 147464 | tf_op jit(solution)/shard_map/ppermute | solution.py:298
  24.2 27.3 %all-to-all-start = ((f32[16,8,128]{2,1,0:T(8,128)}), f32[16,8,128]{2,1,0:T(8,128)S(1)}, u32[]{:S(2)}, u32[]{:S(2)}) async-start(f32[16,8,128]{2,1,0:T(8,128)} %shard_map.59), calls=%async_computation | async-start | bytes 131072 | tf_op jit(solution)/shard_map/all_to_all | solution.py:327
  43.9 7.5 %collective-permute-start.2 = (f32[8,1536]{1,0:T(8,128)S(1)}, f32[8,1536]{1,0:T(8,128)S(1)}, u32[]{:S(2)}, u32[]{:S(2)}) collective-permute-start(f32[8,1536]{1,0:T(8,128)S(1)} %get-tuple-element.22.faces_ref), channel_id=1, source_target_pairs={{0,3},{3,0},{2,5},{5,2},{4,7},{7,4},{6,9},{9,6},{8,11},{11,8},{10,... | collective-permute-start | bytes 147464 | tf_op jit(solution)/shard_map/ppermute | solution.py:298

commit v5 on v4

--- a/solution.py
+++ b/solution.py
@@ -76,11 +76,6 @@
 
 def load_face(ref, f, h, *lead):
     return ref[(*lead, slice(None), slice((2 * f + h) * LANES, (2 * f + h + 1) * LANES))]
-
-
-def load_coarse(ref, core, member):
-    start = (2 * FACES + member) * LANES
-    return ref[core, :, start : start + LANES]
 
 
 def pick_rows(tile, rows):
@@ -228,25 +223,27 @@
         coarse_out[i] = tile
 
 
-def join_kernel(met_ref, coarse_ref, out_ref):
+def turn_kernel(coarse_ref, out_ref):
+    values = jnp.concatenate([coarse_ref[i] for i in range(GROUP)], axis=0).T
+    out_ref[:, :LANES] = values[:RANGE]
+    out_ref[:, LANES:] = values[RANGE : 2 * RANGE]
+
+
+def join_kernel(met_ref, turned_ref, out_ref):
     width = FACES * 2 * LANES
     out_ref[:, :width] = met_ref[...]
-    for i in range(GROUP):
-        out_ref[:, width + i * LANES : width + (i + 1) * LANES] = coarse_ref[i]
+    out_ref[:, width:] = turned_ref[...]
 
 
 def final_kernel(u_ref, f_ref, c_ref, links_ref, faces_ref, met_ref, out_ref):
     core, curve = lax.axis_index("d") % 2, lax.axis_index("d") // 2
     row = sublanes()
-    nearest = []
-    for i in range(GROUP):
-        ahead = i - curve % GROUP
-        aligned = jnp.logical_and(ahead >= -GROUP // 2, ahead < GROUP // 2)
-        first = load_coarse(met_ref, 0, i)
-        second = load_coarse(met_ref, 1, (i + GROUP // 2) % GROUP)
-        nearest.append(jnp.where(aligned, first, second))
-    values = jnp.concatenate(nearest, axis=0).T
-    sums, names = values[:RANGE], values[RANGE : 2 * RANGE]
+    ahead = lanes() // RANGE - curve % GROUP
+    aligned = jnp.logical_and(ahead >= -GROUP // 2, ahead < GROUP // 2)
+    sums, names = [
+        jnp.where(aligned, load_face(met_ref, FACES, h, 0), roll(load_face(met_ref, FACES, h, 1), LANES // 2))
+        for h in range(2)
+    ]
     valid = jnp.logical_and(names >= 0.0, row < FACES)
     at = names.astype(jnp.int32) & (LANES - 1)
 
@@ -325,7 +322,8 @@
     met = meet(faces)
     coarse = call(coarse_kernel, pltpu.VMEM((GROUP, RANGE, LANES), jnp.float32), u, f, c, links, faces)
     coarse = lax.all_to_all(coarse, "d", 0, 0, axis_index_groups=groups16, tiled=True)
-    joined = call(join_kernel, f32(RANGE, (2 * FACES + GROUP) * LANES), met, coarse)
+    turned = call(turn_kernel, f32(RANGE, 2 * LANES), coarse)
+    joined = call(join_kernel, f32(RANGE, (FACES + 1) * 2 * LANES), met, turned)
     return call(final_kernel, f32(RANGE // 2, CELLS), u, f, c, links, faces, gather(joined, cores))
 
 

time: 55.2 us -> 55.1 us (level)
    ppermute x3, waiting for transfers between devices: 11.5 us -> 9.24 us  [on_device(): meet = lambda array: lax.ppermute(array, 'd', exchange)]
    all_to_all x1, waiting for transfers between devices: 0.01 us -> 2.26 us  [on_device(): lax.all_to_all(coarse, 'd', 0, 0, axis_index_groups=groups16, tiled=True)]
    pallas_call x7 -> x8, Pallas kernels: 4.42 us -> 4.44 us  [call(): pl.pallas_call(kernel, out_shape=out_shape, in_specs=specs or [VMEM] * le...]
  transfers between devices with their start and end apart: 4 -> 4, of which waited for: 3 -> 4; matrix products, arithmetic and copies ran while one was open for 0% -> 0% of each run, Pallas kernels for 0% -> 0%
where the time goes in v5:
time: 55.1 us; the launch traced here: 54.7 us
  starting transfers between devices  30.7 us (56%)
  waiting for transfers between devices  11.5 us (21%)
  blocking collectives  8 us (15%)
  Pallas kernels  4.44 us (8%)
    all_to_all x1, starting transfers between devices, on_device(): lax.all_to_all(coarse, 'd', 0, 0, axis_index_groups=groups16, tiled=True)  19.8 us
    ppermute x3, starting transfers between devices, on_device(): meet = lambda array: lax.ppermute(array, 'd', exchange)  11 us
    ppermute x3, waiting for transfers between devices, on_device(): meet = lambda array: lax.ppermute(array, 'd', exchange)  9.24 us
    all_gather x4, blocking collectives, on_device(): lax.all_gather(array, 'd', axis=0, axis_index_groups=members)  8 us
    pallas_call x8, Pallas kernels, call(): pl.pallas_call(kernel, out_shape=out_shape, in_specs=specs or [VMEM] * le...  4.44 us
    all_to_all x1, waiting for transfers between devices, on_device(): lax.all_to_all(coarse, 'd', 0, 0, axis_index_groups=groups16, tiled=True)  2.26 us
  transfers between devices with their start and end apart: 4, of which 4 were waited for; matrix products, arithmetic and copies ran while one was open for 0% of the time, Pallas kernels for 0%

profile of v5, /device:TPU:9, one launch (start us, length us, event | category | flops | bytes accessed | tf_op | source)
XLA Modules:
  0.0 54.7 jit_solution(1036695382839801787)
XLA Ops:
  0.0 1.0 %shard_map.55 = f32[4,12416]{1,0:T(4,128)S(1)} custom-call(f32[4,4096]{1,0:T(4,128)} %p_ref.1, f32[4,4096]{1,0:T(4,128)} %f_ref.1, f32[4,4096]{1,0:T(4,128)} %c_ref.1, s32[4]{0:T(128)} %slot_ref.1, s32[4,6]{1,0:T(4,128)} %links_ref.1), custom_call_target="tpu_custom_call" | custom-call | tf_op jit(solution)/shard_map/pallas_call | solution.py:283
  1.0 2.4 %all-gather.4.packed_ref = f32[2,4,12416]{2,1,0:T(4,128)S(1)} all-gather(f32[1,4,12416]{2,1,0:T(4,128)S(1)} %bitcast.4), channel_id=2, replica_groups={{0,1},{2,3},{4,5},{6,7},{8,9},{10,11},{12,13},{14,15},{16,17},{18,19},{..., dimensions={0}, use_global_device_ids=true | all-gather | bytes 595968 | tf_op jit(solution)/shard_map/all_gather | solution.py:296
  3.4 0.3 shard_map.56
  3.7 4.5 %collective-permute-start = (f32[8,1536]{1,0:T(8,128)S(1)}, f32[8,1536]{1,0:T(8,128)S(1)}, u32[]{:S(2)}, u32[]{:S(2)}) collective-permute-start(f32[8,1536]{1,0:T(8,128)S(1)} %get-tuple-element.18.faces_ref), channel_id=1, source_target_pairs={{0,3},{3,0},{2,5},{5,2},{4,7},{7,4},{6,9},{9,6},{8,11},{11,8},{10,... | collective-permute-start | bytes 147464 | tf_op jit(solution)/shard_map/ppermute | solution.py:295
  8.2 3.0 %collective-permute-done = f32[8,1536]{1,0:T(8,128)S(1)} collective-permute-done((f32[8,1536]{1,0:T(8,128)S(1)}, f32[8,1536]{1,0:T(8,128)S(1)}, u32[]{:S(2)}, u32[]{:S(2)}) %collective-permute-start) | collective-permute-done | bytes 49184 | tf_op jit(solution)/shard_map/ppermute | solution.py:295
  11.2 1.9 %all-gather.1 = f32[16,1536]{1,0:T(8,128)S(1)} all-gather(f32[8,1536]{1,0:T(8,128)S(1)} %collective-permute-done), channel_id=3, replica_groups={{0,1},{2,3},{4,5},{6,7},{8,9},{10,11},{12,13},{14,15},{16,17},{18,19},{..., dimensions={0}, use_global_device_ids=true | all-gather | bytes 147456 | tf_op jit(solution)/shard_map/all_gather | solution.py:296
  13.1 0.4 shard_map.57
  13.5 4.5 %collective-permute-start.1 = (f32[8,1536]{1,0:T(8,128)S(1)}, f32[8,1536]{1,0:T(8,128)S(1)}, u32[]{:S(2)}, u32[]{:S(2)}) collective-permute-start(f32[8,1536]{1,0:T(8,128)S(1)} %get-tuple-element.20.faces_ref), channel_id=1, source_target_pairs={{0,3},{3,0},{2,5},{5,2},{4,7},{7,4},{6,9},{9,6},{8,11},{11,8},{10,... | collective-permute-start | bytes 147464 | tf_op jit(solution)/shard_map/ppermute | solution.py:295
  18.1 3.0 %collective-permute-done.1 = f32[8,1536]{1,0:T(8,128)S(1)} collective-permute-done((f32[8,1536]{1,0:T(8,128)S(1)}, f32[8,1536]{1,0:T(8,128)S(1)}, u32[]{:S(2)}, u32[]{:S(2)}) %collective-permute-start.1) | collective-permute-done | bytes 49184 | tf_op jit(solution)/shard_map/ppermute | solution.py:295
  21.1 1.9 %all-gather.2 = f32[16,1536]{1,0:T(8,128)S(1)} all-gather(f32[8,1536]{1,0:T(8,128)S(1)} %collective-permute-done.1), channel_id=4, replica_groups={{0,1},{2,3},{4,5},{6,7},{8,9},{10,11},{12,13},{14,15},{16,17},{18,19},{..., dimensions={0}, use_global_device_ids=true | all-gather | bytes 147456 | tf_op jit(solution)/shard_map/all_gather | solution.py:296
  22.9 0.4 shard_map.58
  23.4 0.8 %shard_map.59 = f32[16,8,128]{2,1,0:T(8,128)} custom-call(f32[32,8,128]{2,1,0:T(8,128)S(1)} %get-tuple-element.21.u_ref, f32[32,8,128]{2,1,0:T(8,128)S(1)} %get-tuple-element.15.f_ref, f32[32,8,128]{2,1,0:T(8,128)S(1)} %get-tuple-element.16.c_ref, s32[8,128]{1,0:T(8,128)S(1)} %get-tuple-element.17.links_ref, f32[8,1536]{1,0:T(8,128)S(1)} %get-tuple-element.22.faces_ref), custom_call_target="tpu_custom_call" | custom-call | tf_op jit(solution)/shard_map/pallas_call | solution.py:283
  24.2 19.8 %all-to-all-start = ((f32[16,8,128]{2,1,0:T(8,128)}), f32[16,8,128]{2,1,0:T(8,128)S(1)}, u32[]{:S(2)}, u32[]{:S(2)}) async-start(f32[16,8,128]{2,1,0:T(8,128)} %shard_map.59), calls=%async_computation | async-start | bytes 131072 | tf_op jit(solution)/shard_map/all_to_all | solution.py:324
  43.9 1.9 %collective-permute-start.2 = (f32[8,1536]{1,0:T(8,128)S(1)}, f32[8,1536]{1,0:T(8,128)S(1)}, u32[]{:S(2)}, u32[]{:S(2)}) collective-permute-start(f32[8,1536]{1,0:T(8,128)S(1)} %get-tuple-element.22.faces_ref), channel_id=1, source_target_pairs={{0,3},{3,0},{2,5},{5,2},{4,7},{7,4},{6,9},{9,6},{8,11},{11,8},{10,... | collective-permute-start | bytes 147464 | tf_op jit(solution)/shard_map/ppermute | solution.py:295
  45.8 2.3 %all-to-all-done.coarse_ref = f32[16,8,128]{2,1,0:T(8,128)S(1)} async-done(((f32[16,8,128]{2,1,0:T(8,128)}), f32[16,8,128]{2,1,0:T(8,128)S(1)}, u32[]{:S(2)}, u32[]{:S(2)}) %all-to-all-start) | async-done | bytes 65568 | tf_op jit(solution)/shard_map/all_to_all | solution.py:324
  48.2 3.3 %collective-permute-done.2.met_ref = f32[8,1536]{1,0:T(8,128)S(1)} collective-permute-done((f32[8,1536]{1,0:T(8,128)S(1)}, f32[8,1536]{1,0:T(8,128)S(1)}, u32[]{:S(2)}, u32[]{:S(2)}) %collective-permute-start.2) | collective-permute-done | bytes 49184 | tf_op jit(solution)/shard_map/ppermute | solution.py:295
  51.4 1.9 %all-gather.3 = f32[16,1792]{1,0:T(8,128)S(1)} all-gather(f32[8,1792]{1,0:T(8,128)S(1)} %shard_map.61), channel_id=5, replica_groups={{0,1},{2,3},{4,5},{6,7},{8,9},{10,11},{12,13},{14,15},{16,17},{18,19},{..., dimensions={0}, use_global_device_ids=true | all-gather | bytes 172032 | tf_op jit(solution)/shard_map/all_gather | solution.py:296
  53.3 1.4 %shard_map.62 = f32[4,4096]{1,0:T(4,128)} custom-call(f32[32,8,128]{2,1,0:T(8,128)S(1)} %get-tuple-element.21.u_ref, f32[32,8,128]{2,1,0:T(8,128)S(1)} %get-tuple-element.15.f_ref, f32[32,8,128]{2,1,0:T(8,128)S(1)} %get-tuple-element.16.c_ref, s32[8,128]{1,0:T(8,128)S(1)} %get-tuple-element.17.links_ref, f32[8,1536]{1,0:T(8,128)S(1)} %get-tuple-element.22.faces_ref, ...), custom_call_target="tpu_custom_call" | custom-call | tf_op jit(solution)/shard_map/pallas_call | solution.py:283
  (2 shorter events, 0.1 us)
Async XLA Ops:
  3.7 7.5 %collective-permute-start = (f32[8,1536]{1,0:T(8,128)S(1)}, f32[8,1536]{1,0:T(8,128)S(1)}, u32[]{:S(2)}, u32[]{:S(2)}) collective-permute-start(f32[8,1536]{1,0:T(8,128)S(1)} %get-tuple-element.18.faces_ref), channel_id=1, source_target_pairs={{0,3},{3,0},{2,5},{5,2},{4,7},{7,4},{6,9},{9,6},{8,11},{11,8},{10,... | collective-permute-start | bytes 147464 | tf_op jit(solution)/shard_map/ppermute | solution.py:295
  13.5 7.5 %collective-permute-start.1 = (f32[8,1536]{1,0:T(8,128)S(1)}, f32[8,1536]{1,0:T(8,128)S(1)}, u32[]{:S(2)}, u32[]{:S(2)}) collective-permute-start(f32[8,1536]{1,0:T(8,128)S(1)} %get-tuple-element.20.faces_ref), channel_id=1, source_target_pairs={{0,3},{3,0},{2,5},{5,2},{4,7},{7,4},{6,9},{9,6},{8,11},{11,8},{10,... | collective-permute-start | bytes 147464 | tf_op jit(solution)/shard_map/ppermute | solution.py:295
  24.2 23.9 %all-to-all-start = ((f32[16,8,128]{2,1,0:T(8,128)}), f32[16,8,128]{2,1,0:T(8,128)S(1)}, u32[]{:S(2)}, u32[]{:S(2)}) async-start(f32[16,8,128]{2,1,0:T(8,128)} %shard_map.59), calls=%async_computation | async-start | bytes 131072 | tf_op jit(solution)/shard_map/all_to_all | solution.py:324
  43.9 7.5 %collective-permute-start.2 = (f32[8,1536]{1,0:T(8,128)S(1)}, f32[8,1536]{1,0:T(8,128)S(1)}, u32[]{:S(2)}, u32[]{:S(2)}) collective-permute-start(f32[8,1536]{1,0:T(8,128)S(1)} %get-tuple-element.22.faces_ref), channel_id=1, source_target_pairs={{0,3},{3,0},{2,5},{5,2},{4,7},{7,4},{6,9},{9,6},{8,11},{11,8},{10,... | collective-permute-start | bytes 147464 | tf_op jit(solution)/shard_map/ppermute | solution.py:295

commit v6 on v5

--- a/solution.py
+++ b/solution.py
@@ -7,7 +7,6 @@
 from jax.experimental.pallas import tpu as pltpu
 from jax.sharding import Mesh, PartitionSpec as P
 
-
 COARSE_SWEEPS = 4
 RELAXATION = 0.8
 
@@ -17,7 +16,8 @@
 CELLS = 4096
 FACES = 6
 FLIPPED = (1, 0, 3, 2, 5, 4)
-GROUP = 16
+ROW = 4
+SLOTS = 16
 PACKED = 3 * CELLS + LANES
 
 VMEM = pl.BlockSpec(memory_space=pltpu.VMEM)
@@ -219,29 +219,44 @@
         tile = jnp.where(lane == RANGE + d, links[:, d : d + 1].astype(jnp.float32), tile)
     tile = jnp.where(lane == FACES, inner, tile)
     tile = jnp.where(lane == FACES + 1, diag, tile)
-    for i in range(GROUP):
-        coarse_out[i] = tile
-
-
-def turn_kernel(coarse_ref, out_ref):
-    values = jnp.concatenate([coarse_ref[i] for i in range(GROUP)], axis=0).T
+    coarse_out[...] = tile
+
+
+def row_kernel(row_ref, met_ref, out_ref):
+    core, curve = lax.axis_index("d") % 2, lax.axis_index("d") // 2
+    met = jnp.where(core == 0, curve + 1, curve + SLOTS - 1) % SLOTS
+    lane = lanes()
+    edge = jnp.zeros((RANGE, LANES), jnp.float32)
+    for d, column in enumerate(face_sums(lambda f, h: load_face(met_ref, f, h))):
+        edge = jnp.where(lane == d, column, edge)
+    tiles = []
+    for slot in range(SLOTS):
+        place = slot % ROW
+        own = slot // ROW == curve // ROW % (SLOTS // ROW)
+        other = jnp.where(slot == met, edge, 0.0)
+        tiles.append(jnp.where(own, row_ref[place // 2, place % 2], other))
+    values = jnp.concatenate(tiles, axis=0).T
     out_ref[:, :LANES] = values[:RANGE]
     out_ref[:, LANES:] = values[RANGE : 2 * RANGE]
 
 
-def join_kernel(met_ref, turned_ref, out_ref):
+def join_kernel(met_ref, far_ref, out_ref):
     width = FACES * 2 * LANES
     out_ref[:, :width] = met_ref[...]
-    out_ref[:, width:] = turned_ref[...]
-
-
-def final_kernel(u_ref, f_ref, c_ref, links_ref, faces_ref, met_ref, out_ref):
+    out_ref[:, width:] = far_ref[...]
+
+
+def final_kernel(u_ref, f_ref, c_ref, links_ref, faces_ref, row_ref, met_ref, out_ref):
     core, curve = lax.axis_index("d") % 2, lax.axis_index("d") // 2
     row = sublanes()
-    ahead = lanes() // RANGE - curve % GROUP
-    aligned = jnp.logical_and(ahead >= -GROUP // 2, ahead < GROUP // 2)
+    part = (lanes() // (ROW * RANGE) + SLOTS // ROW - curve // ROW % (SLOTS // ROW)) % (SLOTS // ROW)
+    first = jnp.logical_or(part == 3, jnp.logical_and(part == 2, curve % ROW == 0))
     sums, names = [
-        jnp.where(aligned, load_face(met_ref, FACES, h, 0), roll(load_face(met_ref, FACES, h, 1), LANES // 2))
+        jnp.where(
+            part == 0,
+            row_ref[:, h * LANES : (h + 1) * LANES],
+            jnp.where(first, load_face(met_ref, FACES, h, 0), load_face(met_ref, FACES, h, 1)),
+        )
         for h in range(2)
     ]
     valid = jnp.logical_and(names >= 0.0, row < FACES)
@@ -262,7 +277,7 @@
         near = total(named(error)) if step else 0.0
         error = error + RELAXATION * (residual - diag * error + near) / diag
     near = named(error)
-    own = lanes() == curve % GROUP * RANGE + row
+    own = lanes() == curve % SLOTS * RANGE + row
     lift = lane_sum(jnp.where(own, error, 0.0))
     ghosts, _ = ghost_faces(links_ref[...], range_base(), *window(met_ref, faces_ref))
     for d in range(FACES):
@@ -291,9 +306,9 @@
 
 
 def on_device(groups, pressure, source_term, coefficient, new_slot, face_links):
-    cores, groups16, exchange = groups
+    cores, along, across, exchange, far = groups
+    gather = lambda array, members: lax.all_gather(array, "d", axis=0, axis_index_groups=members)
     meet = lambda array: lax.ppermute(array, "d", exchange)
-    gather = lambda array, members: lax.all_gather(array, "d", axis=0, axis_index_groups=members)
     field = f32(CELLS // LANES, RANGE, LANES)
     packed = f32(RANGE, FACES * 2 * LANES)
     whole = call(
@@ -320,26 +335,30 @@
     met = gather(meet(faces), cores)
     u, faces = call(sweep_kernel, [field, packed], u, f, c, links, faces, met)
     met = meet(faces)
-    coarse = call(coarse_kernel, pltpu.VMEM((GROUP, RANGE, LANES), jnp.float32), u, f, c, links, faces)
-    coarse = lax.all_to_all(coarse, "d", 0, 0, axis_index_groups=groups16, tiled=True)
-    turned = call(turn_kernel, f32(RANGE, 2 * LANES), coarse)
-    joined = call(join_kernel, f32(RANGE, (FACES + 1) * 2 * LANES), met, turned)
-    return call(final_kernel, f32(RANGE // 2, CELLS), u, f, c, links, faces, gather(joined, cores))
+    coarse = call(coarse_kernel, f32(RANGE, LANES), u, f, c, links, faces)
+    coarse = gather(coarse, along)
+    coarse = gather(coarse, across)
+    row = call(row_kernel, f32(RANGE, 2 * LANES), coarse, met)
+    joined = call(join_kernel, f32(RANGE, (FACES + 1) * 2 * LANES), met, lax.ppermute(row, "d", far))
+    return call(final_kernel, f32(RANGE // 2, CELLS), u, f, c, links, faces, row, gather(joined, cores))
 
 
 def solution(mesh):
     devices = mesh.devices.reshape(-1)
     count = devices.size // 2
     cores = [[2 * i, 2 * i + 1] for i in range(count)]
-    groups16 = [
-        [2 * ((i + core * GROUP // 2 + k) % count) + core for k in range(GROUP)]
-        for i in range(0, count, GROUP)
-        for core in range(2)
+    firsts = [2 * i + core for i in range(0, count, ROW) for core in range(2)]
+    along = [[i + k, i + k + 2] for i in firsts for k in (0, 4)]
+    across = [[i + k, i + 6 - k] for i in firsts for k in (0, 2)]
+    far = [
+        pair
+        for i in range(count - ROW)
+        for pair in ((2 * i + 1, 2 * (i + ROW)), (2 * (i + ROW), 2 * i + 1))
     ]
     exchange = [pair for i in range(count - 1) for pair in ((2 * i, 2 * i + 3), (2 * i + 3, 2 * i))]
     split, line = P("d", None), P("d")
     return jax.shard_map(
-        functools.partial(on_device, (cores, groups16, exchange)),
+        functools.partial(on_device, (cores, along, across, exchange, far)),
         mesh=Mesh(devices, ("d",)),
         in_specs=(split, split, split, line, split),
         out_specs=split,

time: 55.1 us -> 55.2 us (level)
  the two profiles are of different devices: /device:TPU:9 before, /device:TPU:513 now
where the time goes in v6:
time: 55.2 us; the launch traced here: 54.9 us
  starting transfers between devices  28.2 us (51%)
  blocking collectives  15.6 us (28%)
  waiting for transfers between devices  7.2 us (13%)
  Pallas kernels  3.85 us (7%)
    ppermute x3, starting transfers between devices, on_device(): meet = lambda array: lax.ppermute(array, 'd', exchange)  26.3 us
    all_gather x6, blocking collectives, on_device(): lax.all_gather(array, 'd', axis=0, axis_index_groups=members)  15.6 us
    ppermute x3, waiting for transfers between devices, on_device(): meet = lambda array: lax.ppermute(array, 'd', exchange)  4.16 us
    pallas_call x8, Pallas kernels, call(): pl.pallas_call(kernel, out_shape=out_shape, in_specs=specs or [VMEM] * le...  3.85 us
    ppermute x1, waiting for transfers between devices, on_device(): lax.ppermute(row, 'd', far)  3.04 us
    ppermute x1, starting transfers between devices, on_device(): lax.ppermute(row, 'd', far)  1.93 us
  transfers between devices with their start and end apart: 4, of which 3 were waited for; matrix products, arithmetic and copies ran while one was open for 0% of the time, Pallas kernels for 0%

profile of v6, /device:TPU:513, one launch (start us, length us, event | category | flops | bytes accessed | tf_op | source)
XLA Modules:
  0.0 54.9 jit_solution(4233162931163808345)
XLA Ops:
  0.0 1.0 %shard_map.55 = f32[4,12416]{1,0:T(4,128)S(1)} custom-call(f32[4,4096]{1,0:T(4,128)} %p_ref.1, f32[4,4096]{1,0:T(4,128)} %f_ref.1, f32[4,4096]{1,0:T(4,128)} %c_ref.1, s32[4]{0:T(128)} %slot_ref.1, s32[4,6]{1,0:T(4,128)} %links_ref.1), custom_call_target="tpu_custom_call" | custom-call | tf_op jit(solution)/shard_map/pallas_call | solution.py:298
  1.0 2.4 %all-gather.6.packed_ref = f32[2,4,12416]{2,1,0:T(4,128)S(1)} all-gather(f32[1,4,12416]{2,1,0:T(4,128)S(1)} %bitcast.6), channel_id=2, replica_groups={{0,1},{2,3},{4,5},{6,7},{8,9},{10,11},{12,13},{14,15},{16,17},{18,19},{..., dimensions={0}, use_global_device_ids=true | all-gather | bytes 595968 | tf_op jit(solution)/shard_map/all_gather | solution.py:310
  3.4 0.3 shard_map.56
  3.7 8.8 %collective-permute-start = (f32[8,1536]{1,0:T(8,128)S(1)}, f32[8,1536]{1,0:T(8,128)S(1)}, u32[]{:S(2)}, u32[]{:S(2)}) collective-permute-start(f32[8,1536]{1,0:T(8,128)S(1)} %get-tuple-element.18.faces_ref), channel_id=1, source_target_pairs={{0,3},{3,0},{2,5},{5,2},{4,7},{7,4},{6,9},{9,6},{8,11},{11,8},{10,... | collective-permute-start | bytes 147464 | tf_op jit(solution)/shard_map/ppermute | solution.py:311
  12.5 2.1 %collective-permute-done = f32[8,1536]{1,0:T(8,128)S(1)} collective-permute-done((f32[8,1536]{1,0:T(8,128)S(1)}, f32[8,1536]{1,0:T(8,128)S(1)}, u32[]{:S(2)}, u32[]{:S(2)}) %collective-permute-start) | collective-permute-done | bytes 49184 | tf_op jit(solution)/shard_map/ppermute | solution.py:311
  14.5 1.9 %all-gather.1 = f32[16,1536]{1,0:T(8,128)S(1)} all-gather(f32[8,1536]{1,0:T(8,128)S(1)} %collective-permute-done), channel_id=3, replica_groups={{0,1},{2,3},{4,5},{6,7},{8,9},{10,11},{12,13},{14,15},{16,17},{18,19},{..., dimensions={0}, use_global_device_ids=true | all-gather | bytes 147456 | tf_op jit(solution)/shard_map/all_gather | solution.py:310
  16.4 0.4 shard_map.57
  16.9 8.8 %collective-permute-start.1 = (f32[8,1536]{1,0:T(8,128)S(1)}, f32[8,1536]{1,0:T(8,128)S(1)}, u32[]{:S(2)}, u32[]{:S(2)}) collective-permute-start(f32[8,1536]{1,0:T(8,128)S(1)} %get-tuple-element.20.faces_ref), channel_id=1, source_target_pairs={{0,3},{3,0},{2,5},{5,2},{4,7},{7,4},{6,9},{9,6},{8,11},{11,8},{10,... | collective-permute-start | bytes 147464 | tf_op jit(solution)/shard_map/ppermute | solution.py:311
  25.6 2.1 %collective-permute-done.1 = f32[8,1536]{1,0:T(8,128)S(1)} collective-permute-done((f32[8,1536]{1,0:T(8,128)S(1)}, f32[8,1536]{1,0:T(8,128)S(1)}, u32[]{:S(2)}, u32[]{:S(2)}) %collective-permute-start.1) | collective-permute-done | bytes 49184 | tf_op jit(solution)/shard_map/ppermute | solution.py:311
  27.7 1.9 %all-gather.2 = f32[16,1536]{1,0:T(8,128)S(1)} all-gather(f32[8,1536]{1,0:T(8,128)S(1)} %collective-permute-done.1), channel_id=4, replica_groups={{0,1},{2,3},{4,5},{6,7},{8,9},{10,11},{12,13},{14,15},{16,17},{18,19},{..., dimensions={0}, use_global_device_ids=true | all-gather | bytes 147456 | tf_op jit(solution)/shard_map/all_gather | solution.py:310
  29.6 0.4 shard_map.58
  30.0 8.8 %collective-permute-start.2 = (f32[8,1536]{1,0:T(8,128)S(1)}, f32[8,1536]{1,0:T(8,128)S(1)}, u32[]{:S(2)}, u32[]{:S(2)}) collective-permute-start(f32[8,1536]{1,0:T(8,128)S(1)} %get-tuple-element.22.faces_ref), channel_id=1, source_target_pairs={{0,3},{3,0},{2,5},{5,2},{4,7},{7,4},{6,9},{9,6},{8,11},{11,8},{10,... | collective-permute-start | bytes 147464 | tf_op jit(solution)/shard_map/ppermute | solution.py:311
  38.8 0.1 shard_map.59
  38.9 3.2 %all-gather.3 = f32[16,128]{1,0:T(8,128)S(1)} all-gather(f32[8,128]{1,0:T(8,128)S(1)} %shard_map.59), channel_id=5, replica_groups={{0,2},{4,6},{1,3},{5,7},{8,10},{12,14},{9,11},{13,15},{16,18},{20,22},{..., dimensions={0}, use_global_device_ids=true | all-gather | bytes 12288 | tf_op jit(solution)/shard_map/all_gather | solution.py:310
  42.1 4.4 %all-gather.4 = f32[4,8,128]{2,1,0:T(8,128)S(1)} all-gather(f32[2,8,128]{2,1,0:T(8,128)S(1)} %bitcast.11), channel_id=6, replica_groups={{0,6},{2,4},{1,7},{3,5},{8,14},{10,12},{9,15},{11,13},{16,22},{18,20},{..., dimensions={0}, use_global_device_ids=true | all-gather | bytes 24576 | tf_op jit(solution)/shard_map/all_gather | solution.py:310
  46.5 0.0 collective-permute-done.2.met_ref
  46.5 0.1 shard_map.60.row_ref
  46.7 1.9 %collective-permute-start.3 = (f32[8,256]{1,0:T(8,128)S(1)}, f32[8,256]{1,0:T(8,128)S(1)}, u32[]{:S(2)}, u32[]{:S(2)}) collective-permute-start(f32[8,256]{1,0:T(8,128)S(1)} %shard_map.60.row_ref), channel_id=1, source_target_pairs={{1,8},{8,1},{3,10},{10,3},{5,12},{12,5},{7,14},{14,7},{9,16},{16,9... | collective-permute-start | bytes 24584 | tf_op jit(solution)/shard_map/ppermute | solution.py:342
  48.6 3.0 %collective-permute-done.3.far_ref = f32[8,256]{1,0:T(8,128)S(1)} collective-permute-done((f32[8,256]{1,0:T(8,128)S(1)}, f32[8,256]{1,0:T(8,128)S(1)}, u32[]{:S(2)}, u32[]{:S(2)}) %collective-permute-start.3) | collective-permute-done | bytes 8224 | tf_op jit(solution)/shard_map/ppermute | solution.py:342
  51.7 1.9 %all-gather.5 = f32[16,1792]{1,0:T(8,128)S(1)} all-gather(f32[8,1792]{1,0:T(8,128)S(1)} %shard_map.61), channel_id=7, replica_groups={{0,1},{2,3},{4,5},{6,7},{8,9},{10,11},{12,13},{14,15},{16,17},{18,19},{..., dimensions={0}, use_global_device_ids=true | all-gather | bytes 172032 | tf_op jit(solution)/shard_map/all_gather | solution.py:310
  53.5 1.4 %shard_map.62 = f32[4,4096]{1,0:T(4,128)} custom-call(f32[32,8,128]{2,1,0:T(8,128)S(1)} %get-tuple-element.21.u_ref, f32[32,8,128]{2,1,0:T(8,128)S(1)} %get-tuple-element.15.f_ref, f32[32,8,128]{2,1,0:T(8,128)S(1)} %get-tuple-element.16.c_ref, s32[8,128]{1,0:T(8,128)S(1)} %get-tuple-element.17.links_ref, f32[8,1536]{1,0:T(8,128)S(1)} %get-tuple-element.22.faces_ref, ...), custom_call_target="tpu_custom_call" | custom-call | tf_op jit(solution)/shard_map/pallas_call | solution.py:298
  (1 shorter events, 0.0 us)
Async XLA Ops:
  3.7 10.8 %collective-permute-start = (f32[8,1536]{1,0:T(8,128)S(1)}, f32[8,1536]{1,0:T(8,128)S(1)}, u32[]{:S(2)}, u32[]{:S(2)}) collective-permute-start(f32[8,1536]{1,0:T(8,128)S(1)} %get-tuple-element.18.faces_ref), channel_id=1, source_target_pairs={{0,3},{3,0},{2,5},{5,2},{4,7},{7,4},{6,9},{9,6},{8,11},{11,8},{10,... | collective-permute-start | bytes 147464 | tf_op jit(solution)/shard_map/ppermute | solution.py:311
  16.9 10.8 %collective-permute-start.1 = (f32[8,1536]{1,0:T(8,128)S(1)}, f32[8,1536]{1,0:T(8,128)S(1)}, u32[]{:S(2)}, u32[]{:S(2)}) collective-permute-start(f32[8,1536]{1,0:T(8,128)S(1)} %get-tuple-element.20.faces_ref), channel_id=1, source_target_pairs={{0,3},{3,0},{2,5},{5,2},{4,7},{7,4},{6,9},{9,6},{8,11},{11,8},{10,... | collective-permute-start | bytes 147464 | tf_op jit(solution)/shard_map/ppermute | solution.py:311
  30.0 16.5 %collective-permute-start.2 = (f32[8,1536]{1,0:T(8,128)S(1)}, f32[8,1536]{1,0:T(8,128)S(1)}, u32[]{:S(2)}, u32[]{:S(2)}) collective-permute-start(f32[8,1536]{1,0:T(8,128)S(1)} %get-tuple-element.22.faces_ref), channel_id=1, source_target_pairs={{0,3},{3,0},{2,5},{5,2},{4,7},{7,4},{6,9},{9,6},{8,11},{11,8},{10,... | collective-permute-start | bytes 147464 | tf_op jit(solution)/shard_map/ppermute | solution.py:311
  46.7 5.0 %collective-permute-start.3 = (f32[8,256]{1,0:T(8,128)S(1)}, f32[8,256]{1,0:T(8,128)S(1)}, u32[]{:S(2)}, u32[]{:S(2)}) collective-permute-start(f32[8,256]{1,0:T(8,128)S(1)} %shard_map.60.row_ref), channel_id=1, source_target_pairs={{1,8},{8,1},{3,10},{10,3},{5,12},{12,5},{7,14},{14,7},{9,16},{16,9... | collective-permute-start | bytes 24584 | tf_op jit(solution)/shard_map/ppermute | solution.py:342

commit v7 on v6

--- a/solution.py
+++ b/solution.py
@@ -7,6 +7,7 @@
 from jax.experimental.pallas import tpu as pltpu
 from jax.sharding import Mesh, PartitionSpec as P
 
+PRE_SWEEPS = 2
 COARSE_SWEEPS = 4
 RELAXATION = 0.8
 
@@ -18,7 +19,7 @@
 FLIPPED = (1, 0, 3, 2, 5, 4)
 ROW = 4
 SLOTS = 16
-PACKED = 3 * CELLS + LANES
+PACKED = CELLS + LANES
 
 VMEM = pl.BlockSpec(memory_space=pltpu.VMEM)
 HBM = pl.BlockSpec(memory_space=pltpu.HBM)
@@ -137,15 +138,15 @@
     return lax.axis_index("d") // 2 * RANGE
 
 
-def pack_kernel(p_ref, f_ref, c_ref, slot_ref, links_ref, out_ref, slots, links, sems):
-    small = [pltpu.make_async_copy(slot_ref, slots, sems.at[3]), pltpu.make_async_copy(links_ref, links, sems.at[4])]
-    large = [
-        pltpu.make_async_copy(ref, out_ref.at[:, i * CELLS : (i + 1) * CELLS], sems.at[i])
-        for i, ref in enumerate((p_ref, f_ref, c_ref))
+def pack_kernel(p_ref, f_ref, c_ref, slot_ref, links_ref, p_out, rest_out, slots, links, sems):
+    targets = (p_out.at[:, :CELLS], rest_out.at[:, :CELLS], rest_out.at[:, CELLS:], slots, links)
+    copies = [
+        pltpu.make_async_copy(ref, target, sems.at[i])
+        for i, (ref, target) in enumerate(zip((p_ref, f_ref, c_ref, slot_ref, links_ref), targets))
     ]
-    for copy in small + large:
+    for copy in copies[3:] + copies[:3]:
         copy.start()
-    for copy in small:
+    for copy in copies[3:]:
         copy.wait()
     lane = lanes()[: RANGE // 2]
     row = sublanes()[: RANGE // 2]
@@ -154,27 +155,43 @@
         tile = jnp.where(lane == d, links[:, d : d + 1], tile)
     for i in range(RANGE // 2):
         tile = jnp.where(jnp.logical_and(lane == FACES, row == i), slots[i], tile)
-    out_ref[:, 3 * CELLS :] = tile.astype(jnp.float32)
-    for copy in large:
+    p_out[:, CELLS:] = tile.astype(jnp.float32)
+    for copy in copies[:3]:
         copy.wait()
 
 
-def reorder_kernel(packed_ref, p_out, f_out, c_out, links_out, faces_out):
-    def both(start):
-        span = slice(start, start + LANES)
-        return jnp.concatenate([packed_ref[0, :, span], packed_ref[1, :, span]], axis=0)
-
+def both(ref, start):
+    span = slice(start, start + LANES)
+    return jnp.concatenate([ref[0, :, span], ref[1, :, span]], axis=0)
+
+
+def reorder(ref, start, rows, target):
+    for t in range(CELLS // LANES):
+        target[t] = pick_rows(both(ref, start + t * LANES), rows)
+
+
+def reorder_kernel(packed_ref, p_out, links_out, rows_out, faces_out):
     lane, row = lanes(), sublanes()
-    names = both(3 * CELLS)
+    names = both(packed_ref, CELLS)
     links_out[...] = names.astype(jnp.int32)
     slot = jnp.broadcast_to(names[:, FACES : FACES + 1], (RANGE, LANES)).astype(jnp.int32)
     placed = jnp.sum(jnp.where(slot == lane, row, 0).astype(jnp.float32), axis=0, keepdims=True)
     chosen = jnp.sum(jnp.where(lane == row, placed, 0.0), axis=1, keepdims=True)
     rows = jnp.broadcast_to(chosen, (RANGE, LANES)).astype(jnp.int32)
-    for i, target in enumerate((p_out, f_out, c_out)):
-        for t in range(CELLS // LANES):
-            target[t] = pick_rows(both(i * CELLS + t * LANES), rows)
+    rows_out[...] = rows
+    reorder(packed_ref, 0, rows, p_out)
     store_faces(faces_out, pack_faces(load(p_out)))
+
+
+def reorder_rest_kernel(rest_ref, rows_ref, f_out, c_out):
+    rows = rows_ref[...]
+    reorder(rest_ref, 0, rows, f_out)
+    reorder(rest_ref, CELLS, rows, c_out)
+
+
+def choose_kernel(pair_ref, out_ref):
+    core = lax.axis_index("d") % 2
+    out_ref[...] = jnp.where(core == 0, pair_ref[1], pair_ref[0])
 
 
 def window(met_ref, faces_ref):
@@ -242,8 +259,9 @@
 
 def join_kernel(met_ref, far_ref, out_ref):
     width = FACES * 2 * LANES
+    core = lax.axis_index("d") % 2
     out_ref[:, :width] = met_ref[...]
-    out_ref[:, width:] = far_ref[...]
+    out_ref[:, width:] = jnp.where(core == 0, far_ref[0], far_ref[1])
 
 
 def final_kernel(u_ref, f_ref, c_ref, links_ref, faces_ref, row_ref, met_ref, out_ref):
@@ -293,7 +311,7 @@
             out_ref[:, t * LANES : (t + 1) * LANES] = half
 
 
-def call(kernel, out_shape, *args, specs=None, scratch=()):
+def call(kernel, out_shape, name, *args, specs=None, scratch=()):
     many = isinstance(out_shape, (list, tuple))
     return pl.pallas_call(
         kernel,
@@ -302,18 +320,21 @@
         out_specs=[VMEM] * len(out_shape) if many else VMEM,
         scratch_shapes=scratch,
         compiler_params=pltpu.CompilerParams(vmem_limit_bytes=GRANT),
+        name=name,
     )(*args)
 
 
 def on_device(groups, pressure, source_term, coefficient, new_slot, face_links):
-    cores, along, across, exchange, far = groups
+    cores, pairs, along, across, exchange, far = groups
     gather = lambda array, members: lax.all_gather(array, "d", axis=0, axis_index_groups=members)
     meet = lambda array: lax.ppermute(array, "d", exchange)
     field = f32(CELLS // LANES, RANGE, LANES)
     packed = f32(RANGE, FACES * 2 * LANES)
-    whole = call(
+    index = jax.ShapeDtypeStruct((RANGE, LANES), jnp.int32)
+    whole, rest = call(
         pack_kernel,
-        f32(RANGE // 2, PACKED),
+        [f32(RANGE // 2, PACKED), f32(RANGE // 2, 2 * CELLS)],
+        "pack",
         *[
             pltpu.with_memory_space_constraint(array, pltpu.HBM)
             for array in (pressure, source_term, coefficient, new_slot, face_links)
@@ -325,22 +346,23 @@
             pltpu.SemaphoreType.DMA((5,)),
         ],
     )
-    u, f, c, links, faces = call(
-        reorder_kernel,
-        [field, field, field, jax.ShapeDtypeStruct((RANGE, LANES), jnp.int32), packed],
-        gather(whole, cores),
+    u, links, rows, faces = call(
+        reorder_kernel, [field, index, index, packed], "reorder", gather(whole, cores)
     )
-    met = gather(meet(faces), cores)
-    u, faces = call(sweep_kernel, [field, packed], u, f, c, links, faces, met)
-    met = gather(meet(faces), cores)
-    u, faces = call(sweep_kernel, [field, packed], u, f, c, links, faces, met)
     met = meet(faces)
-    coarse = call(coarse_kernel, f32(RANGE, LANES), u, f, c, links, faces)
-    coarse = gather(coarse, along)
-    coarse = gather(coarse, across)
-    row = call(row_kernel, f32(RANGE, 2 * LANES), coarse, met)
-    joined = call(join_kernel, f32(RANGE, (FACES + 1) * 2 * LANES), met, lax.ppermute(row, "d", far))
-    return call(final_kernel, f32(RANGE // 2, CELLS), u, f, c, links, faces, row, gather(joined, cores))
+    rest, _ = lax.optimization_barrier((rest, faces))
+    f, c = call(reorder_rest_kernel, [field, field], "rest", gather(rest, cores), rows)
+    u, faces = call(sweep_kernel, [field, packed], "sweep", u, f, c, links, faces, gather(met, cores))
+    met = call(choose_kernel, packed, "choose", gather(faces, pairs))
+    u, faces = call(sweep_kernel, [field, packed], "smooth", u, f, c, links, faces, gather(met, cores))
+    met = meet(faces)
+    coarse = call(coarse_kernel, f32(RANGE, LANES), "coarse", u, f, c, links, faces)
+    coarse = gather(gather(coarse, along), across)
+    row = call(row_kernel, f32(RANGE, 2 * LANES), "row", coarse, met)
+    joined = call(join_kernel, f32(RANGE, (FACES + 1) * 2 * LANES), "join", met, gather(row, far))
+    return call(
+        final_kernel, f32(RANGE // 2, CELLS), "final", u, f, c, links, faces, row, gather(joined, cores)
+    )
 
 
 def solution(mesh):
@@ -350,15 +372,14 @@
     firsts = [2 * i + core for i in range(0, count, ROW) for core in range(2)]
     along = [[i + k, i + k + 2] for i in firsts for k in (0, 4)]
     across = [[i + k, i + 6 - k] for i in firsts for k in (0, 2)]
-    far = [
-        pair
-        for i in range(count - ROW)
-        for pair in ((2 * i + 1, 2 * (i + ROW)), (2 * (i + ROW), 2 * i + 1))
-    ]
+    far = [[2 * i + 1, 2 * (i + ROW)] for i in range(count - ROW)]
+    for i in range(0, ROW, 2):
+        far += [[2 * i, 2 * i + 2], [2 * (count - 1 - i) - 1, 2 * (count - 1 - i) + 1]]
+    pairs = [[2 * i, 2 * i + 3] for i in range(count - 1)] + [[2 * count - 2, 1]]
     exchange = [pair for i in range(count - 1) for pair in ((2 * i, 2 * i + 3), (2 * i + 3, 2 * i))]
     split, line = P("d", None), P("d")
     return jax.shard_map(
-        functools.partial(on_device, (cores, along, across, exchange, far)),
+        functools.partial(on_device, (cores, pairs, along, across, exchange, far)),
         mesh=Mesh(devices, ("d",)),
         in_specs=(split, split, split, line, split),
         out_specs=split,

time: 55.2 us -> 54.2 us (0.982)
  the two profiles are of different devices: /device:TPU:513 before, /device:TPU:1 now
where the time goes in v7:
time: 54.2 us; the launch traced here: 54 us
  blocking collectives  48.7 us (90%)
  Pallas kernels  3.89 us (7%)
  starting transfers between devices  1.33 us (2%)
    all_gather x9, blocking collectives, on_device(): lax.all_gather(array, 'd', axis=0, axis_index_groups=members)  48.7 us
    pallas_call x10, Pallas kernels, call(): pl.pallas_call(kernel, out_shape=out_shape, in_specs=specs or [VMEM] * le...  3.89 us
    ppermute x2, starting transfers between devices, on_device(): meet = lambda array: lax.ppermute(array, 'd', exchange)  1.33 us
  transfers between devices with their start and end apart: 2, of which 0 were waited for; matrix products, arithmetic and copies ran while one was open for 0% of the time, Pallas kernels for 0%

profile of v7, /device:TPU:1, one launch (start us, length us, event | category | flops | bytes accessed | tf_op | source)
XLA Modules:
  0.0 54.0 jit_solution(6148251026032457989)
XLA Ops:
  0.0 1.0 %pack.1 = (f32[4,4224]{1,0:T(4,128)S(1)}, f32[4,8192]{1,0:T(4,128)S(1)}) custom-call(f32[4,4096]{1,0:T(4,128)} %p_ref.1, f32[4,4096]{1,0:T(4,128)} %f_ref.1, f32[4,4096]{1,0:T(4,128)} %c_ref.1, s32[4]{0:T(128)} %slot_ref.1, s32[4,6]{1,0:T(4,128)} %links_ref.1), custom_call_target="tpu_custom_call" | custom-call | tf_op jit(solution)/shard_map/pack/pallas_call | solution.py:316
  1.0 12.0 %all-gather.9.packed_ref = f32[2,4,4224]{2,1,0:T(4,128)S(1)} all-gather(f32[1,4,4224]{2,1,0:T(4,128)S(1)} %bitcast.14), channel_id=2, replica_groups={{0,1},{2,3},{4,5},{6,7},{8,9},{10,11},{12,13},{14,15},{16,17},{18,19},{..., dimensions={0}, use_global_device_ids=true | all-gather | bytes 202752 | tf_op jit(solution)/shard_map/all_gather | solution.py:329
  13.0 0.3 reorder.1
  13.3 0.7 %collective-permute-start = (f32[8,1536]{1,0:T(8,128)S(1)}, f32[8,1536]{1,0:T(8,128)S(1)}, u32[]{:S(2)}, u32[]{:S(2)}) collective-permute-start(f32[8,1536]{1,0:T(8,128)S(1)} %get-tuple-element.21.faces_ref), channel_id=1, source_target_pairs={{0,3},{3,0},{2,5},{5,2},{4,7},{7,4},{6,9},{9,6},{8,11},{11,8},{10,... | collective-permute-start | bytes 147464 | tf_op jit(solution)/shard_map/ppermute | solution.py:330
  14.0 3.2 %all-gather.10.rest_ref = f32[2,4,8192]{2,1,0:T(4,128)S(1)} all-gather(f32[1,4,8192]{2,1,0:T(4,128)S(1)} %bitcast.13), channel_id=3, replica_groups={{0,1},{2,3},{4,5},{6,7},{8,9},{10,11},{12,13},{14,15},{16,17},{18,19},{..., dimensions={0}, use_global_device_ids=true | all-gather | bytes 393216 | tf_op jit(solution)/shard_map/all_gather | solution.py:329
  17.3 0.0 collective-permute-done
  17.3 3.3 %all-gather.2 = f32[16,1536]{1,0:T(8,128)S(1)} all-gather(f32[8,1536]{1,0:T(8,128)S(1)} %collective-permute-done), channel_id=4, replica_groups={{0,1},{2,3},{4,5},{6,7},{8,9},{10,11},{12,13},{14,15},{16,17},{18,19},{..., dimensions={0}, use_global_device_ids=true | all-gather | bytes 147456 | tf_op jit(solution)/shard_map/all_gather | solution.py:329
  20.6 0.4 sweep.1
  21.1 11.0 %all-gather.3 = f32[16,1536]{1,0:T(8,128)S(1)} all-gather(f32[8,1536]{1,0:T(8,128)S(1)} %get-tuple-element.28.faces_ref), channel_id=5, replica_groups={{0,3},{2,5},{4,7},{6,9},{8,11},{10,13},{12,15},{14,17},{16,19},{18,21},..., dimensions={0}, use_global_device_ids=true | all-gather | bytes 147456 | tf_op jit(solution)/shard_map/all_gather | solution.py:329
  32.0 1.9 %all-gather.4 = f32[16,1536]{1,0:T(8,128)S(1)} all-gather(f32[8,1536]{1,0:T(8,128)S(1)} %choose.1), channel_id=6, replica_groups={{0,1},{2,3},{4,5},{6,7},{8,9},{10,11},{12,13},{14,15},{16,17},{18,19},{..., dimensions={0}, use_global_device_ids=true | all-gather | bytes 147456 | tf_op jit(solution)/shard_map/all_gather | solution.py:329
  33.9 0.4 smooth.1
  34.4 0.7 %collective-permute-start.1 = (f32[8,1536]{1,0:T(8,128)S(1)}, f32[8,1536]{1,0:T(8,128)S(1)}, u32[]{:S(2)}, u32[]{:S(2)}) collective-permute-start(f32[8,1536]{1,0:T(8,128)S(1)} %get-tuple-element.30.faces_ref), channel_id=1, source_target_pairs={{0,3},{3,0},{2,5},{5,2},{4,7},{7,4},{6,9},{9,6},{8,11},{11,8},{10,... | collective-permute-start | bytes 147464 | tf_op jit(solution)/shard_map/ppermute | solution.py:330
  35.0 0.1 coarse.1
  35.2 4.5 %all-gather.5 = f32[16,128]{1,0:T(8,128)S(1)} all-gather(f32[8,128]{1,0:T(8,128)S(1)} %coarse.1), channel_id=7, replica_groups={{0,2},{4,6},{1,3},{5,7},{8,10},{12,14},{9,11},{13,15},{16,18},{20,22},{..., dimensions={0}, use_global_device_ids=true | all-gather | bytes 12288 | tf_op jit(solution)/shard_map/all_gather | solution.py:329
  39.7 4.4 %all-gather.6 = f32[4,8,128]{2,1,0:T(8,128)S(1)} all-gather(f32[2,8,128]{2,1,0:T(8,128)S(1)} %bitcast.17), channel_id=8, replica_groups={{0,6},{2,4},{1,7},{3,5},{8,14},{10,12},{9,15},{11,13},{16,22},{18,20},{..., dimensions={0}, use_global_device_ids=true | all-gather | bytes 24576 | tf_op jit(solution)/shard_map/all_gather | solution.py:329
  44.1 0.0 collective-permute-done.1.met_ref
  44.1 0.1 row.1.row_ref
  44.2 3.8 %all-gather.7 = f32[16,256]{1,0:T(8,128)S(1)} all-gather(f32[8,256]{1,0:T(8,128)S(1)} %row.1.row_ref), channel_id=9, replica_groups={{1,8},{3,10},{5,12},{7,14},{9,16},{11,18},{13,20},{15,22},{17,24},{19,2..., dimensions={0}, use_global_device_ids=true | all-gather | bytes 24576 | tf_op jit(solution)/shard_map/all_gather | solution.py:329
  48.0 4.5 %all-gather.8 = f32[16,1792]{1,0:T(8,128)S(1)} all-gather(f32[8,1792]{1,0:T(8,128)S(1)} %join.1), channel_id=10, replica_groups={{0,1},{2,3},{4,5},{6,7},{8,9},{10,11},{12,13},{14,15},{16,17},{18,19},{..., dimensions={0}, use_global_device_ids=true | all-gather | bytes 172032 | tf_op jit(solution)/shard_map/all_gather | solution.py:329
  52.6 1.4 %final.1 = f32[4,4096]{1,0:T(4,128)} custom-call(f32[32,8,128]{2,1,0:T(8,128)S(1)} %get-tuple-element.29.u_ref, f32[32,8,128]{2,1,0:T(8,128)S(1)} %get-tuple-element.24.f_ref, f32[32,8,128]{2,1,0:T(8,128)S(1)} %get-tuple-element.25.c_ref, s32[8,128]{1,0:T(8,128)S(1)} %get-tuple-element.26.links_ref, f32[8,1536]{1,0:T(8,128)S(1)} %get-tuple-element.30.faces_ref, ...), custom_call_target="tpu_custom_call" | custom-call | tf_op jit(solution)/shard_map/final/pallas_call | solution.py:316
  (3 shorter events, 0.0 us)
Async XLA Ops:
  13.3 4.0 %collective-permute-start = (f32[8,1536]{1,0:T(8,128)S(1)}, f32[8,1536]{1,0:T(8,128)S(1)}, u32[]{:S(2)}, u32[]{:S(2)}) collective-permute-start(f32[8,1536]{1,0:T(8,128)S(1)} %get-tuple-element.21.faces_ref), channel_id=1, source_target_pairs={{0,3},{3,0},{2,5},{5,2},{4,7},{7,4},{6,9},{9,6},{8,11},{11,8},{10,... | collective-permute-start | bytes 147464 | tf_op jit(solution)/shard_map/ppermute | solution.py:330
  34.4 9.7 %collective-permute-start.1 = (f32[8,1536]{1,0:T(8,128)S(1)}, f32[8,1536]{1,0:T(8,128)S(1)}, u32[]{:S(2)}, u32[]{:S(2)}) collective-permute-start(f32[8,1536]{1,0:T(8,128)S(1)} %get-tuple-element.30.faces_ref), channel_id=1, source_target_pairs={{0,3},{3,0},{2,5},{5,2},{4,7},{7,4},{6,9},{9,6},{8,11},{11,8},{10,... | collective-permute-start | bytes 147464 | tf_op jit(solution)/shard_map/ppermute | solution.py:330

commit v8 on v7

--- a/solution.py
+++ b/solution.py
@@ -19,6 +19,7 @@
 FLIPPED = (1, 0, 3, 2, 5, 4)
 ROW = 4
 SLOTS = 16
+PARTS = 4
 PACKED = CELLS + LANES
 
 VMEM = pl.BlockSpec(memory_space=pltpu.VMEM)
@@ -123,15 +124,14 @@
     return total
 
 
+def relax(tiles, ghosts, source_ref, coefficient_ref, x, h):
+    weight = RELAXATION / (6.0 + coefficient_ref[2 * x + h])
+    gathered = source_ref[2 * x + h] + beside(tiles, ghosts, x, h)
+    return (1.0 - RELAXATION) * tiles[x][h] + weight * gathered
+
+
 def sweep(tiles, ghosts, source_ref, coefficient_ref):
-    out = []
-    for x in range(SIDE):
-        out.append([])
-        for h in range(2):
-            weight = RELAXATION / (6.0 + coefficient_ref[2 * x + h])
-            gathered = source_ref[2 * x + h] + beside(tiles, ghosts, x, h)
-            out[x].append((1.0 - RELAXATION) * tiles[x][h] + weight * gathered)
-    return out
+    return [[relax(tiles, ghosts, source_ref, coefficient_ref, x, h) for h in range(2)] for x in range(SIDE)]
 
 
 def range_base():
@@ -187,11 +187,6 @@
     rows = rows_ref[...]
     reorder(rest_ref, 0, rows, f_out)
     reorder(rest_ref, CELLS, rows, c_out)
-
-
-def choose_kernel(pair_ref, out_ref):
-    core = lax.axis_index("d") % 2
-    out_ref[...] = jnp.where(core == 0, pair_ref[1], pair_ref[0])
 
 
 def window(met_ref, faces_ref):
@@ -264,7 +259,7 @@
     out_ref[:, width:] = jnp.where(core == 0, far_ref[0], far_ref[1])
 
 
-def final_kernel(u_ref, f_ref, c_ref, links_ref, faces_ref, row_ref, met_ref, out_ref):
+def final_kernel(u_ref, f_ref, c_ref, links_ref, faces_ref, row_ref, met_ref, out_ref, held, sems):
     core, curve = lax.axis_index("d") % 2, lax.axis_index("d") // 2
     row = sublanes()
     part = (lanes() // (ROW * RANGE) + SLOTS // ROW - curve // ROW % (SLOTS // ROW)) % (SLOTS // ROW)
@@ -302,22 +297,29 @@
         raised = lane_sum(jnp.where(own, jnp.broadcast_to(near[d : d + 1], (RANGE, LANES)), 0.0))
         ghosts[d] = [half + raised for half in ghosts[d]]
     tiles = [[tile + lift for tile in pair] for pair in load(u_ref)]
-    tiles = sweep(tiles, ghosts, f_ref, c_ref)
+    copies = []
     for x in range(SIDE):
         for h in range(2):
-            tile = tiles[x][h]
+            t = 2 * x + h
+            tile = relax(tiles, ghosts, f_ref, c_ref, x, h)
             half = jnp.where(core == 0, tile[0 : RANGE // 2], tile[RANGE // 2 :])
-            t = 2 * x + h
-            out_ref[:, t * LANES : (t + 1) * LANES] = half
-
-
-def call(kernel, out_shape, name, *args, specs=None, scratch=()):
+            held[:, t * LANES : (t + 1) * LANES] = half
+        if x % (SIDE // PARTS) == SIDE // PARTS - 1:
+            part = len(copies)
+            span = slice(part * CELLS // PARTS, (part + 1) * CELLS // PARTS)
+            copies.append(pltpu.make_async_copy(held.at[:, span], out_ref.at[:, span], sems.at[part]))
+            copies[-1].start()
+    for copy in copies:
+        copy.wait()
+
+
+def call(kernel, out_shape, name, *args, specs=None, out=VMEM, scratch=()):
     many = isinstance(out_shape, (list, tuple))
     return pl.pallas_call(
         kernel,
         out_shape=out_shape,
         in_specs=specs or [VMEM] * len(args),
-        out_specs=[VMEM] * len(out_shape) if many else VMEM,
+        out_specs=[out] * len(out_shape) if many else out,
         scratch_shapes=scratch,
         compiler_params=pltpu.CompilerParams(vmem_limit_bytes=GRANT),
         name=name,
@@ -325,7 +327,7 @@
 
 
 def on_device(groups, pressure, source_term, coefficient, new_slot, face_links):
-    cores, pairs, along, across, exchange, far = groups
+    cores, along, across, exchange, far = groups
     gather = lambda array, members: lax.all_gather(array, "d", axis=0, axis_index_groups=members)
     meet = lambda array: lax.ppermute(array, "d", exchange)
     field = f32(CELLS // LANES, RANGE, LANES)
@@ -353,15 +355,25 @@
     rest, _ = lax.optimization_barrier((rest, faces))
     f, c = call(reorder_rest_kernel, [field, field], "rest", gather(rest, cores), rows)
     u, faces = call(sweep_kernel, [field, packed], "sweep", u, f, c, links, faces, gather(met, cores))
-    met = call(choose_kernel, packed, "choose", gather(faces, pairs))
-    u, faces = call(sweep_kernel, [field, packed], "smooth", u, f, c, links, faces, gather(met, cores))
+    u, faces = call(sweep_kernel, [field, packed], "smooth", u, f, c, links, faces, gather(meet(faces), cores))
     met = meet(faces)
     coarse = call(coarse_kernel, f32(RANGE, LANES), "coarse", u, f, c, links, faces)
     coarse = gather(gather(coarse, along), across)
     row = call(row_kernel, f32(RANGE, 2 * LANES), "row", coarse, met)
     joined = call(join_kernel, f32(RANGE, (FACES + 1) * 2 * LANES), "join", met, gather(row, far))
     return call(
-        final_kernel, f32(RANGE // 2, CELLS), "final", u, f, c, links, faces, row, gather(joined, cores)
+        final_kernel,
+        f32(RANGE // 2, CELLS),
+        "final",
+        u,
+        f,
+        c,
+        links,
+        faces,
+        row,
+        gather(joined, cores),
+        out=HBM,
+        scratch=[pltpu.VMEM((RANGE // 2, CELLS), jnp.float32), pltpu.SemaphoreType.DMA((PARTS,))],
     )
 
 
@@ -375,11 +387,10 @@
     far = [[2 * i + 1, 2 * (i + ROW)] for i in range(count - ROW)]
     for i in range(0, ROW, 2):
         far += [[2 * i, 2 * i + 2], [2 * (count - 1 - i) - 1, 2 * (count - 1 - i) + 1]]
-    pairs = [[2 * i, 2 * i + 3] for i in range(count - 1)] + [[2 * count - 2, 1]]
     exchange = [pair for i in range(count - 1) for pair in ((2 * i, 2 * i + 3), (2 * i + 3, 2 * i))]
     split, line = P("d", None), P("d")
     return jax.shard_map(
-        functools.partial(on_device, (cores, pairs, along, across, exchange, far)),
+        functools.partial(on_device, (cores, along, across, exchange, far)),
         mesh=Mesh(devices, ("d",)),
         in_specs=(split, split, split, line, split),
         out_specs=split,

time: 54.2 us -> 53.9 us (level)
  the two profiles are of different devices: /device:TPU:1 before, /device:TPU:513 now
where the time goes in v8:
time: 53.9 us; the launch traced here: 53.6 us
  starting transfers between devices  26.2 us (49%)
  blocking collectives  21.3 us (40%)
  Pallas kernels  3.89 us (7%)
  waiting for transfers between devices  2.17 us (4%)
    ppermute x3, starting transfers between devices, on_device(): meet = lambda array: lax.ppermute(array, 'd', exchange)  26.2 us
    all_gather x8, blocking collectives, on_device(): lax.all_gather(array, 'd', axis=0, axis_index_groups=members)  21.3 us
    pallas_call x9, Pallas kernels, call(): pl.pallas_call(kernel, out_shape=out_shape, in_specs=specs or [VMEM] * le...  3.89 us
    ppermute x3, waiting for transfers between devices, on_device(): meet = lambda array: lax.ppermute(array, 'd', exchange)  2.17 us
  transfers between devices with their start and end apart: 3, of which 2 were waited for; matrix products, arithmetic and copies ran while one was open for 0% of the time, Pallas kernels for 0%

profile of v8, /device:TPU:513, one launch (start us, length us, event | category | flops | bytes accessed | tf_op | source)
XLA Modules:
  0.0 53.6 jit_solution(17588313862933131588)
XLA Ops:
  0.0 1.0 %pack.1 = (f32[4,4224]{1,0:T(4,128)S(1)}, f32[4,8192]{1,0:T(4,128)S(1)}) custom-call(f32[4,4096]{1,0:T(4,128)} %p_ref.1, f32[4,4096]{1,0:T(4,128)} %f_ref.1, f32[4,4096]{1,0:T(4,128)} %c_ref.1, s32[4]{0:T(128)} %slot_ref.1, s32[4,6]{1,0:T(4,128)} %links_ref.1), custom_call_target="tpu_custom_call" | custom-call | tf_op jit(solution)/shard_map/pack/pallas_call | solution.py:318
  1.0 2.2 %all-gather.8.packed_ref = f32[2,4,4224]{2,1,0:T(4,128)S(1)} all-gather(f32[1,4,4224]{2,1,0:T(4,128)S(1)} %bitcast.12), channel_id=2, replica_groups={{0,1},{2,3},{4,5},{6,7},{8,9},{10,11},{12,13},{14,15},{16,17},{18,19},{..., dimensions={0}, use_global_device_ids=true | all-gather | bytes 202752 | tf_op jit(solution)/shard_map/all_gather | solution.py:331
  3.2 0.3 reorder.1
  3.5 8.7 %collective-permute-start = (f32[8,1536]{1,0:T(8,128)S(1)}, f32[8,1536]{1,0:T(8,128)S(1)}, u32[]{:S(2)}, u32[]{:S(2)}) collective-permute-start(f32[8,1536]{1,0:T(8,128)S(1)} %get-tuple-element.21.faces_ref), channel_id=1, source_target_pairs={{0,3},{3,0},{2,5},{5,2},{4,7},{7,4},{6,9},{9,6},{8,11},{11,8},{10,... | collective-permute-start | bytes 147464 | tf_op jit(solution)/shard_map/ppermute | solution.py:332
  12.3 2.0 %all-gather.9.rest_ref = f32[2,4,8192]{2,1,0:T(4,128)S(1)} all-gather(f32[1,4,8192]{2,1,0:T(4,128)S(1)} %bitcast.11), channel_id=3, replica_groups={{0,1},{2,3},{4,5},{6,7},{8,9},{10,11},{12,13},{14,15},{16,17},{18,19},{..., dimensions={0}, use_global_device_ids=true | all-gather | bytes 393216 | tf_op jit(solution)/shard_map/all_gather | solution.py:331
  14.3 0.1 collective-permute-done
  14.4 1.9 %all-gather.2 = f32[16,1536]{1,0:T(8,128)S(1)} all-gather(f32[8,1536]{1,0:T(8,128)S(1)} %collective-permute-done), channel_id=4, replica_groups={{0,1},{2,3},{4,5},{6,7},{8,9},{10,11},{12,13},{14,15},{16,17},{18,19},{..., dimensions={0}, use_global_device_ids=true | all-gather | bytes 147456 | tf_op jit(solution)/shard_map/all_gather | solution.py:331
  16.2 0.4 sweep.1
  16.7 8.7 %collective-permute-start.1 = (f32[8,1536]{1,0:T(8,128)S(1)}, f32[8,1536]{1,0:T(8,128)S(1)}, u32[]{:S(2)}, u32[]{:S(2)}) collective-permute-start(f32[8,1536]{1,0:T(8,128)S(1)} %get-tuple-element.28.faces_ref), channel_id=1, source_target_pairs={{0,3},{3,0},{2,5},{5,2},{4,7},{7,4},{6,9},{9,6},{8,11},{11,8},{10,... | collective-permute-start | bytes 147464 | tf_op jit(solution)/shard_map/ppermute | solution.py:332
  25.4 2.1 %collective-permute-done.1 = f32[8,1536]{1,0:T(8,128)S(1)} collective-permute-done((f32[8,1536]{1,0:T(8,128)S(1)}, f32[8,1536]{1,0:T(8,128)S(1)}, u32[]{:S(2)}, u32[]{:S(2)}) %collective-permute-start.1) | collective-permute-done | bytes 49184 | tf_op jit(solution)/shard_map/ppermute | solution.py:332
  27.5 1.9 %all-gather.3 = f32[16,1536]{1,0:T(8,128)S(1)} all-gather(f32[8,1536]{1,0:T(8,128)S(1)} %collective-permute-done.1), channel_id=5, replica_groups={{0,1},{2,3},{4,5},{6,7},{8,9},{10,11},{12,13},{14,15},{16,17},{18,19},{..., dimensions={0}, use_global_device_ids=true | all-gather | bytes 147456 | tf_op jit(solution)/shard_map/all_gather | solution.py:331
  29.4 0.4 smooth.1
  29.8 8.7 %collective-permute-start.2 = (f32[8,1536]{1,0:T(8,128)S(1)}, f32[8,1536]{1,0:T(8,128)S(1)}, u32[]{:S(2)}, u32[]{:S(2)}) collective-permute-start(f32[8,1536]{1,0:T(8,128)S(1)} %get-tuple-element.30.faces_ref), channel_id=1, source_target_pairs={{0,3},{3,0},{2,5},{5,2},{4,7},{7,4},{6,9},{9,6},{8,11},{11,8},{10,... | collective-permute-start | bytes 147464 | tf_op jit(solution)/shard_map/ppermute | solution.py:332
  38.6 0.1 coarse.1
  38.7 3.2 %all-gather.4 = f32[16,128]{1,0:T(8,128)S(1)} all-gather(f32[8,128]{1,0:T(8,128)S(1)} %coarse.1), channel_id=6, replica_groups={{0,2},{4,6},{1,3},{5,7},{8,10},{12,14},{9,11},{13,15},{16,18},{20,22},{..., dimensions={0}, use_global_device_ids=true | all-gather | bytes 12288 | tf_op jit(solution)/shard_map/all_gather | solution.py:331
  41.9 4.4 %all-gather.5 = f32[4,8,128]{2,1,0:T(8,128)S(1)} all-gather(f32[2,8,128]{2,1,0:T(8,128)S(1)} %bitcast.15), channel_id=7, replica_groups={{0,6},{2,4},{1,7},{3,5},{8,14},{10,12},{9,15},{11,13},{16,22},{18,20},{..., dimensions={0}, use_global_device_ids=true | all-gather | bytes 24576 | tf_op jit(solution)/shard_map/all_gather | solution.py:331
  46.3 0.0 collective-permute-done.2.met_ref
  46.3 0.1 row.1.row_ref
  46.5 3.8 %all-gather.6 = f32[16,256]{1,0:T(8,128)S(1)} all-gather(f32[8,256]{1,0:T(8,128)S(1)} %row.1.row_ref), channel_id=8, replica_groups={{1,8},{3,10},{5,12},{7,14},{9,16},{11,18},{13,20},{15,22},{17,24},{19,2..., dimensions={0}, use_global_device_ids=true | all-gather | bytes 24576 | tf_op jit(solution)/shard_map/all_gather | solution.py:331
  50.3 1.9 %all-gather.7 = f32[16,1792]{1,0:T(8,128)S(1)} all-gather(f32[8,1792]{1,0:T(8,128)S(1)} %join.1), channel_id=9, replica_groups={{0,1},{2,3},{4,5},{6,7},{8,9},{10,11},{12,13},{14,15},{16,17},{18,19},{..., dimensions={0}, use_global_device_ids=true | all-gather | bytes 172032 | tf_op jit(solution)/shard_map/all_gather | solution.py:331
  52.2 1.4 %final.1 = f32[4,4096]{1,0:T(4,128)} custom-call(f32[32,8,128]{2,1,0:T(8,128)S(1)} %get-tuple-element.29.u_ref, f32[32,8,128]{2,1,0:T(8,128)S(1)} %get-tuple-element.24.f_ref, f32[32,8,128]{2,1,0:T(8,128)S(1)} %get-tuple-element.25.c_ref, s32[8,128]{1,0:T(8,128)S(1)} %get-tuple-element.26.links_ref, f32[8,1536]{1,0:T(8,128)S(1)} %get-tuple-element.30.faces_ref, ...), custom_call_target="tpu_custom_call" | custom-call | tf_op jit(solution)/shard_map/final/pallas_call | solution.py:318
  (2 shorter events, 0.0 us)
Async XLA Ops:
  3.5 10.8 %collective-permute-start = (f32[8,1536]{1,0:T(8,128)S(1)}, f32[8,1536]{1,0:T(8,128)S(1)}, u32[]{:S(2)}, u32[]{:S(2)}) collective-permute-start(f32[8,1536]{1,0:T(8,128)S(1)} %get-tuple-element.21.faces_ref), channel_id=1, source_target_pairs={{0,3},{3,0},{2,5},{5,2},{4,7},{7,4},{6,9},{9,6},{8,11},{11,8},{10,... | collective-permute-start | bytes 147464 | tf_op jit(solution)/shard_map/ppermute | solution.py:332
  16.7 10.8 %collective-permute-start.1 = (f32[8,1536]{1,0:T(8,128)S(1)}, f32[8,1536]{1,0:T(8,128)S(1)}, u32[]{:S(2)}, u32[]{:S(2)}) collective-permute-start(f32[8,1536]{1,0:T(8,128)S(1)} %get-tuple-element.28.faces_ref), channel_id=1, source_target_pairs={{0,3},{3,0},{2,5},{5,2},{4,7},{7,4},{6,9},{9,6},{8,11},{11,8},{10,... | collective-permute-start | bytes 147464 | tf_op jit(solution)/shard_map/ppermute | solution.py:332
  29.8 16.5 %collective-permute-start.2 = (f32[8,1536]{1,0:T(8,128)S(1)}, f32[8,1536]{1,0:T(8,128)S(1)}, u32[]{:S(2)}, u32[]{:S(2)}) collective-permute-start(f32[8,1536]{1,0:T(8,128)S(1)} %get-tuple-element.30.faces_ref), channel_id=1, source_target_pairs={{0,3},{3,0},{2,5},{5,2},{4,7},{7,4},{6,9},{9,6},{8,11},{11,8},{10,... | collective-permute-start | bytes 147464 | tf_op jit(solution)/shard_map/ppermute | solution.py:332

commit v9 on v8

--- a/solution.py
+++ b/solution.py
@@ -18,8 +18,8 @@
 FACES = 6
 FLIPPED = (1, 0, 3, 2, 5, 4)
 ROW = 4
+BROKEN = 2
 SLOTS = 16
-PARTS = 4
 PACKED = CELLS + LANES
 
 VMEM = pl.BlockSpec(memory_space=pltpu.VMEM)
@@ -187,6 +187,12 @@
     rows = rows_ref[...]
     reorder(rest_ref, 0, rows, f_out)
     reorder(rest_ref, CELLS, rows, c_out)
+
+
+def choose_kernel(pair_ref, single_ref, out_ref):
+    me = lax.axis_index("d")
+    single = jnp.logical_or(me == 2 * BROKEN, me == 2 * BROKEN + 3)
+    out_ref[...] = jnp.where(single, single_ref[...], jnp.where(me % 2 == 0, pair_ref[1], pair_ref[0]))
 
 
 def window(met_ref, faces_ref):
@@ -259,7 +265,7 @@
     out_ref[:, width:] = jnp.where(core == 0, far_ref[0], far_ref[1])
 
 
-def final_kernel(u_ref, f_ref, c_ref, links_ref, faces_ref, row_ref, met_ref, out_ref, held, sems):
+def final_kernel(u_ref, f_ref, c_ref, links_ref, faces_ref, row_ref, met_ref, out_ref):
     core, curve = lax.axis_index("d") % 2, lax.axis_index("d") // 2
     row = sublanes()
     part = (lanes() // (ROW * RANGE) + SLOTS // ROW - curve // ROW % (SLOTS // ROW)) % (SLOTS // ROW)
@@ -285,41 +291,42 @@
     diag = jnp.broadcast_to(sums[FACES + 1 : FACES + 2], (RANGE, LANES))
     diag = jnp.where(diag > 0.0, diag, 1.0)
     residual = inner + total(named(sums))
-    error = jnp.zeros((RANGE, LANES), jnp.float32)
-    for step in range(COARSE_SWEEPS):
-        near = total(named(error)) if step else 0.0
-        error = error + RELAXATION * (residual - diag * error + near) / diag
+    weight = RELAXATION / diag
+    error = weight * residual
+    for step in range(COARSE_SWEEPS - 1):
+        error = (1.0 - RELAXATION) * error + weight * (residual + total(named(error)))
     near = named(error)
     own = lanes() == curve % SLOTS * RANGE + row
     lift = lane_sum(jnp.where(own, error, 0.0))
     ghosts, _ = ghost_faces(links_ref[...], range_base(), *window(met_ref, faces_ref))
+    raised = []
     for d in range(FACES):
-        raised = lane_sum(jnp.where(own, jnp.broadcast_to(near[d : d + 1], (RANGE, LANES)), 0.0))
-        ghosts[d] = [half + raised for half in ghosts[d]]
-    tiles = [[tile + lift for tile in pair] for pair in load(u_ref)]
-    copies = []
+        raised.append(lane_sum(jnp.where(own, jnp.broadcast_to(near[d : d + 1], (RANGE, LANES)), 0.0)))
+    lane = lanes()
+    z = lane % SIDE
+    around = []
+    for h in range(2):
+        low_y = jnp.where(lane < SIDE, raised[2], lift) if h == 0 else lift
+        high_y = jnp.where(lane >= LANES - SIDE, raised[3], lift) if h == 1 else lift
+        around.append(low_y + high_y + jnp.where(z == 0, raised[4], lift) + jnp.where(z == SIDE - 1, raised[5], lift))
+    tiles = load(u_ref)
     for x in range(SIDE):
         for h in range(2):
             t = 2 * x + h
-            tile = relax(tiles, ghosts, f_ref, c_ref, x, h)
+            weight = RELAXATION / (6.0 + c_ref[t])
+            near = around[h] + (lift if x else raised[0]) + (lift if x < SIDE - 1 else raised[1])
+            tile = relax(tiles, ghosts, f_ref, c_ref, x, h) + ((1.0 - RELAXATION) * lift + weight * near)
             half = jnp.where(core == 0, tile[0 : RANGE // 2], tile[RANGE // 2 :])
-            held[:, t * LANES : (t + 1) * LANES] = half
-        if x % (SIDE // PARTS) == SIDE // PARTS - 1:
-            part = len(copies)
-            span = slice(part * CELLS // PARTS, (part + 1) * CELLS // PARTS)
-            copies.append(pltpu.make_async_copy(held.at[:, span], out_ref.at[:, span], sems.at[part]))
-            copies[-1].start()
-    for copy in copies:
-        copy.wait()
-
-
-def call(kernel, out_shape, name, *args, specs=None, out=VMEM, scratch=()):
+            out_ref[:, t * LANES : (t + 1) * LANES] = half
+
+
+def call(kernel, out_shape, name, *args, specs=None, scratch=()):
     many = isinstance(out_shape, (list, tuple))
     return pl.pallas_call(
         kernel,
         out_shape=out_shape,
         in_specs=specs or [VMEM] * len(args),
-        out_specs=[out] * len(out_shape) if many else out,
+        out_specs=[VMEM] * len(out_shape) if many else VMEM,
         scratch_shapes=scratch,
         compiler_params=pltpu.CompilerParams(vmem_limit_bytes=GRANT),
         name=name,
@@ -327,7 +334,7 @@
 
 
 def on_device(groups, pressure, source_term, coefficient, new_slot, face_links):
-    cores, along, across, exchange, far = groups
+    cores, pairs, single, along, across, exchange, far = groups
     gather = lambda array, members: lax.all_gather(array, "d", axis=0, axis_index_groups=members)
     meet = lambda array: lax.ppermute(array, "d", exchange)
     field = f32(CELLS // LANES, RANGE, LANES)
@@ -355,7 +362,8 @@
     rest, _ = lax.optimization_barrier((rest, faces))
     f, c = call(reorder_rest_kernel, [field, field], "rest", gather(rest, cores), rows)
     u, faces = call(sweep_kernel, [field, packed], "sweep", u, f, c, links, faces, gather(met, cores))
-    u, faces = call(sweep_kernel, [field, packed], "smooth", u, f, c, links, faces, gather(meet(faces), cores))
+    met = call(choose_kernel, packed, "choose", gather(faces, pairs), lax.ppermute(faces, "d", single))
+    u, faces = call(sweep_kernel, [field, packed], "smooth", u, f, c, links, faces, gather(met, cores))
     met = meet(faces)
     coarse = call(coarse_kernel, f32(RANGE, LANES), "coarse", u, f, c, links, faces)
     coarse = gather(gather(coarse, along), across)
@@ -372,8 +380,6 @@
         faces,
         row,
         gather(joined, cores),
-        out=HBM,
-        scratch=[pltpu.VMEM((RANGE // 2, CELLS), jnp.float32), pltpu.SemaphoreType.DMA((PARTS,))],
     )
 
 
@@ -387,10 +393,13 @@
     far = [[2 * i + 1, 2 * (i + ROW)] for i in range(count - ROW)]
     for i in range(0, ROW, 2):
         far += [[2 * i, 2 * i + 2], [2 * (count - 1 - i) - 1, 2 * (count - 1 - i) + 1]]
+    pairs = [[2 * i, 2 * i + 3] for i in range(count - 1) if i != BROKEN]
+    pairs += [[2 * BROKEN, 1], [2 * count - 2, 2 * BROKEN + 3]]
+    single = [(2 * BROKEN, 2 * BROKEN + 3), (2 * BROKEN + 3, 2 * BROKEN)]
     exchange = [pair for i in range(count - 1) for pair in ((2 * i, 2 * i + 3), (2 * i + 3, 2 * i))]
     split, line = P("d", None), P("d")
     return jax.shard_map(
-        functools.partial(on_device, (cores, along, across, exchange, far)),
+        functools.partial(on_device, (cores, pairs, single, along, across, exchange, far)),
         mesh=Mesh(devices, ("d",)),
         in_specs=(split, split, split, line, split),
         out_specs=split,

time: 53.9 us -> 53.2 us (0.987)
  blocking collectives: 21.3 us -> 30.9 us
  starting transfers between devices: 26.2 us -> 18.1 us
  waiting for transfers between devices: 2.17 us -> 0.07 us
    all_gather x8 -> x9, blocking collectives: 21.3 us -> 30.9 us  [on_device(): lax.all_gather(array, 'd', axis=0, axis_index_groups=members)]
    ppermute x3 -> x2, starting transfers between devices: 26.2 us -> 17.4 us  [on_device(): meet = lambda array: lax.ppermute(array, 'd', exchange)]
    ppermute x3 -> x2, waiting for transfers between devices: 2.17 us -> 0.07 us  [on_device(): meet = lambda array: lax.ppermute(array, 'd', exchange)]
    ppermute x0 -> x1, starting transfers between devices: none -> 0.66 us  [on_device(): lax.ppermute(faces, 'd', single)]
    pallas_call x9 -> x10, Pallas kernels: 3.89 us -> 3.72 us  [call(): pl.pallas_call(kernel, out_shape=out_shape, in_specs=specs or [VMEM] * le...]
  transfers between devices with their start and end apart: 3 -> 3, of which waited for: 2 -> 1; matrix products, arithmetic and copies ran while one was open for 0% -> 0% of each run, Pallas kernels for 0% -> 0%
where the time goes in v9:
time: 53.2 us; the launch traced here: 52.9 us
  blocking collectives  30.9 us (58%)
  starting transfers between devices  18.1 us (34%)
  Pallas kernels  3.72 us (7%)
    all_gather x9, blocking collectives, on_device(): lax.all_gather(array, 'd', axis=0, axis_index_groups=members)  30.9 us
    ppermute x2, starting transfers between devices, on_device(): meet = lambda array: lax.ppermute(array, 'd', exchange)  17.4 us
    pallas_call x10, Pallas kernels, call(): pl.pallas_call(kernel, out_shape=out_shape, in_specs=specs or [VMEM] * le...  3.72 us
  transfers between devices with their start and end apart: 3, of which 1 were waited for; matrix products, arithmetic and copies ran while one was open for 0% of the time, Pallas kernels for 0%

profile of v9, /device:TPU:513, one launch (start us, length us, event | category | flops | bytes accessed | tf_op | source)
XLA Modules:
  0.0 52.9 jit_solution(13549481805614504902)
XLA Ops:
  0.0 1.0 %pack.1 = (f32[4,4224]{1,0:T(4,128)S(1)}, f32[4,8192]{1,0:T(4,128)S(1)}) custom-call(f32[4,4096]{1,0:T(4,128)} %p_ref.1, f32[4,4096]{1,0:T(4,128)} %f_ref.1, f32[4,4096]{1,0:T(4,128)} %c_ref.1, s32[4]{0:T(128)} %slot_ref.1, s32[4,6]{1,0:T(4,128)} %links_ref.1), custom_call_target="tpu_custom_call" | custom-call | tf_op jit(solution)/shard_map/pack/pallas_call | solution.py:325
  1.0 2.2 %all-gather.9.packed_ref = f32[2,4,4224]{2,1,0:T(4,128)S(1)} all-gather(f32[1,4,4224]{2,1,0:T(4,128)S(1)} %bitcast.14), channel_id=2, replica_groups={{0,1},{2,3},{4,5},{6,7},{8,9},{10,11},{12,13},{14,15},{16,17},{18,19},{..., dimensions={0}, use_global_device_ids=true | all-gather | bytes 202752 | tf_op jit(solution)/shard_map/all_gather | solution.py:338
  3.2 0.3 reorder.1
  3.5 8.7 %collective-permute-start = (f32[8,1536]{1,0:T(8,128)S(1)}, f32[8,1536]{1,0:T(8,128)S(1)}, u32[]{:S(2)}, u32[]{:S(2)}) collective-permute-start(f32[8,1536]{1,0:T(8,128)S(1)} %get-tuple-element.21.faces_ref), channel_id=1, source_target_pairs={{0,3},{3,0},{2,5},{5,2},{4,7},{7,4},{6,9},{9,6},{8,11},{11,8},{10,... | collective-permute-start | bytes 147464 | tf_op jit(solution)/shard_map/ppermute | solution.py:339
  12.3 2.0 %all-gather.10.rest_ref = f32[2,4,8192]{2,1,0:T(4,128)S(1)} all-gather(f32[1,4,8192]{2,1,0:T(4,128)S(1)} %bitcast.13), channel_id=3, replica_groups={{0,1},{2,3},{4,5},{6,7},{8,9},{10,11},{12,13},{14,15},{16,17},{18,19},{..., dimensions={0}, use_global_device_ids=true | all-gather | bytes 393216 | tf_op jit(solution)/shard_map/all_gather | solution.py:338
  14.3 0.1 collective-permute-done
  14.4 1.9 %all-gather.2 = f32[16,1536]{1,0:T(8,128)S(1)} all-gather(f32[8,1536]{1,0:T(8,128)S(1)} %collective-permute-done), channel_id=4, replica_groups={{0,1},{2,3},{4,5},{6,7},{8,9},{10,11},{12,13},{14,15},{16,17},{18,19},{..., dimensions={0}, use_global_device_ids=true | all-gather | bytes 147456 | tf_op jit(solution)/shard_map/all_gather | solution.py:338
  16.2 0.4 sweep.1
  16.7 0.7 %collective-permute-start.1 = (f32[8,1536]{1,0:T(8,128)S(1)}, f32[8,1536]{1,0:T(8,128)S(1)}, u32[]{:S(2)}, u32[]{:S(2)}) collective-permute-start(f32[8,1536]{1,0:T(8,128)S(1)} %get-tuple-element.28.faces_ref), channel_id=1, source_target_pairs={{4,7},{7,4}} | collective-permute-start | bytes 147464 | tf_op jit(solution)/shard_map/ppermute | solution.py:365
  17.4 9.6 %all-gather.3 = f32[16,1536]{1,0:T(8,128)S(1)} all-gather(f32[8,1536]{1,0:T(8,128)S(1)} %get-tuple-element.28.faces_ref), channel_id=5, replica_groups={{0,3},{2,5},{6,9},{8,11},{10,13},{12,15},{14,17},{16,19},{18,21},{20,23..., dimensions={0}, use_global_device_ids=true | all-gather | bytes 147456 | tf_op jit(solution)/shard_map/all_gather | solution.py:338
  27.0 0.0 collective-permute-done.1.single_ref
  27.0 1.9 %all-gather.4 = f32[16,1536]{1,0:T(8,128)S(1)} all-gather(f32[8,1536]{1,0:T(8,128)S(1)} %choose.1), channel_id=6, replica_groups={{0,1},{2,3},{4,5},{6,7},{8,9},{10,11},{12,13},{14,15},{16,17},{18,19},{..., dimensions={0}, use_global_device_ids=true | all-gather | bytes 147456 | tf_op jit(solution)/shard_map/all_gather | solution.py:338
  28.9 0.4 smooth.1
  29.3 8.7 %collective-permute-start.2 = (f32[8,1536]{1,0:T(8,128)S(1)}, f32[8,1536]{1,0:T(8,128)S(1)}, u32[]{:S(2)}, u32[]{:S(2)}) collective-permute-start(f32[8,1536]{1,0:T(8,128)S(1)} %get-tuple-element.30.faces_ref), channel_id=1, source_target_pairs={{0,3},{3,0},{2,5},{5,2},{4,7},{7,4},{6,9},{9,6},{8,11},{11,8},{10,... | collective-permute-start | bytes 147464 | tf_op jit(solution)/shard_map/ppermute | solution.py:339
  38.1 0.1 coarse.1
  38.2 3.2 %all-gather.5 = f32[16,128]{1,0:T(8,128)S(1)} all-gather(f32[8,128]{1,0:T(8,128)S(1)} %coarse.1), channel_id=7, replica_groups={{0,2},{4,6},{1,3},{5,7},{8,10},{12,14},{9,11},{13,15},{16,18},{20,22},{..., dimensions={0}, use_global_device_ids=true | all-gather | bytes 12288 | tf_op jit(solution)/shard_map/all_gather | solution.py:338
  41.4 4.4 %all-gather.6 = f32[4,8,128]{2,1,0:T(8,128)S(1)} all-gather(f32[2,8,128]{2,1,0:T(8,128)S(1)} %bitcast.17), channel_id=8, replica_groups={{0,6},{2,4},{1,7},{3,5},{8,14},{10,12},{9,15},{11,13},{16,22},{18,20},{..., dimensions={0}, use_global_device_ids=true | all-gather | bytes 24576 | tf_op jit(solution)/shard_map/all_gather | solution.py:338
  45.8 0.0 collective-permute-done.2.met_ref
  45.8 0.1 row.1.row_ref
  46.0 3.8 %all-gather.7 = f32[16,256]{1,0:T(8,128)S(1)} all-gather(f32[8,256]{1,0:T(8,128)S(1)} %row.1.row_ref), channel_id=9, replica_groups={{1,8},{3,10},{5,12},{7,14},{9,16},{11,18},{13,20},{15,22},{17,24},{19,2..., dimensions={0}, use_global_device_ids=true | all-gather | bytes 24576 | tf_op jit(solution)/shard_map/all_gather | solution.py:338
  49.8 1.9 %all-gather.8 = f32[16,1792]{1,0:T(8,128)S(1)} all-gather(f32[8,1792]{1,0:T(8,128)S(1)} %join.1), channel_id=10, replica_groups={{0,1},{2,3},{4,5},{6,7},{8,9},{10,11},{12,13},{14,15},{16,17},{18,19},{..., dimensions={0}, use_global_device_ids=true | all-gather | bytes 172032 | tf_op jit(solution)/shard_map/all_gather | solution.py:338
  51.7 1.2 %final.1 = f32[4,4096]{1,0:T(4,128)} custom-call(f32[32,8,128]{2,1,0:T(8,128)S(1)} %get-tuple-element.29.u_ref, f32[32,8,128]{2,1,0:T(8,128)S(1)} %get-tuple-element.24.f_ref, f32[32,8,128]{2,1,0:T(8,128)S(1)} %get-tuple-element.25.c_ref, s32[8,128]{1,0:T(8,128)S(1)} %get-tuple-element.26.links_ref, f32[8,1536]{1,0:T(8,128)S(1)} %get-tuple-element.30.faces_ref, ...), custom_call_target="tpu_custom_call" | custom-call | tf_op jit(solution)/shard_map/final/pallas_call | solution.py:325
  (3 shorter events, 0.1 us)
Async XLA Ops:
  3.5 10.8 %collective-permute-start = (f32[8,1536]{1,0:T(8,128)S(1)}, f32[8,1536]{1,0:T(8,128)S(1)}, u32[]{:S(2)}, u32[]{:S(2)}) collective-permute-start(f32[8,1536]{1,0:T(8,128)S(1)} %get-tuple-element.21.faces_ref), channel_id=1, source_target_pairs={{0,3},{3,0},{2,5},{5,2},{4,7},{7,4},{6,9},{9,6},{8,11},{11,8},{10,... | collective-permute-start | bytes 147464 | tf_op jit(solution)/shard_map/ppermute | solution.py:339
  16.7 10.3 %collective-permute-start.1 = (f32[8,1536]{1,0:T(8,128)S(1)}, f32[8,1536]{1,0:T(8,128)S(1)}, u32[]{:S(2)}, u32[]{:S(2)}) collective-permute-start(f32[8,1536]{1,0:T(8,128)S(1)} %get-tuple-element.28.faces_ref), channel_id=1, source_target_pairs={{4,7},{7,4}} | collective-permute-start | bytes 147464 | tf_op jit(solution)/shard_map/ppermute | solution.py:365
  29.3 16.5 %collective-permute-start.2 = (f32[8,1536]{1,0:T(8,128)S(1)}, f32[8,1536]{1,0:T(8,128)S(1)}, u32[]{:S(2)}, u32[]{:S(2)}) collective-permute-start(f32[8,1536]{1,0:T(8,128)S(1)} %get-tuple-element.30.faces_ref), channel_id=1, source_target_pairs={{0,3},{3,0},{2,5},{5,2},{4,7},{7,4},{6,9},{9,6},{8,11},{11,8},{10,... | collective-permute-start | bytes 147464 | tf_op jit(solution)/shard_map/ppermute | solution.py:339

commit v10 on v9

--- a/solution.py
+++ b/solution.py
@@ -63,10 +63,10 @@
         here = lane // SIDE == place
         y_low[part] = jnp.where(here, roll(tiles[x][0], SIDE * place), y_low[part])
         y_high[part] = jnp.where(here, roll(tiles[x][1], SIDE * place + SIDE), y_high[part])
-        column = lane % SIDE == x
         for h in range(2):
-            z_low[h] = jnp.where(column, roll(tiles[x][h], x), z_low[h])
-            z_high[h] = jnp.where(column, roll(tiles[x][h], x - (SIDE - 1)), z_high[h])
+            turned = roll(tiles[x][h], x)
+            z_low[h] = jnp.where(lane % SIDE == x, turned, z_low[h])
+            z_high[h] = jnp.where(lane % SIDE == (x + SIDE - 1) % SIDE, turned, z_high[h])
     return [tiles[0], tiles[SIDE - 1], y_low, y_high, z_low, z_high]
 
 
@@ -119,19 +119,19 @@
     total = total + jnp.where(lane < SIDE, outer_minus, roll(here, SIDE))
     total = total + jnp.where(lane >= LANES - SIDE, outer_plus, roll(here, -SIDE))
     z = lane % SIDE
-    total = total + jnp.where(z == 0, roll(ghosts[4][h], -x), roll(here, 1))
+    total = total + jnp.where(z == 0, roll(ghosts[4][h], 1 - SIDE - x), roll(here, 1))
     total = total + jnp.where(z == SIDE - 1, roll(ghosts[5][h], SIDE - 1 - x), roll(here, -1))
     return total
 
 
-def relax(tiles, ghosts, source_ref, coefficient_ref, x, h):
-    weight = RELAXATION / (6.0 + coefficient_ref[2 * x + h])
+def relax(tiles, ghosts, source_ref, weight_ref, x, h):
+    weight = weight_ref[2 * x + h]
     gathered = source_ref[2 * x + h] + beside(tiles, ghosts, x, h)
     return (1.0 - RELAXATION) * tiles[x][h] + weight * gathered
 
 
-def sweep(tiles, ghosts, source_ref, coefficient_ref):
-    return [[relax(tiles, ghosts, source_ref, coefficient_ref, x, h) for h in range(2)] for x in range(SIDE)]
+def sweep(tiles, ghosts, source_ref, weight_ref):
+    return [[relax(tiles, ghosts, source_ref, weight_ref, x, h) for h in range(2)] for x in range(SIDE)]
 
 
 def range_base():
@@ -183,10 +183,12 @@
     store_faces(faces_out, pack_faces(load(p_out)))
 
 
-def reorder_rest_kernel(rest_ref, rows_ref, f_out, c_out):
+def reorder_rest_kernel(rest_ref, rows_ref, f_out, c_out, weight_out):
     rows = rows_ref[...]
     reorder(rest_ref, 0, rows, f_out)
     reorder(rest_ref, CELLS, rows, c_out)
+    for t in range(CELLS // LANES):
+        weight_out[t] = RELAXATION / (6.0 + c_out[t])
 
 
 def choose_kernel(pair_ref, single_ref, out_ref):
@@ -202,9 +204,9 @@
     return before, own, after
 
 
-def sweep_kernel(u_ref, f_ref, c_ref, links_ref, faces_ref, met_ref, u_out, faces_out):
+def sweep_kernel(u_ref, f_ref, weight_ref, links_ref, faces_ref, met_ref, u_out, faces_out):
     ghosts, _ = ghost_faces(links_ref[...], range_base(), *window(met_ref, faces_ref))
-    tiles = sweep(load(u_ref), ghosts, f_ref, c_ref)
+    tiles = sweep(load(u_ref), ghosts, f_ref, weight_ref)
     store(u_out, tiles)
     store_faces(faces_out, pack_faces(tiles))
 
@@ -265,7 +267,7 @@
     out_ref[:, width:] = jnp.where(core == 0, far_ref[0], far_ref[1])
 
 
-def final_kernel(u_ref, f_ref, c_ref, links_ref, faces_ref, row_ref, met_ref, out_ref):
+def final_kernel(u_ref, f_ref, weight_ref, links_ref, faces_ref, row_ref, met_ref, out_ref):
     core, curve = lax.axis_index("d") % 2, lax.axis_index("d") // 2
     row = sublanes()
     part = (lanes() // (ROW * RANGE) + SLOTS // ROW - curve // ROW % (SLOTS // ROW)) % (SLOTS // ROW)
@@ -313,9 +315,8 @@
     for x in range(SIDE):
         for h in range(2):
             t = 2 * x + h
-            weight = RELAXATION / (6.0 + c_ref[t])
             near = around[h] + (lift if x else raised[0]) + (lift if x < SIDE - 1 else raised[1])
-            tile = relax(tiles, ghosts, f_ref, c_ref, x, h) + ((1.0 - RELAXATION) * lift + weight * near)
+            tile = relax(tiles, ghosts, f_ref, weight_ref, x, h) + ((1.0 - RELAXATION) * lift + weight_ref[t] * near)
             half = jnp.where(core == 0, tile[0 : RANGE // 2], tile[RANGE // 2 :])
             out_ref[:, t * LANES : (t + 1) * LANES] = half
 
@@ -360,10 +361,10 @@
     )
     met = meet(faces)
     rest, _ = lax.optimization_barrier((rest, faces))
-    f, c = call(reorder_rest_kernel, [field, field], "rest", gather(rest, cores), rows)
-    u, faces = call(sweep_kernel, [field, packed], "sweep", u, f, c, links, faces, gather(met, cores))
+    f, c, w = call(reorder_rest_kernel, [field] * 3, "rest", gather(rest, cores), rows)
+    u, faces = call(sweep_kernel, [field, packed], "sweep", u, f, w, links, faces, gather(met, cores))
     met = call(choose_kernel, packed, "choose", gather(faces, pairs), lax.ppermute(faces, "d", single))
-    u, faces = call(sweep_kernel, [field, packed], "smooth", u, f, c, links, faces, gather(met, cores))
+    u, faces = call(sweep_kernel, [field, packed], "smooth", u, f, w, links, faces, gather(met, cores))
     met = meet(faces)
     coarse = call(coarse_kernel, f32(RANGE, LANES), "coarse", u, f, c, links, faces)
     coarse = gather(gather(coarse, along), across)
@@ -375,7 +376,7 @@
         "final",
         u,
         f,
-        c,
+        w,
         links,
         faces,
         row,

time: 53.2 us -> 53.1 us (level)
  transfers between devices with their start and end apart: 3 -> 3, of which waited for: 1 -> 0; matrix products, arithmetic and copies ran while one was open for 0% -> 0% of each run, Pallas kernels for 0% -> 0%
where the time goes in v10:
time: 53.1 us; the launch traced here: 52.8 us
  blocking collectives  30.9 us (58%)
  starting transfers between devices  18.1 us (34%)
  Pallas kernels  3.66 us (7%)
    all_gather x9, blocking collectives, on_device(): lax.all_gather(array, 'd', axis=0, axis_index_groups=members)  30.9 us
    ppermute x2, starting transfers between devices, on_device(): meet = lambda array: lax.ppermute(array, 'd', exchange)  17.4 us
    pallas_call x10, Pallas kernels, call(): pl.pallas_call(kernel, out_shape=out_shape, in_specs=specs or [VMEM] * le...  3.66 us
  transfers between devices with their start and end apart: 3, of which 0 were waited for; matrix products, arithmetic and copies ran while one was open for 0% of the time, Pallas kernels for 0%

profile of v10, /device:TPU:513, one launch (start us, length us, event | category | flops | bytes accessed | tf_op | source)
XLA Modules:
  0.0 52.8 jit_solution(11356600217117375480)
XLA Ops:
  0.0 1.0 %pack.1 = (f32[4,4224]{1,0:T(4,128)S(1)}, f32[4,8192]{1,0:T(4,128)S(1)}) custom-call(f32[4,4096]{1,0:T(4,128)} %p_ref.1, f32[4,4096]{1,0:T(4,128)} %f_ref.1, f32[4,4096]{1,0:T(4,128)} %c_ref.1, s32[4]{0:T(128)} %slot_ref.1, s32[4,6]{1,0:T(4,128)} %links_ref.1), custom_call_target="tpu_custom_call" | custom-call | tf_op jit(solution)/shard_map/pack/pallas_call | solution.py:326
  1.0 2.2 %all-gather.9.packed_ref = f32[2,4,4224]{2,1,0:T(4,128)S(1)} all-gather(f32[1,4,4224]{2,1,0:T(4,128)S(1)} %bitcast.14), channel_id=2, replica_groups={{0,1},{2,3},{4,5},{6,7},{8,9},{10,11},{12,13},{14,15},{16,17},{18,19},{..., dimensions={0}, use_global_device_ids=true | all-gather | bytes 202752 | tf_op jit(solution)/shard_map/all_gather | solution.py:339
  3.2 0.3 reorder.1
  3.5 8.7 %collective-permute-start = (f32[8,1536]{1,0:T(8,128)S(1)}, f32[8,1536]{1,0:T(8,128)S(1)}, u32[]{:S(2)}, u32[]{:S(2)}) collective-permute-start(f32[8,1536]{1,0:T(8,128)S(1)} %get-tuple-element.22.faces_ref), channel_id=1, source_target_pairs={{0,3},{3,0},{2,5},{5,2},{4,7},{7,4},{6,9},{9,6},{8,11},{11,8},{10,... | collective-permute-start | bytes 147464 | tf_op jit(solution)/shard_map/ppermute | solution.py:340
  12.2 2.0 %all-gather.10.rest_ref = f32[2,4,8192]{2,1,0:T(4,128)S(1)} all-gather(f32[1,4,8192]{2,1,0:T(4,128)S(1)} %bitcast.13), channel_id=3, replica_groups={{0,1},{2,3},{4,5},{6,7},{8,9},{10,11},{12,13},{14,15},{16,17},{18,19},{..., dimensions={0}, use_global_device_ids=true | all-gather | bytes 393216 | tf_op jit(solution)/shard_map/all_gather | solution.py:339
  14.2 0.1 rest.1
  14.3 0.0 collective-permute-done
  14.3 1.9 %all-gather.2 = f32[16,1536]{1,0:T(8,128)S(1)} all-gather(f32[8,1536]{1,0:T(8,128)S(1)} %collective-permute-done), channel_id=4, replica_groups={{0,1},{2,3},{4,5},{6,7},{8,9},{10,11},{12,13},{14,15},{16,17},{18,19},{..., dimensions={0}, use_global_device_ids=true | all-gather | bytes 147456 | tf_op jit(solution)/shard_map/all_gather | solution.py:339
  16.2 0.4 sweep.1
  16.6 0.7 %collective-permute-start.1 = (f32[8,1536]{1,0:T(8,128)S(1)}, f32[8,1536]{1,0:T(8,128)S(1)}, u32[]{:S(2)}, u32[]{:S(2)}) collective-permute-start(f32[8,1536]{1,0:T(8,128)S(1)} %get-tuple-element.29.faces_ref), channel_id=1, source_target_pairs={{4,7},{7,4}} | collective-permute-start | bytes 147464 | tf_op jit(solution)/shard_map/ppermute | solution.py:366
  17.3 9.6 %all-gather.3 = f32[16,1536]{1,0:T(8,128)S(1)} all-gather(f32[8,1536]{1,0:T(8,128)S(1)} %get-tuple-element.29.faces_ref), channel_id=5, replica_groups={{0,3},{2,5},{6,9},{8,11},{10,13},{12,15},{14,17},{16,19},{18,21},{20,23..., dimensions={0}, use_global_device_ids=true | all-gather | bytes 147456 | tf_op jit(solution)/shard_map/all_gather | solution.py:339
  26.9 0.0 collective-permute-done.1.single_ref
  27.0 1.9 %all-gather.4 = f32[16,1536]{1,0:T(8,128)S(1)} all-gather(f32[8,1536]{1,0:T(8,128)S(1)} %choose.1), channel_id=6, replica_groups={{0,1},{2,3},{4,5},{6,7},{8,9},{10,11},{12,13},{14,15},{16,17},{18,19},{..., dimensions={0}, use_global_device_ids=true | all-gather | bytes 147456 | tf_op jit(solution)/shard_map/all_gather | solution.py:339
  28.8 0.4 smooth.1
  29.3 8.7 %collective-permute-start.2 = (f32[8,1536]{1,0:T(8,128)S(1)}, f32[8,1536]{1,0:T(8,128)S(1)}, u32[]{:S(2)}, u32[]{:S(2)}) collective-permute-start(f32[8,1536]{1,0:T(8,128)S(1)} %get-tuple-element.31.faces_ref), channel_id=1, source_target_pairs={{0,3},{3,0},{2,5},{5,2},{4,7},{7,4},{6,9},{9,6},{8,11},{11,8},{10,... | collective-permute-start | bytes 147464 | tf_op jit(solution)/shard_map/ppermute | solution.py:340
  38.0 0.1 coarse.1
  38.1 3.2 %all-gather.5 = f32[16,128]{1,0:T(8,128)S(1)} all-gather(f32[8,128]{1,0:T(8,128)S(1)} %coarse.1), channel_id=7, replica_groups={{0,2},{4,6},{1,3},{5,7},{8,10},{12,14},{9,11},{13,15},{16,18},{20,22},{..., dimensions={0}, use_global_device_ids=true | all-gather | bytes 12288 | tf_op jit(solution)/shard_map/all_gather | solution.py:339
  41.4 4.4 %all-gather.6 = f32[4,8,128]{2,1,0:T(8,128)S(1)} all-gather(f32[2,8,128]{2,1,0:T(8,128)S(1)} %bitcast.17), channel_id=8, replica_groups={{0,6},{2,4},{1,7},{3,5},{8,14},{10,12},{9,15},{11,13},{16,22},{18,20},{..., dimensions={0}, use_global_device_ids=true | all-gather | bytes 24576 | tf_op jit(solution)/shard_map/all_gather | solution.py:339
  45.8 0.0 collective-permute-done.2.met_ref
  45.8 0.1 row.1.row_ref
  45.9 3.8 %all-gather.7 = f32[16,256]{1,0:T(8,128)S(1)} all-gather(f32[8,256]{1,0:T(8,128)S(1)} %row.1.row_ref), channel_id=9, replica_groups={{1,8},{3,10},{5,12},{7,14},{9,16},{11,18},{13,20},{15,22},{17,24},{19,2..., dimensions={0}, use_global_device_ids=true | all-gather | bytes 24576 | tf_op jit(solution)/shard_map/all_gather | solution.py:339
  49.7 1.9 %all-gather.8 = f32[16,1792]{1,0:T(8,128)S(1)} all-gather(f32[8,1792]{1,0:T(8,128)S(1)} %join.1), channel_id=10, replica_groups={{0,1},{2,3},{4,5},{6,7},{8,9},{10,11},{12,13},{14,15},{16,17},{18,19},{..., dimensions={0}, use_global_device_ids=true | all-gather | bytes 172032 | tf_op jit(solution)/shard_map/all_gather | solution.py:339
  51.6 1.2 %final.1 = f32[4,4096]{1,0:T(4,128)} custom-call(f32[32,8,128]{2,1,0:T(8,128)S(1)} %get-tuple-element.30.u_ref, f32[32,8,128]{2,1,0:T(8,128)S(1)} %get-tuple-element.25.f_ref, f32[32,8,128]{2,1,0:T(8,128)S(1)} %get-tuple-element.26.weight_ref, s32[8,128]{1,0:T(8,128)S(1)} %get-tuple-element.27.links_ref, f32[8,1536]{1,0:T(8,128)S(1)} %get-tuple-element.31.faces_ref, ...), custom_call_target="tpu_custom_call" | custom-call | tf_op jit(solution)/shard_map/final/pallas_call | solution.py:326
  (2 shorter events, 0.0 us)
Async XLA Ops:
  3.5 10.8 %collective-permute-start = (f32[8,1536]{1,0:T(8,128)S(1)}, f32[8,1536]{1,0:T(8,128)S(1)}, u32[]{:S(2)}, u32[]{:S(2)}) collective-permute-start(f32[8,1536]{1,0:T(8,128)S(1)} %get-tuple-element.22.faces_ref), channel_id=1, source_target_pairs={{0,3},{3,0},{2,5},{5,2},{4,7},{7,4},{6,9},{9,6},{8,11},{11,8},{10,... | collective-permute-start | bytes 147464 | tf_op jit(solution)/shard_map/ppermute | solution.py:340
  16.6 10.3 %collective-permute-start.1 = (f32[8,1536]{1,0:T(8,128)S(1)}, f32[8,1536]{1,0:T(8,128)S(1)}, u32[]{:S(2)}, u32[]{:S(2)}) collective-permute-start(f32[8,1536]{1,0:T(8,128)S(1)} %get-tuple-element.29.faces_ref), channel_id=1, source_target_pairs={{4,7},{7,4}} | collective-permute-start | bytes 147464 | tf_op jit(solution)/shard_map/ppermute | solution.py:366
  29.3 16.5 %collective-permute-start.2 = (f32[8,1536]{1,0:T(8,128)S(1)}, f32[8,1536]{1,0:T(8,128)S(1)}, u32[]{:S(2)}, u32[]{:S(2)}) collective-permute-start(f32[8,1536]{1,0:T(8,128)S(1)} %get-tuple-element.31.faces_ref), channel_id=1, source_target_pairs={{0,3},{3,0},{2,5},{5,2},{4,7},{7,4},{6,9},{9,6},{8,11},{11,8},{10,... | collective-permute-start | bytes 147464 | tf_op jit(solution)/shard_map/ppermute | solution.py:340

commit v11 on v10

--- a/solution.py
+++ b/solution.py
@@ -17,6 +17,7 @@
 CELLS = 4096
 FACES = 6
 FLIPPED = (1, 0, 3, 2, 5, 4)
+TURN = {3: LANES - SIDE, 5: 2 * SIDE - 2}
 ROW = 4
 BROKEN = 2
 SLOTS = 16
@@ -97,7 +98,7 @@
             mid = pick_rows(own(face, h), rows)
             high = pick_rows(after(face, h), rows)
             picked = jnp.where(local < 0, low, jnp.where(local >= RANGE, high, mid))
-            halves.append(jnp.where(link >= 0, picked, 0.0))
+            halves.append(roll(jnp.where(link >= 0, picked, 0.0), TURN.get(d, 0)))
         ghosts.append(halves)
         valid.append(link >= 0)
     return ghosts, valid
@@ -110,17 +111,18 @@
     plus = tiles[x + 1][h] if x < SIDE - 1 else ghosts[1][h]
     total = minus + plus
     part, place = x // 8, x % 8
+    outer_y = roll(jnp.where(lane // SIDE == place, ghosts[2][part], ghosts[3][part]), -SIDE * place)
     if h == 0:
-        outer_minus = roll(ghosts[2][part], -SIDE * place)
-        outer_plus = roll(tiles[x][1], -SIDE)
+        outer_minus, outer_plus = outer_y, roll(tiles[x][1], -SIDE)
     else:
-        outer_minus = roll(tiles[x][0], SIDE)
-        outer_plus = roll(ghosts[3][part], LANES - SIDE - SIDE * place)
+        outer_minus, outer_plus = roll(tiles[x][0], SIDE), outer_y
     total = total + jnp.where(lane < SIDE, outer_minus, roll(here, SIDE))
     total = total + jnp.where(lane >= LANES - SIDE, outer_plus, roll(here, -SIDE))
     z = lane % SIDE
-    total = total + jnp.where(z == 0, roll(ghosts[4][h], 1 - SIDE - x), roll(here, 1))
-    total = total + jnp.where(z == SIDE - 1, roll(ghosts[5][h], SIDE - 1 - x), roll(here, -1))
+    column = (x + SIDE - 1) % SIDE
+    outer_z = roll(jnp.where(z == column, ghosts[4][h], ghosts[5][h]), 1 - SIDE - x)
+    total = total + jnp.where(z == 0, outer_z, roll(here, 1))
+    total = total + jnp.where(z == SIDE - 1, outer_z, roll(here, -1))
     return total
 
 
@@ -365,9 +367,10 @@
     u, faces = call(sweep_kernel, [field, packed], "sweep", u, f, w, links, faces, gather(met, cores))
     met = call(choose_kernel, packed, "choose", gather(faces, pairs), lax.ppermute(faces, "d", single))
     u, faces = call(sweep_kernel, [field, packed], "smooth", u, f, w, links, faces, gather(met, cores))
+    coarse = gather(call(coarse_kernel, f32(RANGE, LANES), "coarse", u, f, c, links, faces), along)
+    faces, coarse = lax.optimization_barrier((faces, coarse))
     met = meet(faces)
-    coarse = call(coarse_kernel, f32(RANGE, LANES), "coarse", u, f, c, links, faces)
-    coarse = gather(gather(coarse, along), across)
+    coarse = gather(coarse, across)
     row = call(row_kernel, f32(RANGE, 2 * LANES), "row", coarse, met)
     joined = call(join_kernel, f32(RANGE, (FACES + 1) * 2 * LANES), "join", met, gather(row, far))
     return call(

time: 53.1 us -> 54.4 us (1.024)
  starting transfers between devices: 18.1 us -> 19.3 us
    ppermute x2, starting transfers between devices: 17.4 us -> 18.6 us  [on_device(): meet = lambda array: lax.ppermute(array, 'd', exchange)]
where the time goes in v11:
time: 54.4 us; the launch traced here: 54.1 us
  blocking collectives  31.2 us (57%)
  starting transfers between devices  19.3 us (35%)
  Pallas kernels  3.55 us (7%)
    all_gather x9, blocking collectives, on_device(): lax.all_gather(array, 'd', axis=0, axis_index_groups=members)  31.2 us
    ppermute x2, starting transfers between devices, on_device(): meet = lambda array: lax.ppermute(array, 'd', exchange)  18.6 us
    pallas_call x10, Pallas kernels, call(): pl.pallas_call(kernel, out_shape=out_shape, in_specs=specs or [VMEM] * le...  3.55 us
  transfers between devices with their start and end apart: 3, of which 0 were waited for; matrix products, arithmetic and copies ran while one was open for 0% of the time, Pallas kernels for 0%

profile of v11, /device:TPU:513, one launch (start us, length us, event | category | flops | bytes accessed | tf_op | source)
XLA Modules:
  0.0 54.1 jit_solution(9064071650833254483)
XLA Ops:
  0.0 1.0 %pack.1 = (f32[4,4224]{1,0:T(4,128)S(1)}, f32[4,8192]{1,0:T(4,128)S(1)}) custom-call(f32[4,4096]{1,0:T(4,128)} %p_ref.1, f32[4,4096]{1,0:T(4,128)} %f_ref.1, f32[4,4096]{1,0:T(4,128)} %c_ref.1, s32[4]{0:T(128)} %slot_ref.1, s32[4,6]{1,0:T(4,128)} %links_ref.1), custom_call_target="tpu_custom_call" | custom-call | tf_op jit(solution)/shard_map/pack/pallas_call | solution.py:328
  1.0 2.2 %all-gather.9.packed_ref = f32[2,4,4224]{2,1,0:T(4,128)S(1)} all-gather(f32[1,4,4224]{2,1,0:T(4,128)S(1)} %bitcast.14), channel_id=2, replica_groups={{0,1},{2,3},{4,5},{6,7},{8,9},{10,11},{12,13},{14,15},{16,17},{18,19},{..., dimensions={0}, use_global_device_ids=true | all-gather | bytes 202752 | tf_op jit(solution)/shard_map/all_gather | solution.py:341
  3.2 0.3 reorder.1
  3.5 8.7 %collective-permute-start = (f32[8,1536]{1,0:T(8,128)S(1)}, f32[8,1536]{1,0:T(8,128)S(1)}, u32[]{:S(2)}, u32[]{:S(2)}) collective-permute-start(f32[8,1536]{1,0:T(8,128)S(1)} %get-tuple-element.24.faces_ref), channel_id=1, source_target_pairs={{0,3},{3,0},{2,5},{5,2},{4,7},{7,4},{6,9},{9,6},{8,11},{11,8},{10,... | collective-permute-start | bytes 147464 | tf_op jit(solution)/shard_map/ppermute | solution.py:342
  12.2 2.0 %all-gather.10.rest_ref = f32[2,4,8192]{2,1,0:T(4,128)S(1)} all-gather(f32[1,4,8192]{2,1,0:T(4,128)S(1)} %bitcast.13), channel_id=3, replica_groups={{0,1},{2,3},{4,5},{6,7},{8,9},{10,11},{12,13},{14,15},{16,17},{18,19},{..., dimensions={0}, use_global_device_ids=true | all-gather | bytes 393216 | tf_op jit(solution)/shard_map/all_gather | solution.py:341
  14.2 0.1 rest.1
  14.3 0.0 collective-permute-done
  14.3 1.9 %all-gather.2 = f32[16,1536]{1,0:T(8,128)S(1)} all-gather(f32[8,1536]{1,0:T(8,128)S(1)} %collective-permute-done), channel_id=4, replica_groups={{0,1},{2,3},{4,5},{6,7},{8,9},{10,11},{12,13},{14,15},{16,17},{18,19},{..., dimensions={0}, use_global_device_ids=true | all-gather | bytes 147456 | tf_op jit(solution)/shard_map/all_gather | solution.py:341
  16.2 0.4 sweep.1
  16.6 0.7 %collective-permute-start.1 = (f32[8,1536]{1,0:T(8,128)S(1)}, f32[8,1536]{1,0:T(8,128)S(1)}, u32[]{:S(2)}, u32[]{:S(2)}) collective-permute-start(f32[8,1536]{1,0:T(8,128)S(1)} %get-tuple-element.31.faces_ref), channel_id=1, source_target_pairs={{4,7},{7,4}} | collective-permute-start | bytes 147464 | tf_op jit(solution)/shard_map/ppermute | solution.py:368
  17.3 9.6 %all-gather.3 = f32[16,1536]{1,0:T(8,128)S(1)} all-gather(f32[8,1536]{1,0:T(8,128)S(1)} %get-tuple-element.31.faces_ref), channel_id=5, replica_groups={{0,3},{2,5},{6,9},{8,11},{10,13},{12,15},{14,17},{16,19},{18,21},{20,23..., dimensions={0}, use_global_device_ids=true | all-gather | bytes 147456 | tf_op jit(solution)/shard_map/all_gather | solution.py:341
  26.9 0.0 collective-permute-done.1.single_ref
  26.9 1.9 %all-gather.4 = f32[16,1536]{1,0:T(8,128)S(1)} all-gather(f32[8,1536]{1,0:T(8,128)S(1)} %choose.1), channel_id=6, replica_groups={{0,1},{2,3},{4,5},{6,7},{8,9},{10,11},{12,13},{14,15},{16,17},{18,19},{..., dimensions={0}, use_global_device_ids=true | all-gather | bytes 147456 | tf_op jit(solution)/shard_map/all_gather | solution.py:341
  28.8 0.4 smooth.1
  29.2 0.1 coarse.1
  29.3 3.2 %all-gather.5 = f32[16,128]{1,0:T(8,128)S(1)} all-gather(f32[8,128]{1,0:T(8,128)S(1)} %coarse.1), channel_id=7, replica_groups={{0,2},{4,6},{1,3},{5,7},{8,10},{12,14},{9,11},{13,15},{16,18},{20,22},{..., dimensions={0}, use_global_device_ids=true | all-gather | bytes 12288 | tf_op jit(solution)/shard_map/all_gather | solution.py:341
  32.5 9.9 %collective-permute-start.2 = (f32[8,1536]{1,0:T(8,128)S(1)}, f32[8,1536]{1,0:T(8,128)S(1)}, u32[]{:S(2)}, u32[]{:S(2)}) collective-permute-start(f32[8,1536]{1,0:T(8,128)S(1)} %get-tuple-element.35.faces_ref), channel_id=1, source_target_pairs={{0,3},{3,0},{2,5},{5,2},{4,7},{7,4},{6,9},{9,6},{8,11},{11,8},{10,... | collective-permute-start | bytes 147464 | tf_op jit(solution)/shard_map/ppermute | solution.py:342
  42.4 4.7 %all-gather.6 = f32[4,8,128]{2,1,0:T(8,128)S(1)} all-gather(f32[2,8,128]{2,1,0:T(8,128)S(1)} %bitcast.17), channel_id=8, replica_groups={{0,6},{2,4},{1,7},{3,5},{8,14},{10,12},{9,15},{11,13},{16,22},{18,20},{..., dimensions={0}, use_global_device_ids=true | all-gather | bytes 24576 | tf_op jit(solution)/shard_map/all_gather | solution.py:341
  47.1 0.0 collective-permute-done.2.met_ref
  47.1 0.1 row.1.row_ref
  47.2 3.8 %all-gather.7 = f32[16,256]{1,0:T(8,128)S(1)} all-gather(f32[8,256]{1,0:T(8,128)S(1)} %row.1.row_ref), channel_id=9, replica_groups={{1,8},{3,10},{5,12},{7,14},{9,16},{11,18},{13,20},{15,22},{17,24},{19,2..., dimensions={0}, use_global_device_ids=true | all-gather | bytes 24576 | tf_op jit(solution)/shard_map/all_gather | solution.py:341
  51.0 1.9 %all-gather.8 = f32[16,1792]{1,0:T(8,128)S(1)} all-gather(f32[8,1792]{1,0:T(8,128)S(1)} %join.1), channel_id=10, replica_groups={{0,1},{2,3},{4,5},{6,7},{8,9},{10,11},{12,13},{14,15},{16,17},{18,19},{..., dimensions={0}, use_global_device_ids=true | all-gather | bytes 172032 | tf_op jit(solution)/shard_map/all_gather | solution.py:341
  52.9 1.2 %final.1 = f32[4,4096]{1,0:T(4,128)} custom-call(f32[32,8,128]{2,1,0:T(8,128)S(1)} %get-tuple-element.32.u_ref, f32[32,8,128]{2,1,0:T(8,128)S(1)} %get-tuple-element.27.f_ref, f32[32,8,128]{2,1,0:T(8,128)S(1)} %get-tuple-element.28.weight_ref, s32[8,128]{1,0:T(8,128)S(1)} %get-tuple-element.29.links_ref, f32[8,1536]{1,0:T(8,128)S(1)} %get-tuple-element.35.faces_ref, ...), custom_call_target="tpu_custom_call" | custom-call | tf_op jit(solution)/shard_map/final/pallas_call | solution.py:328
  (2 shorter events, 0.0 us)
Async XLA Ops:
  3.5 10.8 %collective-permute-start = (f32[8,1536]{1,0:T(8,128)S(1)}, f32[8,1536]{1,0:T(8,128)S(1)}, u32[]{:S(2)}, u32[]{:S(2)}) collective-permute-start(f32[8,1536]{1,0:T(8,128)S(1)} %get-tuple-element.24.faces_ref), channel_id=1, source_target_pairs={{0,3},{3,0},{2,5},{5,2},{4,7},{7,4},{6,9},{9,6},{8,11},{11,8},{10,... | collective-permute-start | bytes 147464 | tf_op jit(solution)/shard_map/ppermute | solution.py:342
  16.6 10.3 %collective-permute-start.1 = (f32[8,1536]{1,0:T(8,128)S(1)}, f32[8,1536]{1,0:T(8,128)S(1)}, u32[]{:S(2)}, u32[]{:S(2)}) collective-permute-start(f32[8,1536]{1,0:T(8,128)S(1)} %get-tuple-element.31.faces_ref), channel_id=1, source_target_pairs={{4,7},{7,4}} | collective-permute-start | bytes 147464 | tf_op jit(solution)/shard_map/ppermute | solution.py:368
  32.5 14.5 %collective-permute-start.2 = (f32[8,1536]{1,0:T(8,128)S(1)}, f32[8,1536]{1,0:T(8,128)S(1)}, u32[]{:S(2)}, u32[]{:S(2)}) collective-permute-start(f32[8,1536]{1,0:T(8,128)S(1)} %get-tuple-element.35.faces_ref), channel_id=1, source_target_pairs={{0,3},{3,0},{2,5},{5,2},{4,7},{7,4},{6,9},{9,6},{8,11},{11,8},{10,... | collective-permute-start | bytes 147464 | tf_op jit(solution)/shard_map/ppermute | solution.py:342

commit v12 on v11

--- a/solution.py
+++ b/solution.py
@@ -367,10 +367,9 @@
     u, faces = call(sweep_kernel, [field, packed], "sweep", u, f, w, links, faces, gather(met, cores))
     met = call(choose_kernel, packed, "choose", gather(faces, pairs), lax.ppermute(faces, "d", single))
     u, faces = call(sweep_kernel, [field, packed], "smooth", u, f, w, links, faces, gather(met, cores))
-    coarse = gather(call(coarse_kernel, f32(RANGE, LANES), "coarse", u, f, c, links, faces), along)
-    faces, coarse = lax.optimization_barrier((faces, coarse))
     met = meet(faces)
-    coarse = gather(coarse, across)
+    coarse = call(coarse_kernel, f32(RANGE, LANES), "coarse", u, f, c, links, faces)
+    coarse = gather(gather(coarse, along), across)
     row = call(row_kernel, f32(RANGE, 2 * LANES), "row", coarse, met)
     joined = call(join_kernel, f32(RANGE, (FACES + 1) * 2 * LANES), "join", met, gather(row, far))
     return call(

time: 54.4 us -> 53 us (0.974)
  starting transfers between devices: 19.3 us -> 18.1 us
    ppermute x2, starting transfers between devices: 18.6 us -> 17.4 us  [on_device(): meet = lambda array: lax.ppermute(array, 'd', exchange)]
where the time goes in v12:
time: 53 us; the launch traced here: 52.7 us
  blocking collectives  30.9 us (58%)
  starting transfers between devices  18.1 us (34%)
  Pallas kernels  3.55 us (7%)
    all_gather x9, blocking collectives, on_device(): lax.all_gather(array, 'd', axis=0, axis_index_groups=members)  30.9 us
    ppermute x2, starting transfers between devices, on_device(): meet = lambda array: lax.ppermute(array, 'd', exchange)  17.4 us
    pallas_call x10, Pallas kernels, call(): pl.pallas_call(kernel, out_shape=out_shape, in_specs=specs or [VMEM] * le...  3.55 us
  transfers between devices with their start and end apart: 3, of which 0 were waited for; matrix products, arithmetic and copies ran while one was open for 0% of the time, Pallas kernels for 0%

profile of v12, /device:TPU:513, one launch (start us, length us, event | category | flops | bytes accessed | tf_op | source)
XLA Modules:
  0.0 52.7 jit_solution(15454672659755417787)
XLA Ops:
  0.0 1.0 %pack.1 = (f32[4,4224]{1,0:T(4,128)S(1)}, f32[4,8192]{1,0:T(4,128)S(1)}) custom-call(f32[4,4096]{1,0:T(4,128)} %p_ref.1, f32[4,4096]{1,0:T(4,128)} %f_ref.1, f32[4,4096]{1,0:T(4,128)} %c_ref.1, s32[4]{0:T(128)} %slot_ref.1, s32[4,6]{1,0:T(4,128)} %links_ref.1), custom_call_target="tpu_custom_call" | custom-call | tf_op jit(solution)/shard_map/pack/pallas_call | solution.py:328
  1.0 2.2 %all-gather.9.packed_ref = f32[2,4,4224]{2,1,0:T(4,128)S(1)} all-gather(f32[1,4,4224]{2,1,0:T(4,128)S(1)} %bitcast.14), channel_id=2, replica_groups={{0,1},{2,3},{4,5},{6,7},{8,9},{10,11},{12,13},{14,15},{16,17},{18,19},{..., dimensions={0}, use_global_device_ids=true | all-gather | bytes 202752 | tf_op jit(solution)/shard_map/all_gather | solution.py:341
  3.2 0.3 reorder.1
  3.5 8.7 %collective-permute-start = (f32[8,1536]{1,0:T(8,128)S(1)}, f32[8,1536]{1,0:T(8,128)S(1)}, u32[]{:S(2)}, u32[]{:S(2)}) collective-permute-start(f32[8,1536]{1,0:T(8,128)S(1)} %get-tuple-element.22.faces_ref), channel_id=1, source_target_pairs={{0,3},{3,0},{2,5},{5,2},{4,7},{7,4},{6,9},{9,6},{8,11},{11,8},{10,... | collective-permute-start | bytes 147464 | tf_op jit(solution)/shard_map/ppermute | solution.py:342
  12.2 2.0 %all-gather.10.rest_ref = f32[2,4,8192]{2,1,0:T(4,128)S(1)} all-gather(f32[1,4,8192]{2,1,0:T(4,128)S(1)} %bitcast.13), channel_id=3, replica_groups={{0,1},{2,3},{4,5},{6,7},{8,9},{10,11},{12,13},{14,15},{16,17},{18,19},{..., dimensions={0}, use_global_device_ids=true | all-gather | bytes 393216 | tf_op jit(solution)/shard_map/all_gather | solution.py:341
  14.2 0.1 rest.1
  14.3 0.0 collective-permute-done
  14.3 1.9 %all-gather.2 = f32[16,1536]{1,0:T(8,128)S(1)} all-gather(f32[8,1536]{1,0:T(8,128)S(1)} %collective-permute-done), channel_id=4, replica_groups={{0,1},{2,3},{4,5},{6,7},{8,9},{10,11},{12,13},{14,15},{16,17},{18,19},{..., dimensions={0}, use_global_device_ids=true | all-gather | bytes 147456 | tf_op jit(solution)/shard_map/all_gather | solution.py:341
  16.2 0.4 sweep.1
  16.6 0.7 %collective-permute-start.1 = (f32[8,1536]{1,0:T(8,128)S(1)}, f32[8,1536]{1,0:T(8,128)S(1)}, u32[]{:S(2)}, u32[]{:S(2)}) collective-permute-start(f32[8,1536]{1,0:T(8,128)S(1)} %get-tuple-element.29.faces_ref), channel_id=1, source_target_pairs={{4,7},{7,4}} | collective-permute-start | bytes 147464 | tf_op jit(solution)/shard_map/ppermute | solution.py:368
  17.3 9.6 %all-gather.3 = f32[16,1536]{1,0:T(8,128)S(1)} all-gather(f32[8,1536]{1,0:T(8,128)S(1)} %get-tuple-element.29.faces_ref), channel_id=5, replica_groups={{0,3},{2,5},{6,9},{8,11},{10,13},{12,15},{14,17},{16,19},{18,21},{20,23..., dimensions={0}, use_global_device_ids=true | all-gather | bytes 147456 | tf_op jit(solution)/shard_map/all_gather | solution.py:341
  26.9 0.0 collective-permute-done.1.single_ref
  26.9 1.9 %all-gather.4 = f32[16,1536]{1,0:T(8,128)S(1)} all-gather(f32[8,1536]{1,0:T(8,128)S(1)} %choose.1), channel_id=6, replica_groups={{0,1},{2,3},{4,5},{6,7},{8,9},{10,11},{12,13},{14,15},{16,17},{18,19},{..., dimensions={0}, use_global_device_ids=true | all-gather | bytes 147456 | tf_op jit(solution)/shard_map/all_gather | solution.py:341
  28.8 0.4 smooth.1
  29.2 8.7 %collective-permute-start.2 = (f32[8,1536]{1,0:T(8,128)S(1)}, f32[8,1536]{1,0:T(8,128)S(1)}, u32[]{:S(2)}, u32[]{:S(2)}) collective-permute-start(f32[8,1536]{1,0:T(8,128)S(1)} %get-tuple-element.31.faces_ref), channel_id=1, source_target_pairs={{0,3},{3,0},{2,5},{5,2},{4,7},{7,4},{6,9},{9,6},{8,11},{11,8},{10,... | collective-permute-start | bytes 147464 | tf_op jit(solution)/shard_map/ppermute | solution.py:342
  37.9 0.1 coarse.1
  38.0 3.2 %all-gather.5 = f32[16,128]{1,0:T(8,128)S(1)} all-gather(f32[8,128]{1,0:T(8,128)S(1)} %coarse.1), channel_id=7, replica_groups={{0,2},{4,6},{1,3},{5,7},{8,10},{12,14},{9,11},{13,15},{16,18},{20,22},{..., dimensions={0}, use_global_device_ids=true | all-gather | bytes 12288 | tf_op jit(solution)/shard_map/all_gather | solution.py:341
  41.3 4.4 %all-gather.6 = f32[4,8,128]{2,1,0:T(8,128)S(1)} all-gather(f32[2,8,128]{2,1,0:T(8,128)S(1)} %bitcast.17), channel_id=8, replica_groups={{0,6},{2,4},{1,7},{3,5},{8,14},{10,12},{9,15},{11,13},{16,22},{18,20},{..., dimensions={0}, use_global_device_ids=true | all-gather | bytes 24576 | tf_op jit(solution)/shard_map/all_gather | solution.py:341
  45.7 0.0 collective-permute-done.2.met_ref
  45.7 0.1 row.1.row_ref
  45.8 3.8 %all-gather.7 = f32[16,256]{1,0:T(8,128)S(1)} all-gather(f32[8,256]{1,0:T(8,128)S(1)} %row.1.row_ref), channel_id=9, replica_groups={{1,8},{3,10},{5,12},{7,14},{9,16},{11,18},{13,20},{15,22},{17,24},{19,2..., dimensions={0}, use_global_device_ids=true | all-gather | bytes 24576 | tf_op jit(solution)/shard_map/all_gather | solution.py:341
  49.6 1.9 %all-gather.8 = f32[16,1792]{1,0:T(8,128)S(1)} all-gather(f32[8,1792]{1,0:T(8,128)S(1)} %join.1), channel_id=10, replica_groups={{0,1},{2,3},{4,5},{6,7},{8,9},{10,11},{12,13},{14,15},{16,17},{18,19},{..., dimensions={0}, use_global_device_ids=true | all-gather | bytes 172032 | tf_op jit(solution)/shard_map/all_gather | solution.py:341
  51.5 1.2 %final.1 = f32[4,4096]{1,0:T(4,128)} custom-call(f32[32,8,128]{2,1,0:T(8,128)S(1)} %get-tuple-element.30.u_ref, f32[32,8,128]{2,1,0:T(8,128)S(1)} %get-tuple-element.25.f_ref, f32[32,8,128]{2,1,0:T(8,128)S(1)} %get-tuple-element.26.weight_ref, s32[8,128]{1,0:T(8,128)S(1)} %get-tuple-element.27.links_ref, f32[8,1536]{1,0:T(8,128)S(1)} %get-tuple-element.31.faces_ref, ...), custom_call_target="tpu_custom_call" | custom-call | tf_op jit(solution)/shard_map/final/pallas_call | solution.py:328
  (2 shorter events, 0.0 us)
Async XLA Ops:
  3.5 10.8 %collective-permute-start = (f32[8,1536]{1,0:T(8,128)S(1)}, f32[8,1536]{1,0:T(8,128)S(1)}, u32[]{:S(2)}, u32[]{:S(2)}) collective-permute-start(f32[8,1536]{1,0:T(8,128)S(1)} %get-tuple-element.22.faces_ref), channel_id=1, source_target_pairs={{0,3},{3,0},{2,5},{5,2},{4,7},{7,4},{6,9},{9,6},{8,11},{11,8},{10,... | collective-permute-start | bytes 147464 | tf_op jit(solution)/shard_map/ppermute | solution.py:342
  16.6 10.3 %collective-permute-start.1 = (f32[8,1536]{1,0:T(8,128)S(1)}, f32[8,1536]{1,0:T(8,128)S(1)}, u32[]{:S(2)}, u32[]{:S(2)}) collective-permute-start(f32[8,1536]{1,0:T(8,128)S(1)} %get-tuple-element.29.faces_ref), channel_id=1, source_target_pairs={{4,7},{7,4}} | collective-permute-start | bytes 147464 | tf_op jit(solution)/shard_map/ppermute | solution.py:368
  29.2 16.5 %collective-permute-start.2 = (f32[8,1536]{1,0:T(8,128)S(1)}, f32[8,1536]{1,0:T(8,128)S(1)}, u32[]{:S(2)}, u32[]{:S(2)}) collective-permute-start(f32[8,1536]{1,0:T(8,128)S(1)} %get-tuple-element.31.faces_ref), channel_id=1, source_target_pairs={{0,3},{3,0},{2,5},{5,2},{4,7},{7,4},{6,9},{9,6},{8,11},{11,8},{10,... | collective-permute-start | bytes 147464 | tf_op jit(solution)/shard_map/ppermute | solution.py:342

commit v13 on v12

--- a/solution.py
+++ b/solution.py
@@ -300,12 +300,12 @@
     for step in range(COARSE_SWEEPS - 1):
         error = (1.0 - RELAXATION) * error + weight * (residual + total(named(error)))
     near = named(error)
-    own = lanes() == curve % SLOTS * RANGE + row
-    lift = lane_sum(jnp.where(own, error, 0.0))
+    own = curve % SLOTS * RANGE + row
+    lift = jnp.take_along_axis(error, own, axis=1)
     ghosts, _ = ghost_faces(links_ref[...], range_base(), *window(met_ref, faces_ref))
     raised = []
     for d in range(FACES):
-        raised.append(lane_sum(jnp.where(own, jnp.broadcast_to(near[d : d + 1], (RANGE, LANES)), 0.0)))
+        raised.append(jnp.take_along_axis(jnp.broadcast_to(near[d : d + 1], (RANGE, LANES)), own, axis=1))
     lane = lanes()
     z = lane % SIDE
     around = []

time: 53 us -> 53 us (level)
  no operation moved by 1% of the time
where the time goes in v13:
time: 53 us; the launch traced here: 52.7 us
  blocking collectives  30.9 us (58%)
  starting transfers between devices  18.1 us (34%)
  Pallas kernels  3.56 us (7%)
    all_gather x9, blocking collectives, on_device(): lax.all_gather(array, 'd', axis=0, axis_index_groups=members)  30.9 us
    ppermute x2, starting transfers between devices, on_device(): meet = lambda array: lax.ppermute(array, 'd', exchange)  17.4 us
    pallas_call x10, Pallas kernels, call(): pl.pallas_call(kernel, out_shape=out_shape, in_specs=specs or [VMEM] * le...  3.56 us
  transfers between devices with their start and end apart: 3, of which 0 were waited for; matrix products, arithmetic and copies ran while one was open for 0% of the time, Pallas kernels for 0%

profile of v13, /device:TPU:513, one launch (start us, length us, event | category | flops | bytes accessed | tf_op | source)
XLA Modules:
  0.0 52.7 jit_solution(14532302395316300076)
XLA Ops:
  0.0 1.0 %pack.1 = (f32[4,4224]{1,0:T(4,128)S(1)}, f32[4,8192]{1,0:T(4,128)S(1)}) custom-call(f32[4,4096]{1,0:T(4,128)} %p_ref.1, f32[4,4096]{1,0:T(4,128)} %f_ref.1, f32[4,4096]{1,0:T(4,128)} %c_ref.1, s32[4]{0:T(128)} %slot_ref.1, s32[4,6]{1,0:T(4,128)} %links_ref.1), custom_call_target="tpu_custom_call" | custom-call | tf_op jit(solution)/shard_map/pack/pallas_call | solution.py:328
  1.0 2.2 %all-gather.9.packed_ref = f32[2,4,4224]{2,1,0:T(4,128)S(1)} all-gather(f32[1,4,4224]{2,1,0:T(4,128)S(1)} %bitcast.14), channel_id=2, replica_groups={{0,1},{2,3},{4,5},{6,7},{8,9},{10,11},{12,13},{14,15},{16,17},{18,19},{..., dimensions={0}, use_global_device_ids=true | all-gather | bytes 202752 | tf_op jit(solution)/shard_map/all_gather | solution.py:341
  3.2 0.3 reorder.1
  3.5 8.7 %collective-permute-start = (f32[8,1536]{1,0:T(8,128)S(1)}, f32[8,1536]{1,0:T(8,128)S(1)}, u32[]{:S(2)}, u32[]{:S(2)}) collective-permute-start(f32[8,1536]{1,0:T(8,128)S(1)} %get-tuple-element.22.faces_ref), channel_id=1, source_target_pairs={{0,3},{3,0},{2,5},{5,2},{4,7},{7,4},{6,9},{9,6},{8,11},{11,8},{10,... | collective-permute-start | bytes 147464 | tf_op jit(solution)/shard_map/ppermute | solution.py:342
  12.2 2.0 %all-gather.10.rest_ref = f32[2,4,8192]{2,1,0:T(4,128)S(1)} all-gather(f32[1,4,8192]{2,1,0:T(4,128)S(1)} %bitcast.13), channel_id=3, replica_groups={{0,1},{2,3},{4,5},{6,7},{8,9},{10,11},{12,13},{14,15},{16,17},{18,19},{..., dimensions={0}, use_global_device_ids=true | all-gather | bytes 393216 | tf_op jit(solution)/shard_map/all_gather | solution.py:341
  14.2 0.1 rest.1
  14.3 0.0 collective-permute-done
  14.3 1.9 %all-gather.2 = f32[16,1536]{1,0:T(8,128)S(1)} all-gather(f32[8,1536]{1,0:T(8,128)S(1)} %collective-permute-done), channel_id=4, replica_groups={{0,1},{2,3},{4,5},{6,7},{8,9},{10,11},{12,13},{14,15},{16,17},{18,19},{..., dimensions={0}, use_global_device_ids=true | all-gather | bytes 147456 | tf_op jit(solution)/shard_map/all_gather | solution.py:341
  16.2 0.4 sweep.1
  16.6 0.7 %collective-permute-start.1 = (f32[8,1536]{1,0:T(8,128)S(1)}, f32[8,1536]{1,0:T(8,128)S(1)}, u32[]{:S(2)}, u32[]{:S(2)}) collective-permute-start(f32[8,1536]{1,0:T(8,128)S(1)} %get-tuple-element.29.faces_ref), channel_id=1, source_target_pairs={{4,7},{7,4}} | collective-permute-start | bytes 147464 | tf_op jit(solution)/shard_map/ppermute | solution.py:368
  17.3 9.6 %all-gather.3 = f32[16,1536]{1,0:T(8,128)S(1)} all-gather(f32[8,1536]{1,0:T(8,128)S(1)} %get-tuple-element.29.faces_ref), channel_id=5, replica_groups={{0,3},{2,5},{6,9},{8,11},{10,13},{12,15},{14,17},{16,19},{18,21},{20,23..., dimensions={0}, use_global_device_ids=true | all-gather | bytes 147456 | tf_op jit(solution)/shard_map/all_gather | solution.py:341
  26.9 0.0 collective-permute-done.1.single_ref
  26.9 1.9 %all-gather.4 = f32[16,1536]{1,0:T(8,128)S(1)} all-gather(f32[8,1536]{1,0:T(8,128)S(1)} %choose.1), channel_id=6, replica_groups={{0,1},{2,3},{4,5},{6,7},{8,9},{10,11},{12,13},{14,15},{16,17},{18,19},{..., dimensions={0}, use_global_device_ids=true | all-gather | bytes 147456 | tf_op jit(solution)/shard_map/all_gather | solution.py:341
  28.8 0.4 smooth.1
  29.2 8.7 %collective-permute-start.2 = (f32[8,1536]{1,0:T(8,128)S(1)}, f32[8,1536]{1,0:T(8,128)S(1)}, u32[]{:S(2)}, u32[]{:S(2)}) collective-permute-start(f32[8,1536]{1,0:T(8,128)S(1)} %get-tuple-element.31.faces_ref), channel_id=1, source_target_pairs={{0,3},{3,0},{2,5},{5,2},{4,7},{7,4},{6,9},{9,6},{8,11},{11,8},{10,... | collective-permute-start | bytes 147464 | tf_op jit(solution)/shard_map/ppermute | solution.py:342
  37.9 0.1 coarse.1
  38.0 3.2 %all-gather.5 = f32[16,128]{1,0:T(8,128)S(1)} all-gather(f32[8,128]{1,0:T(8,128)S(1)} %coarse.1), channel_id=7, replica_groups={{0,2},{4,6},{1,3},{5,7},{8,10},{12,14},{9,11},{13,15},{16,18},{20,22},{..., dimensions={0}, use_global_device_ids=true | all-gather | bytes 12288 | tf_op jit(solution)/shard_map/all_gather | solution.py:341
  41.3 4.4 %all-gather.6 = f32[4,8,128]{2,1,0:T(8,128)S(1)} all-gather(f32[2,8,128]{2,1,0:T(8,128)S(1)} %bitcast.17), channel_id=8, replica_groups={{0,6},{2,4},{1,7},{3,5},{8,14},{10,12},{9,15},{11,13},{16,22},{18,20},{..., dimensions={0}, use_global_device_ids=true | all-gather | bytes 24576 | tf_op jit(solution)/shard_map/all_gather | solution.py:341
  45.7 0.0 collective-permute-done.2.met_ref
  45.7 0.1 row.1.row_ref
  45.8 3.8 %all-gather.7 = f32[16,256]{1,0:T(8,128)S(1)} all-gather(f32[8,256]{1,0:T(8,128)S(1)} %row.1.row_ref), channel_id=9, replica_groups={{1,8},{3,10},{5,12},{7,14},{9,16},{11,18},{13,20},{15,22},{17,24},{19,2..., dimensions={0}, use_global_device_ids=true | all-gather | bytes 24576 | tf_op jit(solution)/shard_map/all_gather | solution.py:341
  49.6 1.9 %all-gather.8 = f32[16,1792]{1,0:T(8,128)S(1)} all-gather(f32[8,1792]{1,0:T(8,128)S(1)} %join.1), channel_id=10, replica_groups={{0,1},{2,3},{4,5},{6,7},{8,9},{10,11},{12,13},{14,15},{16,17},{18,19},{..., dimensions={0}, use_global_device_ids=true | all-gather | bytes 172032 | tf_op jit(solution)/shard_map/all_gather | solution.py:341
  51.5 1.2 %final.1 = f32[4,4096]{1,0:T(4,128)} custom-call(f32[32,8,128]{2,1,0:T(8,128)S(1)} %get-tuple-element.30.u_ref, f32[32,8,128]{2,1,0:T(8,128)S(1)} %get-tuple-element.25.f_ref, f32[32,8,128]{2,1,0:T(8,128)S(1)} %get-tuple-element.26.weight_ref, s32[8,128]{1,0:T(8,128)S(1)} %get-tuple-element.27.links_ref, f32[8,1536]{1,0:T(8,128)S(1)} %get-tuple-element.31.faces_ref, ...), custom_call_target="tpu_custom_call" | custom-call | tf_op jit(solution)/shard_map/final/pallas_call | solution.py:328
  (2 shorter events, 0.0 us)
Async XLA Ops:
  3.5 10.8 %collective-permute-start = (f32[8,1536]{1,0:T(8,128)S(1)}, f32[8,1536]{1,0:T(8,128)S(1)}, u32[]{:S(2)}, u32[]{:S(2)}) collective-permute-start(f32[8,1536]{1,0:T(8,128)S(1)} %get-tuple-element.22.faces_ref), channel_id=1, source_target_pairs={{0,3},{3,0},{2,5},{5,2},{4,7},{7,4},{6,9},{9,6},{8,11},{11,8},{10,... | collective-permute-start | bytes 147464 | tf_op jit(solution)/shard_map/ppermute | solution.py:342
  16.6 10.3 %collective-permute-start.1 = (f32[8,1536]{1,0:T(8,128)S(1)}, f32[8,1536]{1,0:T(8,128)S(1)}, u32[]{:S(2)}, u32[]{:S(2)}) collective-permute-start(f32[8,1536]{1,0:T(8,128)S(1)} %get-tuple-element.29.faces_ref), channel_id=1, source_target_pairs={{4,7},{7,4}} | collective-permute-start | bytes 147464 | tf_op jit(solution)/shard_map/ppermute | solution.py:368
  29.2 16.5 %collective-permute-start.2 = (f32[8,1536]{1,0:T(8,128)S(1)}, f32[8,1536]{1,0:T(8,128)S(1)}, u32[]{:S(2)}, u32[]{:S(2)}) collective-permute-start(f32[8,1536]{1,0:T(8,128)S(1)} %get-tuple-element.31.faces_ref), channel_id=1, source_target_pairs={{0,3},{3,0},{2,5},{5,2},{4,7},{7,4},{6,9},{9,6},{8,11},{11,8},{10,... | collective-permute-start | bytes 147464 | tf_op jit(solution)/shard_map/ppermute | solution.py:342
